TPU v7x, 32 devices: a whole 2x2x4 slice. The times are simulated.
32 devices in a mesh: dp: 2 (over core), ctx: 8 (over z, y), tp: 2 (over x).
Axes of the slice: x: 2, y: 2, z: 4, core: 2. Of those that a mesh axis runs over, the one named last changes fastest.
Arguments:
- prompt_states: bfloat16 [2048, 2048], P(('dp', 'ctx')), may hold values from -6 to 6
- continuation_states: bfloat16 [8192, 2048], P(('dp', 'ctx')), may hold values from -6 to 6
- continuation_offset: int32 [16], P(('dp', 'ctx')), may hold values from 0 to 511
- attention_gain: bfloat16 [2048], replicated, may hold values from 0.099609375 to 1.8984375
- query_weight: bfloat16 [2048, 1280], P(('dp', 'ctx'), 'tp'), may hold values from -0.125 to 0.125
- key_weight: bfloat16 [2048, 320], P(('dp', 'ctx')), may hold values from -0.125 to 0.125
- value_weight: bfloat16 [2048, 320], P(('dp', 'ctx')), may hold values from -0.125 to 0.125
- query_gain: bfloat16 [64], replicated, may hold values from 0.099609375 to 1.8984375
- key_gain: bfloat16 [64], replicated, may hold values from 0.099609375 to 1.8984375
- output_weight: bfloat16 [1280, 2048], P('tp', ('dp', 'ctx')), may hold values from -6 to 6
- feedforward_gain: bfloat16 [2048], replicated, may hold values from 0.099609375 to 1.8984375
- gate_weight: bfloat16 [2048, 5120], P(('dp', 'ctx'), 'tp'), may hold values from -0.125 to 0.125
- up_weight: bfloat16 [2048, 5120], P(('dp', 'ctx'), 'tp'), may hold values from -0.125 to 0.125
- down_weight: bfloat16 [5120, 2048], P('tp', ('dp', 'ctx')), may hold values from -0.078125 to 0.078125
- grad_prompt: bfloat16 [2048, 2048], P(('dp', 'ctx')), may hold values from -6 to 6
- grad_continuation: bfloat16 [8192, 2048], P(('dp', 'ctx')), may hold values from -6 to 6
Outputs:
- prompt_output: bfloat16 [2048, 2048], P(('dp', 'ctx'))
- continuation_output: bfloat16 [8192, 2048], P(('dp', 'ctx'))
- prompt_input_grad: bfloat16 [2048, 2048], P(('dp', 'ctx'))
- continuation_input_grad: bfloat16 [8192, 2048], P(('dp', 'ctx'))
- attention_gain_grad: float32 [2048], replicated
- query_weight_grad: float32 [2048, 1280], P(('dp', 'ctx'), 'tp')
- key_weight_grad: float32 [2048, 320], P(('dp', 'ctx'))
- value_weight_grad: float32 [2048, 320], P(('dp', 'ctx'))
- query_gain_grad: float32 [64], replicated
- key_gain_grad: float32 [64], replicated
- output_weight_grad: float32 [1280, 2048], P('tp', ('dp', 'ctx'))
- feedforward_gain_grad: float32 [2048], replicated
- gate_weight_grad: float32 [2048, 5120], P(('dp', 'ctx'), 'tp')
- up_weight_grad: float32 [2048, 5120], P(('dp', 'ctx'), 'tp')
- down_weight_grad: float32 [5120, 2048], P('tp', ('dp', 'ctx'))
All inputs are finite; a program needn't handle non-finite values.
Results may differ from a plain program's by a relative error of at most 0.019.
Values may be sent and summed in bfloat16 or wider, within the bound.
No kernel may reach another device: no remote copies, remote signals or barrier semaphores. Data moves between devices by JAX's collectives and lax.ppermute only.
A program may use at most 256 MiB of HBM per device.

v0:
```python
from functools import partial

import jax
import jax.numpy as jnp
from jax import lax
from jax.sharding import PartitionSpec as P

epsilon = 1e-06


def rms_norm(values, norm_gain):
    scale = lax.rsqrt(jnp.mean(values * values, axis=-1, keepdims=True) + epsilon)
    return values * scale * norm_gain


def rope_tables(positions, width):
    half_width = width // 2
    freqs = 10000.0 ** (-(2.0 * jnp.arange(half_width, dtype=jnp.float32)) / width)
    angles = positions[:, None] * freqs[None, :]
    angles = jnp.concatenate([angles, angles], axis=1)
    return (jnp.cos(angles), jnp.sin(angles))


def head_prep(raw_heads, norm_gain, cosine_table, sine_table):
    normed = rms_norm(raw_heads, norm_gain)
    half_width = raw_heads.shape[-1] // 2
    turned = jnp.concatenate([-normed[..., half_width:], normed[..., :half_width]], axis=-1)
    return normed * cosine_table[:, None, :] + turned * sine_table[:, None, :]


def swiglu(gate_rows, up_rows):
    return jax.nn.silu(gate_rows) * up_rows


def contract_last(left_rows, right_rows):
    return lax.dot_general(
        left_rows, right_rows, (((1,), (1,)), ((), ())), preferred_element_type=jnp.float32
    )


def contract_first(left_rows, right_rows):
    return lax.dot_general(
        left_rows, right_rows, (((0,), (0,)), ((), ())), preferred_element_type=jnp.float32
    )


def fold_columns(inputs, pieces):
    return tuple(
        (
            jnp.dot(inputs, weight_piece, preferred_element_type=jnp.float32)
            for weight_piece in pieces
        )
    )


def tensor_sum(values):
    return lax.psum(values.astype(jnp.bfloat16), "tp").astype(jnp.float32)


def on_device(
    prompt_states,
    continuation_states,
    continuation_offset,
    attention_gain,
    query_weight,
    key_weight,
    value_weight,
    query_gain,
    key_gain,
    output_weight,
    feedforward_gain,
    gate_weight,
    up_weight,
    down_weight,
    grad_prompt,
    grad_continuation,
):
    prompt_here = prompt_states.shape[0]
    cont_length = continuation_states.shape[0]
    rows_here = prompt_here + cont_length
    prompt_length = prompt_here * lax.axis_size("ctx")
    key_count = prompt_length + cont_length
    head_size = query_gain.shape[0]
    local_heads = query_weight.shape[1] // head_size
    shared_heads = key_weight.shape[1] // head_size
    group_size = local_heads * lax.axis_size("tp") // shared_heads
    context_rank = lax.axis_index("ctx")
    tensor_rank = lax.axis_index("tp")
    inputs = jnp.concatenate([prompt_states, continuation_states], axis=0)
    input_float = inputs.astype(jnp.float32)
    row_ids = jnp.arange(rows_here, dtype=jnp.int32)
    prompt_place = context_rank * prompt_here + row_ids
    positions = jnp.where(
        row_ids < prompt_here,
        prompt_place,
        prompt_length + continuation_offset[0] + row_ids - prompt_here,
    ).astype(jnp.float32)
    cosine_table, sine_table = rope_tables(positions, head_size)
    key_ids = jnp.arange(key_count, dtype=jnp.int32)
    allowed = jnp.where(
        (row_ids < prompt_here)[:, None],
        key_ids[None, :] <= prompt_place[:, None],
        (key_ids[None, :] < prompt_length)
        | (key_ids[None, :] - prompt_length <= (row_ids - prompt_here)[:, None]),
    )
    rotate = partial(head_prep, cosine_table=cosine_table, sine_table=sine_table)
    normed, attn_norm_back = jax.vjp(rms_norm, input_float, attention_gain.astype(jnp.float32))
    normed_low = normed.astype(jnp.bfloat16)
    query_raw, key_raw, value_raw = fold_columns(
        normed_low,
        (
            lax.all_gather(query_weight, ("dp", "ctx"), axis=0, tiled=True),
            lax.all_gather(key_weight, ("dp", "ctx"), axis=0, tiled=True),
            lax.all_gather(value_weight, ("dp", "ctx"), axis=0, tiled=True),
        ),
    )
    query_rot, query_back = jax.vjp(
        rotate, query_raw.reshape(rows_here, local_heads, head_size), query_gain.astype(jnp.float32)
    )
    query_low = query_rot.reshape(rows_here, local_heads * head_size).astype(jnp.bfloat16)
    key_rot, key_back = jax.vjp(
        rotate, key_raw.reshape(rows_here, shared_heads, head_size), key_gain.astype(jnp.float32)
    )
    key_low = key_rot.reshape(rows_here, shared_heads * head_size).astype(jnp.bfloat16)
    value_low = value_raw.astype(jnp.bfloat16)
    prompt_keys, prompt_values = (
        lax.all_gather(key_low[:prompt_here], "ctx", axis=0, tiled=True),
        lax.all_gather(value_low[:prompt_here], "ctx", axis=0, tiled=True),
    )
    all_keys = jnp.concatenate([prompt_keys, key_low[prompt_here:]], axis=0)
    all_values = jnp.concatenate([prompt_values, value_low[prompt_here:]], axis=0)

    def head_slices(head_index):
        shared_index = (tensor_rank * local_heads + head_index) // group_size
        query_head = lax.dynamic_slice_in_dim(query_low, head_index * head_size, head_size, 1)
        key_head = lax.dynamic_slice_in_dim(all_keys, shared_index * head_size, head_size, 1)
        value_head = lax.dynamic_slice_in_dim(all_values, shared_index * head_size, head_size, 1)
        return (query_head, key_head, value_head, shared_index)

    def scores_of(query_head, key_head):
        scores = contract_last(query_head, key_head) * 0.125
        return jnp.where(allowed, scores, -1e30)

    def head_forward(head_index):
        query_head, key_head, value_head, shared_index = head_slices(head_index)
        scores = scores_of(query_head, key_head)
        row_max = jnp.max(scores, axis=1, keepdims=True)
        weights = jnp.exp(scores - row_max)
        totals = jnp.sum(weights, axis=1, keepdims=True)
        probabilities = (weights / totals).astype(jnp.bfloat16)
        combined = jnp.dot(probabilities, value_head, preferred_element_type=jnp.float32)
        return (combined, (row_max + jnp.log(totals))[:, 0])

    per_head, log_sums = lax.map(head_forward, jnp.arange(local_heads, dtype=jnp.int32))
    attended_low = (
        jnp.transpose(per_head, (1, 0, 2))
        .reshape(rows_here, local_heads * head_size)
        .astype(jnp.bfloat16)
    )
    output_full, down_full = (
        lax.all_gather(output_weight, ("dp", "ctx"), axis=1, tiled=True),
        lax.all_gather(down_weight, ("dp", "ctx"), axis=1, tiled=True),
    )
    resid = input_float + tensor_sum(
        jnp.dot(attended_low, output_full, preferred_element_type=jnp.float32)
    )
    normed_two, ffn_norm_back = jax.vjp(rms_norm, resid, feedforward_gain.astype(jnp.float32))
    normed_two_low = normed_two.astype(jnp.bfloat16)
    gate_rows, up_rows = fold_columns(
        normed_two_low,
        (
            lax.all_gather(gate_weight, ("dp", "ctx"), axis=0, tiled=True),
            lax.all_gather(up_weight, ("dp", "ctx"), axis=0, tiled=True),
        ),
    )
    hidden, swiglu_back = jax.vjp(swiglu, gate_rows, up_rows)
    hidden_low = hidden.astype(jnp.bfloat16)
    output = resid + tensor_sum(jnp.dot(hidden_low, down_full, preferred_element_type=jnp.float32))
    prompt_output = output[:prompt_here].astype(jnp.bfloat16)
    continuation_output = output[prompt_here:].astype(jnp.bfloat16)
    grad_out = jnp.concatenate([grad_prompt, grad_continuation], axis=0)
    grad_down = contract_first(hidden_low, grad_out)
    output_back, down_back = (
        lax.all_gather(output_weight, ("dp", "ctx"), axis=1, tiled=True),
        lax.all_gather(down_weight, ("dp", "ctx"), axis=1, tiled=True),
    )
    grad_hidden = contract_last(grad_out, down_back)
    grad_gate, grad_up = swiglu_back(grad_hidden)
    grad_gate_low = grad_gate.astype(jnp.bfloat16)
    grad_up_low = grad_up.astype(jnp.bfloat16)
    grad_gate_weight = contract_first(normed_two_low, grad_gate_low)
    grad_up_weight = contract_first(normed_two_low, grad_up_low)
    pieces = (
        lax.all_gather(gate_weight, ("dp", "ctx"), axis=0, tiled=True),
        lax.all_gather(up_weight, ("dp", "ctx"), axis=0, tiled=True),
    )
    product = contract_last(grad_gate_low, pieces[0]) + contract_last(grad_up_low, pieces[1])
    grad_resid_part, grad_ffn_gain = ffn_norm_back(tensor_sum(product))
    grad_resid = grad_out.astype(jnp.float32) + grad_resid_part
    grad_resid_low = grad_resid.astype(jnp.bfloat16)
    grad_output_weight = contract_first(attended_low, grad_resid_low)
    grad_attended = contract_last(grad_resid_low, output_back).astype(jnp.bfloat16)

    def head_backward(carry, head_index):
        key_totals, value_totals = carry
        query_head, key_head, value_head, shared_index = head_slices(head_index)
        grad_head = lax.dynamic_slice_in_dim(grad_attended, head_index * head_size, head_size, 1)
        probabilities = jnp.exp(scores_of(query_head, key_head) - log_sums[head_index][:, None])
        grad_value = contract_first(probabilities.astype(jnp.bfloat16), grad_head)
        grad_probs = contract_last(grad_head, value_head)
        delta = jnp.sum(probabilities * grad_probs, axis=1, keepdims=True)
        grad_scores = (probabilities * (grad_probs - delta) * 0.125).astype(jnp.bfloat16)
        grad_query = jnp.dot(grad_scores, key_head, preferred_element_type=jnp.float32)
        grad_key = contract_first(grad_scores, query_head)
        column = shared_index * head_size
        key_totals = lax.dynamic_update_slice_in_dim(
            key_totals,
            lax.dynamic_slice_in_dim(key_totals, column, head_size, 1) + grad_key,
            column,
            1,
        )
        value_totals = lax.dynamic_update_slice_in_dim(
            value_totals,
            lax.dynamic_slice_in_dim(value_totals, column, head_size, 1) + grad_value,
            column,
            1,
        )
        return ((key_totals, value_totals), grad_query)

    zeros_keys = jnp.zeros((key_count, shared_heads * head_size), jnp.float32)
    (grad_keys, grad_values), grad_queries = lax.scan(
        head_backward, (zeros_keys, zeros_keys), jnp.arange(local_heads, dtype=jnp.int32)
    )
    grad_query_rot = jnp.transpose(grad_queries, (1, 0, 2))
    grad_query_raw, grad_query_gain = query_back(grad_query_rot)
    grad_query_low = grad_query_raw.reshape(rows_here, local_heads * head_size).astype(jnp.bfloat16)
    prompt_key_grad, prompt_value_grad = (
        lax.psum_scatter(
            grad_keys[:prompt_length].astype(jnp.bfloat16), "ctx", scatter_dimension=0, tiled=True
        ).astype(jnp.float32),
        lax.psum_scatter(
            grad_values[:prompt_length].astype(jnp.bfloat16), "ctx", scatter_dimension=0, tiled=True
        ).astype(jnp.float32),
    )
    own_key_grad = jnp.concatenate([prompt_key_grad, grad_keys[prompt_length:]], axis=0)
    own_value_grad = jnp.concatenate([prompt_value_grad, grad_values[prompt_length:]], axis=0)
    own_key_grad, own_value_grad, grad_query_gain = (
        lax.psum(own_key_grad.astype(jnp.bfloat16), "tp").astype(jnp.float32),
        lax.psum(own_value_grad.astype(jnp.bfloat16), "tp").astype(jnp.float32),
        lax.psum(grad_query_gain.astype(jnp.bfloat16), "tp").astype(jnp.float32),
    )
    grad_key_raw, grad_key_gain = key_back(own_key_grad.reshape(rows_here, shared_heads, head_size))
    grad_key_low = grad_key_raw.reshape(rows_here, shared_heads * head_size).astype(jnp.bfloat16)
    grad_value_low = own_value_grad.astype(jnp.bfloat16)
    grad_query_weight = contract_first(normed_low, grad_query_low)
    grad_key_weight = contract_first(normed_low, grad_key_low)
    grad_value_weight = contract_first(normed_low, grad_value_low)
    pieces = (
        lax.all_gather(query_weight, ("dp", "ctx"), axis=0, tiled=True),
        lax.all_gather(key_weight, ("dp", "ctx"), axis=0, tiled=True),
        lax.all_gather(value_weight, ("dp", "ctx"), axis=0, tiled=True),
    )
    query_part = contract_last(grad_query_low, pieces[0])
    shared_part = contract_last(grad_key_low, pieces[1]) + contract_last(grad_value_low, pieces[2])
    grad_normed = tensor_sum(query_part) + shared_part
    grad_input_part, grad_attn_gain = attn_norm_back(grad_normed)
    grad_input = (grad_resid + grad_input_part).astype(jnp.bfloat16)
    query_done, key_done, value_done, gate_done, up_done = (
        lax.psum_scatter(grad_query_weight, ("dp", "ctx"), scatter_dimension=0, tiled=True),
        lax.psum_scatter(grad_key_weight, ("dp", "ctx"), scatter_dimension=0, tiled=True),
        lax.psum_scatter(grad_value_weight, ("dp", "ctx"), scatter_dimension=0, tiled=True),
        lax.psum_scatter(grad_gate_weight, ("dp", "ctx"), scatter_dimension=0, tiled=True),
        lax.psum_scatter(grad_up_weight, ("dp", "ctx"), scatter_dimension=0, tiled=True),
    )
    outward = (
        lax.psum_scatter(grad_output_weight, ("dp", "ctx"), scatter_dimension=1, tiled=True),
        lax.psum_scatter(grad_down, ("dp", "ctx"), scatter_dimension=1, tiled=True),
    )
    gain_sums = lax.psum(
        (grad_attn_gain, grad_ffn_gain, grad_query_gain, grad_key_gain), ("dp", "ctx")
    )
    return (
        prompt_output,
        continuation_output,
        grad_input[:prompt_here],
        grad_input[prompt_here:],
        gain_sums[0],
        query_done,
        key_done,
        value_done,
        gain_sums[2],
        gain_sums[3],
        outward[0],
        gain_sums[1],
        gate_done,
        up_done,
        outward[1],
    )


def solution(mesh):
    in_specs = (
        P(("dp", "ctx"), None),
        P(("dp", "ctx"), None),
        P(("dp", "ctx")),
        P(),
        P(("dp", "ctx"), "tp"),
        P(("dp", "ctx"), None),
        P(("dp", "ctx"), None),
        P(),
        P(),
        P("tp", ("dp", "ctx")),
        P(),
        P(("dp", "ctx"), "tp"),
        P(("dp", "ctx"), "tp"),
        P("tp", ("dp", "ctx")),
        P(("dp", "ctx"), None),
        P(("dp", "ctx"), None),
    )
    out_specs = (
        P(("dp", "ctx"), None),
        P(("dp", "ctx"), None),
        P(("dp", "ctx"), None),
        P(("dp", "ctx"), None),
        P(),
        P(("dp", "ctx"), "tp"),
        P(("dp", "ctx"), None),
        P(("dp", "ctx"), None),
        P(),
        P(),
        P("tp", ("dp", "ctx")),
        P(),
        P(("dp", "ctx"), "tp"),
        P(("dp", "ctx"), "tp"),
        P("tp", ("dp", "ctx")),
    )
    return jax.shard_map(
        on_device, mesh=mesh, in_specs=in_specs, out_specs=out_specs, check_vma=False
    )
```

profile of v0, /device:TPU:9, one launch (start us, length us, event | category | flops | bytes accessed | tf_op | source)
XLA Modules:
  0.0 2211.0 jit_solution(14134863726572111871)
XLA Ops:
  17.5 32.0 %all-gather.10.cloned.1.call-done = bf16[2048,320]{0,1:T(8,128)(2,1)} async-done(((bf16[128,320]{0,1:T(8,128)(2,1)}), bf16[2048,320]{0,1:T(8,128)(2,1)}) %all-gather.10.cloned.1.call-update) | async-done | bytes 1310736 | tf_op jit(solution)/shard_map/all_gather | solution.py:113
  54.7 34.0 %all-gather.12.cloned.1.call-done = bf16[2048,320]{0,1:T(8,128)(2,1)} async-done(((bf16[128,320]{0,1:T(8,128)(2,1)}), bf16[2048,320]{0,1:T(8,128)(2,1)}) %all-gather.12.cloned.1.call-update) | async-done | bytes 1310736 | tf_op jit(solution)/shard_map/all_gather | solution.py:114
  92.8 23.9 %all_gather.36 = bf16[1024,320]{0,1:T(8,128)(2,1)S(1)} all-gather(bf16[128,320]{0,1:T(8,128)(2,1)S(1)} %slice.74), channel_id=1, replica_groups=mesh['dp'=2,'ctx'=8,'tp'=2] {'ctx'}, dimensions={0}, use_global_device_ids=true | all-gather | bytes 737280 | tf_op jit(solution)/shard_map/all_gather | solution.py:127
  120.1 26.0 %all_gather.38 = bf16[1024,320]{0,1:T(8,128)(2,1)S(1)} all-gather(bf16[128,320]{0,1:T(8,128)(2,1)S(1)} %slice.76), channel_id=1, replica_groups=mesh['dp'=2,'ctx'=8,'tp'=2] {'ctx'}, dimensions={0}, use_global_device_ids=true | all-gather | bytes 737280 | tf_op jit(solution)/shard_map/all_gather | solution.py:128
  158.7 124.3 %while.34 = (s32[]{:T(128)}, bf16[10,640,64]{1,2,0:T(8,128)(2,1)}, f32[10,640]{1,0:T(8,128)}, s32[10]{0:T(128)S(1)}, bf16[640,640]{1,0:T(8,128)(2,1)S(1)}, /*ind...) while((s32[]{:T(128)}, bf16[10,640,64]{1,2,0:T(8,128)(2,1)}, ...), condition=%wide.region_6.7_spmd.clone.clone, body=%wide.region_3.6_spmd.clone.sunk.clone | while | flops 263454112 | bytes 28690356 | solution.py:154
  295.9 74.5 %all-reduce.10.cloned.1.call-done = bf16[640,2048]{1,0:T(8,128)(2,1)} async-done(((bf16[640,2048]{1,0:T(8,128)(2,1)}), bf16[640,2048]{1,0:T(8,128)(2,1)}) %all-reduce.10.cloned.1.call-update) | async-done | bytes 2621456 | tf_op jit(solution)/shard_map/psum | solution.py:57
  376.2 83.9 %all-gather.16.cloned.1.call-done = bf16[2048,2560]{1,0:T(8,128)(2,1)} async-done(((bf16[128,2560]{1,0:T(8,128)(2,1)}), bf16[2048,2560]{1,0:T(8,128)(2,1)}) %all-gather.16.cloned.1.call-update) | async-done | bytes 10485776 | tf_op jit(solution)/shard_map/all_gather | solution.py:172
  460.1 12.3 fusion.75
  472.5 76.2 %all-gather.18.cloned.1.call-done = bf16[2048,2560]{1,0:T(8,128)(2,1)} async-done(((bf16[128,2560]{1,0:T(8,128)(2,1)}), bf16[2048,2560]{1,0:T(8,128)(2,1)}) %all-gather.18.cloned.1.call-update) | async-done | bytes 10485776 | tf_op jit(solution)/shard_map/all_gather | solution.py:173
  548.7 12.1 fusion.76
  560.8 78.3 %all-gather.20.cloned.1.call-done = bf16[2560,2048]{1,0:T(8,128)(2,1)} async-done(((bf16[2560,128]{1,0:T(8,128)(2,1)}), bf16[2560,2048]{1,0:T(8,128)(2,1)}) %all-gather.20.cloned.1.call-update) | async-done | bytes 10485776 | tf_op jit(solution)/shard_map/all_gather | solution.py:162
  639.1 17.8 multiply_convert_fusion.1
  656.9 10.8 fusion.77
  667.7 11.2 add_convert_fusion
  679.0 74.0 %all-reduce.12.cloned.1.call-done = bf16[640,2048]{1,0:T(8,128)(2,1)} async-done(((bf16[640,2048]{1,0:T(8,128)(2,1)}), bf16[640,2048]{1,0:T(8,128)(2,1)}) %all-reduce.12.cloned.1.call-update) | async-done | bytes 2621456 | tf_op jit(solution)/shard_map/psum | solution.py:57
  767.2 208.5 %while.35 = (s32[]{:T(128)}, f32[1536,320]{0,1:T(8,128)}, f32[1536,320]{0,1:T(8,128)}, f32[10,640,64]{1,2,0:T(8,128)}, s32[10]{0:T(128)S(1)}, /*index=5*/s32[]{:...) while((s32[]{:T(128)}, f32[1536,320]{0,1:T(8,128)}, ...), condition=%wide.region_14.15_spmd.clone.clone, body=%wide.region_12.14_spmd.clone.sunk.clone | while | flops 643104128 | bytes 48826372 | solution.py:231
  979.6 12.0 convolution_convert_fusion.1
  1005.8 34.3 %reduce-scatter.30.cloned.1.call-done = bf16[128,320]{1,0:T(8,128)(2,1)} async-done(((bf16[1024,320]{1,0:T(8,128)(2,1)}), bf16[128,320]{1,0:T(8,128)(2,1)}) %reduce-scatter.30.cloned.1.call-update) | async-done | bytes 81936
  1042.0 63.9 %reduce-scatter.28.cloned.1.call-done = bf16[128,320]{1,0:T(8,128)(2,1)} async-done(((bf16[1024,320]{1,0:T(8,128)(2,1)}), bf16[128,320]{1,0:T(8,128)(2,1)}) %reduce-scatter.28.cloned.1.call-update) | async-done | bytes 81936
  1108.8 8.6 fusion.53
  1125.5 133.8 %all-reduce.14.cloned.1.call-done = (bf16[640,2048]{1,0:T(8,128)(2,1)}, bf16[640,5,64]{0,2,1:T(8,128)(2,1)}, bf16[640,2048]{1,0:T(8,128)(2,1)}, bf16[640,320]{0,1:T(8,128)(2,1)}) async-done(((bf16[640,2048]{1,0:T(8,128)(2,1)}, bf16[640,5,64]{0,2,1:T(8,128)(2,1)}, bf16[640,2048]{1,0:T(8,128)(2,1)}, bf16[640,320]{0,1:T(8,128)(2,1)}), (bf16[640,2048]{1,0:T(8,128)(2,1)}, bf16[640,5,64]{0,2,1:T(8,128)(2,1)}, ...) | async-done | bytes 6062096 | tf_op jit(solution)/shard_map/psum | solution.py:57
  1270.5 15.1 fusion.80
  1285.7 14.9 fusion.81
  1301.0 14.7 fusion.82
  1326.5 6.9 fusion.46
  1338.0 61.0 %all-reduce.4 = (f32[2048]{0:T(1024)}, f32[64]{0:T(128)}, f32[64]{0:T(128)}, f32[2048]{0:T(1024)}) all-reduce(f32[2048]{0:T(1024)S(1)} %get-tuple-element.423, bf16[64]{0:T(256)(128)(2,1)S(1)} %psum.84, f32[64]{0:T(128)S(1)} %get-tuple-element.427, f32[2048]{0:T(1024)S(1)} %copy-done.46), channel_id=1, replica_groups=mesh['dp'=2,'ctx'=8,'tp'=2] {'dp','ctx'}, use_global_device_ids=true, to_apply=%region_24.25 | all-reduce | flops 4224 | bytes 33664 | tf_op jit(solution)/shard_map/psum | solution.py:279
  1399.0 25.1 %reduce-scatter.14.cloned.1.call-done = f32[128,640]{1,0:T(8,128)} async-done(((f32[2048,640]{1,0:T(8,128)}), f32[128,640]{1,0:T(8,128)}) %reduce-scatter.14.cloned.1.call-update) | async-done | bytes 327696 | tf_op jit(solution)/shard_map/reduce_scatter | solution.py:269
  1424.0 66.9 %reduce-scatter.16.cloned.1.call-done = f32[128,320]{0,1:T(8,128)} async-done(((f32[2048,320]{0,1:T(8,128)}), f32[128,320]{0,1:T(8,128)}) %reduce-scatter.16.cloned.1.call-update) | async-done | bytes 163856 | tf_op jit(solution)/shard_map/reduce_scatter | solution.py:270
  1490.9 67.6 %reduce-scatter.18.cloned.1.call-done = f32[128,320]{0,1:T(8,128)} async-done(((f32[2048,320]{0,1:T(8,128)}), f32[128,320]{0,1:T(8,128)}) %reduce-scatter.18.cloned.1.call-update) | async-done | bytes 163856 | tf_op jit(solution)/shard_map/reduce_scatter | solution.py:271
  1558.5 215.3 %reduce-scatter.22.cloned.1.call-done = f32[128,2560]{1,0:T(8,128)} async-done(((f32[2048,2560]{1,0:T(8,128)}), f32[128,2560]{1,0:T(8,128)}) %reduce-scatter.22.cloned.1.call-update) | async-done | bytes 1310736 | tf_op jit(solution)/shard_map/reduce_scatter | solution.py:272
  1773.8 215.1 %reduce-scatter.24.cloned.1.call-done = f32[128,2560]{1,0:T(8,128)} async-done(((f32[2048,2560]{1,0:T(8,128)}), f32[128,2560]{1,0:T(8,128)}) %reduce-scatter.24.cloned.1.call-update) | async-done | bytes 1310736 | tf_op jit(solution)/shard_map/reduce_scatter | solution.py:273
  1988.9 215.1 %reduce-scatter.26.cloned.1.call-done = f32[2560,128]{1,0:T(8,128)} async-done(((f32[2560,2048]{1,0:T(8,128)}), f32[2560,128]{1,0:T(8,128)}) %reduce-scatter.26.cloned.1.call-update) | async-done | bytes 1310736 | tf_op jit(solution)/shard_map/reduce_scatter | solution.py:277
  (442 shorter events, 410.9 us)
Async XLA Ops:
  7.2 42.3 %all-gather.10.cloned.1.call-start = ((), (), s32[]{:S(2)}) async-start(), calls=%async_computation.10 | async-start | bytes 1392640 | tf_op jit(solution)/shard_map/all_gather | solution.py:113
  8.0 80.8 %all-gather.12.cloned.1.call-start = ((), (), s32[]{:S(2)}) async-start(), calls=%async_computation.11 | async-start | bytes 1392640 | tf_op jit(solution)/shard_map/all_gather | solution.py:114
  8.7 140.8 %all-gather.8.cloned.1.call-start = ((), (), s32[]{:S(2)}) async-start(), calls=%async_computation.9 | async-start | bytes 2785280 | tf_op jit(solution)/shard_map/all_gather | solution.py:112
  9.5 273.5 %all-gather.14.cloned.1.call-start = ((), (), s32[]{:S(2)}) async-start(), calls=%async_computation.12 | async-start | bytes 2785280 | tf_op jit(solution)/shard_map/all_gather | solution.py:161
  10.0 360.4 %all-reduce.10.cloned.1.call-start = ((), (), s32[]{:S(2)}) async-start(), calls=%async_computation.13 | async-start | bytes 5242880 | tf_op jit(solution)/shard_map/psum | solution.py:57
  14.0 39.0 %copy-start.47 = (f32[64]{0:T(128)}, f32[64]{0:T(128)S(1)}, u32[]{:S(2)}) copy-start(f32[64]{0:T(128)S(1)} %convert_element_type.144) | copy-start | bytes 772
  15.1 140.3 %copy-start.20 = (f32[640,64]{0,1:T(8,128)}, f32[640,64]{0,1:T(8,128)S(1)}, u32[]{:S(2)}) copy-start(f32[640,64]{0,1:T(8,128)S(1)} %get-tuple-element.514) | copy-start | bytes 491524
  15.1 140.4 %copy-start.15 = (f32[640,64]{0,1:T(8,128)}, f32[640,64]{0,1:T(8,128)S(1)}, u32[]{:S(2)}) copy-start(f32[640,64]{0,1:T(8,128)S(1)} %get-tuple-element.513) | copy-start | bytes 491524
  15.2 139.3 %copy-start.49 = (f32[64]{0:T(128)}, f32[64]{0:T(128)S(1)}, u32[]{:S(2)}) copy-start(f32[64]{0:T(128)S(1)} %convert_element_type.141) | copy-start | bytes 772
  54.7 62.0 %copy-start.26 = (bf16[512,320]{0,1:T(8,128)(2,1)S(1)}, bf16[512,320]{0,1:T(8,128)(2,1)}, u32[]{:S(2)}) copy-start(bf16[512,320]{0,1:T(8,128)(2,1)} %slice.75) | copy-start | bytes 983044
  117.7 28.4 %copy-start.27 = (bf16[512,320]{0,1:T(8,128)(2,1)S(1)}, bf16[512,320]{0,1:T(8,128)(2,1)}, u32[]{:S(2)}) copy-start(bf16[512,320]{0,1:T(8,128)(2,1)} %slice.77) | copy-start | bytes 983044
  288.7 171.4 %all-gather.16.cloned.1.call-start = ((), (), s32[]{:S(2)}) async-start(), calls=%async_computation.14 | async-start | bytes 11141120 | tf_op jit(solution)/shard_map/all_gather | solution.py:172
  289.3 259.4 %all-gather.18.cloned.1.call-start = ((), (), s32[]{:S(2)}) async-start(), calls=%async_computation.15 | async-start | bytes 11141120 | tf_op jit(solution)/shard_map/all_gather | solution.py:173
  290.0 349.0 %all-gather.20.cloned.1.call-start = ((), (), s32[]{:S(2)}) async-start(), calls=%async_computation.16 | async-start | bytes 11141120 | tf_op jit(solution)/shard_map/all_gather | solution.py:162
  290.8 462.2 %all-reduce.12.cloned.1.call-start = ((), (), s32[]{:S(2)}) async-start(), calls=%async_computation.17 | async-start | bytes 5242880 | tf_op jit(solution)/shard_map/psum | solution.py:57
  656.9 10.8 copy-start.59
  678.9 361.2 %reduce-scatter.30.cloned.1.call-start = ((), (), s32[]{:S(2)}) async-start(), calls=%async_computation.26 | async-start | bytes 884736
  979.5 126.3 %reduce-scatter.28.cloned.1.call-start = ((), (), s32[]{:S(2)}) async-start(), calls=%async_computation.25 | async-start | bytes 884736
  979.6 12.0 copy-start.12
  996.7 262.6 %all-reduce.14.cloned.1.call-start = ((), (), s32[]{:S(2)}) async-start(), calls=%async_computation.27 | async-start | bytes 12124160 | tf_op jit(solution)/shard_map/psum | solution.py:57
  1002.1 39.1 %slice-start = ((bf16[1536,320]{0,1:T(8,128)(2,1)}), bf16[512,320]{0,1:T(8,128)(2,1)S(1)}, s32[]{:S(2)}) async-start(bf16[1536,320]{0,1:T(8,128)(2,1)} %copy-done.22), calls=%async_computation.28 | async-start | bytes 655360 | tf_op jit(solution)/shard_map/slice | solution.py:246
  1002.1 104.8 %slice-start.1 = ((bf16[1536,320]{0,1:T(8,128)(2,1)}), bf16[512,320]{0,1:T(8,128)(2,1)S(1)}, s32[]{:S(2)}) async-start(bf16[1536,320]{0,1:T(8,128)(2,1)} %copy-done.23), calls=%async_computation.29 | async-start | bytes 655360 | tf_op jit(solution)/shard_map/slice | solution.py:245
  1107.7 291.3 %reduce-scatter.20.cloned.1.call-start = ((), (), s32[]{:S(2)}) async-start(), calls=%async_computation.21 | async-start | bytes 5570560 | tf_op jit(solution)/shard_map/reduce_scatter | solution.py:276
  1117.4 306.6 %reduce-scatter.14.cloned.1.call-start = ((), (), s32[]{:S(2)}) async-start(), calls=%async_computation.18 | async-start | bytes 5570560 | tf_op jit(solution)/shard_map/reduce_scatter | solution.py:269
  1125.2 135.3 %copy-start.10 = (f32[640,320]{0,1:T(8,128)S(1)}, f32[640,320]{0,1:T(8,128)}, u32[]{:S(2)}) copy-start(f32[640,320]{0,1:T(8,128)} %copy-done.9) | copy-start | bytes 2457604
  1125.2 135.3 %copy-start.35 = (f32[640,5]{0,1:T(8,128)S(1)}, f32[640,5]{0,1:T(8,128)}, u32[]{:S(2)}) copy-start(f32[640,5]{0,1:T(8,128)} %copy-done.34) | copy-start | bytes 38404
  1125.2 135.3 %copy-start.48 = (f32[64]{0:T(128)S(1)}, f32[64]{0:T(128)}, u32[]{:S(2)}) copy-start(f32[64]{0:T(128)} %copy-done.47) | copy-start | bytes 772
  1125.2 365.7 %reduce-scatter.16.cloned.1.call-start = ((), (), s32[]{:S(2)}) async-start(), calls=%async_computation.19 | async-start | bytes 2785280 | tf_op jit(solution)/shard_map/reduce_scatter | solution.py:270
  1265.0 293.5 %reduce-scatter.18.cloned.1.call-start = ((), (), s32[]{:S(2)}) async-start(), calls=%async_computation.20 | async-start | bytes 2785280 | tf_op jit(solution)/shard_map/reduce_scatter | solution.py:271
  1270.5 503.3 %reduce-scatter.22.cloned.1.call-start = ((), (), s32[]{:S(2)}) async-start(), calls=%async_computation.22 | async-start | bytes 22282240 | tf_op jit(solution)/shard_map/reduce_scatter | solution.py:272
  1285.7 703.2 %reduce-scatter.24.cloned.1.call-start = ((), (), s32[]{:S(2)}) async-start(), calls=%async_computation.23 | async-start | bytes 22282240 | tf_op jit(solution)/shard_map/reduce_scatter | solution.py:273
  1300.7 903.3 %reduce-scatter.26.cloned.1.call-start = ((), (), s32[]{:S(2)}) async-start(), calls=%async_computation.24 | async-start | bytes 22282240 | tf_op jit(solution)/shard_map/reduce_scatter | solution.py:277
  (67 other events, 196.8 us)
Sparse Core Ops, SparseCore 0:
  10.1 39.3 all-gather.9
  51.6 37.0 all-gather.11
  90.9 45.8 all-gather.7
  138.8 44.8 all-gather.13
  288.8 81.5 all-reduce.9
  372.8 87.3 all-gather.15
  462.6 86.0 all-gather.17
  551.0 88.0 all-gather.19
  679.1 73.9 all-reduce.11
  979.6 60.4 reduce-scatter.29
  1044.4 61.4 reduce-scatter.27
  1108.9 150.3 all-reduce.13
  1264.2 76.8 reduce-scatter.19
  1345.9 78.0 reduce-scatter.13
  1428.7 62.1 reduce-scatter.15
  1495.6 62.9 reduce-scatter.17
  1563.6 210.1 reduce-scatter.21
  1778.9 209.9 reduce-scatter.23
  1994.2 209.8 reduce-scatter.25
where the time goes:
time: 2220 us; the launch traced here: 2210 us
  waiting for transfers between devices  1490 us (67%)
  matrix products  400 us (18%)
  blocking collectives  115 us (5%)
  local copies, waits for them, and re-layouts  86.3 us (4%)
  other arithmetic  51.3 us (2%)
  loops' own time  46.5 us (2%)
    psum x3, waiting for transfers between devices, tensor_sum(): return lax.psum(values.astype(jnp.bfloat16), 'tp').astype(jnp.float32)  282 us
    reduce_scatter x1, waiting for transfers between devices, on_device(): lax.psum_scatter(grad_gate_weight, ('dp', 'ctx'), scatter_dimension=0, ti...  215 us
    reduce_scatter x1, waiting for transfers between devices, on_device(): lax.psum_scatter(grad_up_weight, ('dp', 'ctx'), scatter_dimension=0, tile...  215 us
    reduce_scatter x1, waiting for transfers between devices, on_device(): lax.psum_scatter(grad_down, ('dp', 'ctx'), scatter_dimension=1, tiled=True)  215 us
    dot_general x37, matrix products, contract_last(): lax.dot_general(left_rows, right_rows, (((1,), (1,)), ((), ())), preferre...  169 us
    dot_general x27, matrix products, contract_first(): lax.dot_general(left_rows, right_rows, (((0,), (0,)), ((), ())), preferre...  115 us
    unnamed x21, waiting for transfers between devices  103 us
    all_gather x1, waiting for transfers between devices, on_device(): lax.all_gather(gate_weight, ('dp', 'ctx'), axis=0, tiled=True)  83.9 us
  transfers between devices with their start and end apart: 19, of which 16 were waited for; matrix products, arithmetic and copies ran while one was open for 12% of the time, Pallas kernels for 0%

commit v1 on v0

v1 whole, which is shorter than its diff:
```python
from functools import partial

import jax
import jax.numpy as jnp
from jax import lax
from jax.experimental import pallas as pl
from jax.experimental.pallas import tpu as pltpu
from jax.sharding import PartitionSpec as P

epsilon = 1e-06
bf16 = jnp.bfloat16
f32 = jnp.float32
lanes = 128


def params(megabytes=48):
    return pltpu.CompilerParams(vmem_limit_bytes=megabytes << 20)


def cost(flops, bytes_accessed, transcendentals=0):
    return pl.CostEstimate(
        flops=int(flops), bytes_accessed=int(bytes_accessed), transcendentals=int(transcendentals)
    )


def dot_nn(left, right):
    return jnp.dot(left, right, preferred_element_type=f32)


def dot_nt(left, right):
    return lax.dot_general(left, right, (((1,), (1,)), ((), ())), preferred_element_type=f32)


def dot_tn(left, right):
    return lax.dot_general(left, right, (((0,), (0,)), ((), ())), preferred_element_type=f32)


def half_mask(shape, size):
    return lax.broadcasted_iota(jnp.int32, shape, 1) % (2 * size) < size


def swap_quarters(values, head_size):
    quarter = head_size // 2
    low = half_mask(values.shape, quarter)
    return jnp.where(low, pltpu.roll(values, lanes - quarter, 1), pltpu.roll(values, quarter, 1))


def head_sums(values, low):
    first = jnp.sum(jnp.where(low, values, 0.0), axis=1, keepdims=True)
    second = jnp.sum(jnp.where(low, 0.0, values), axis=1, keepdims=True)
    return jnp.where(low, first, second)


def prep_kernel(raw_ref, cos_ref, sin_ref, gain_ref, out_ref, *, query_blocks, head_size, scale):
    block = pl.program_id(0)
    raw = raw_ref[...]
    low = half_mask(raw.shape, head_size)
    inverse = lax.rsqrt(head_sums(raw * raw, low) * (1.0 / head_size) + epsilon)
    normed = raw * inverse * gain_ref[0]
    rotated = normed * cos_ref[...] + swap_quarters(normed, head_size) * sin_ref[...]
    is_query = block < query_blocks
    rotated = rotated * jnp.where(is_query, scale, 1.0)
    out_ref[...] = jnp.where(jnp.logical_or(is_query, low), rotated, raw).astype(bf16)


def head_prep(raw, cos_table, sin_table, gains, query_blocks, head_size, scale):
    rows, width = raw.shape
    return pl.pallas_call(
        partial(prep_kernel, query_blocks=query_blocks, head_size=head_size, scale=scale),
        grid=(width // lanes,),
        in_specs=[
            pl.BlockSpec((rows, lanes), lambda i: (0, i)),
            pl.BlockSpec((rows, lanes), lambda i: (0, 0)),
            pl.BlockSpec((rows, lanes), lambda i: (0, 0)),
            pl.BlockSpec((1, 1, lanes), lambda i: (i, 0, 0)),
        ],
        out_specs=pl.BlockSpec((rows, lanes), lambda i: (0, i)),
        out_shape=jax.ShapeDtypeStruct((rows, width), bf16),
        compiler_params=params(),
        cost_estimate=cost(rows * width * 40, rows * width * 6),
        name="head_prep",
    )(raw, cos_table, sin_table, gains)


def prep_back_kernel(
    raw_ref, grad_ref, cos_ref, sin_ref, gain_ref, out_ref, gain_out_ref, *, has_value, head_size
):
    raw = raw_ref[...]
    grad = grad_ref[...]
    low = half_mask(raw.shape, head_size)
    turned = grad * cos_ref[...] + swap_quarters(grad * sin_ref[...], head_size)
    inverse = lax.rsqrt(head_sums(raw * raw, low) * (1.0 / head_size) + epsilon)
    normed = raw * inverse
    weighted = turned * gain_ref[0]
    mean = head_sums(weighted * normed, low) * (1.0 / head_size)
    result = inverse * (weighted - normed * mean)
    if has_value:
        result = jnp.where(low, result, grad)
    out_ref[...] = result.astype(bf16)
    gain_out_ref[0] = jnp.sum(turned * normed, axis=0, keepdims=True)


def head_prep_back(raw, raw_block, grad, cos_table, sin_table, gains, has_value, head_size):
    rows, width = grad.shape
    blocks = width // lanes
    return pl.pallas_call(
        partial(prep_back_kernel, has_value=has_value, head_size=head_size),
        grid=(blocks,),
        in_specs=[
            pl.BlockSpec((rows, lanes), lambda i: (0, i + raw_block)),
            pl.BlockSpec((rows, lanes), lambda i: (0, i)),
            pl.BlockSpec((rows, lanes), lambda i: (0, 0)),
            pl.BlockSpec((rows, lanes), lambda i: (0, 0)),
            pl.BlockSpec((1, 1, lanes), lambda i: (i + raw_block, 0, 0)),
        ],
        out_specs=[
            pl.BlockSpec((rows, lanes), lambda i: (0, i)),
            pl.BlockSpec((1, 1, lanes), lambda i: (i, 0, 0)),
        ],
        out_shape=[
            jax.ShapeDtypeStruct((rows, width), bf16),
            jax.ShapeDtypeStruct((blocks, 1, lanes), f32),
        ],
        compiler_params=params(),
        cost_estimate=cost(rows * width * 60, rows * width * 10),
        name="head_prep_back",
    )(raw, grad, cos_table, sin_table, gains)


def head_lanes(pair, index, head_size):
    values = pair.astype(f32)
    if index:
        values = pltpu.roll(values, head_size, 1)
    return jnp.where(half_mask(values.shape, head_size), values, 0.0)


def diagonal_mask(keys, rows):
    return lax.broadcasted_iota(jnp.int32, (keys, rows), 0) <= lax.broadcasted_iota(
        jnp.int32, (keys, rows), 1
    )


def attn_fwd_kernel(
    slot_ref, query_ref, keys_ref, mask_ref, out_ref, inverse_ref, acc, *, prompt_here, chunk, head_size
):
    rows = query_ref.shape[0]
    prompt_keys = mask_ref.shape[1]
    cont = rows - prompt_here
    half = cont // 2
    pair = query_ref[...]
    low = half_mask((1, lanes), head_size)
    results = []
    for index in range(2):
        query = head_lanes(pair, index, head_size).astype(bf16)

        def weigh(scores, keyvalue):
            ones_value = jnp.where(low, jnp.ones((), bf16), keyvalue)
            return dot_nn(jnp.exp(scores).astype(bf16), ones_value)

        keyvalue = keys_ref[0:prompt_keys]
        scores = dot_nt(query[:prompt_here], keyvalue)
        weights = (jnp.exp(scores) * mask_ref[...]).astype(bf16)
        acc[0:prompt_here] = dot_nn(weights, jnp.where(low, jnp.ones((), bf16), keyvalue))

        acc[prompt_here:rows] = jnp.zeros((cont, lanes), f32)
        cont_query = query[prompt_here:]

        def prompt_step(step, carry):
            piece = keys_ref[pl.ds(pl.multiple_of(step * chunk, chunk), chunk)]
            acc[prompt_here:rows] += weigh(dot_nt(cont_query, piece), piece)
            return carry

        lax.fori_loop(0, prompt_keys // chunk, prompt_step, 0)
        for block in range(2):
            start = prompt_here + block * half
            piece = keys_ref[prompt_keys + block * half : prompt_keys + (block + 1) * half]
            scores = dot_nt(query[start:], piece)
            row_ids = lax.broadcasted_iota(jnp.int32, scores.shape, 0)
            key_ids = lax.broadcasted_iota(jnp.int32, scores.shape, 1)
            acc[start:rows] += weigh(jnp.where(key_ids <= row_ids, scores, -1e30), piece)
        total = acc[...]
        results.append((total, pltpu.roll(total, head_size, 1)))
    first, first_moved = results[0]
    second, second_moved = results[1]
    full_low = half_mask((rows, lanes), head_size)
    inverse = 1.0 / jnp.where(full_low, first, second_moved)
    inverse_ref[...] = inverse
    out_ref[...] = (jnp.where(full_low, first_moved, second) * inverse).astype(bf16)


def attention_forward(slots, rotated, keys, prompt_mask, pairs, prompt_here, head_size):
    rows = rotated.shape[0]
    key_count = keys.shape[0]
    prompt_keys = prompt_mask.shape[1]
    chunk = min(512, prompt_keys)
    elements = 2 * pairs * rows * key_count
    return pl.pallas_call(
        partial(attn_fwd_kernel, prompt_here=prompt_here, chunk=chunk, head_size=head_size),
        grid_spec=pltpu.PrefetchScalarGridSpec(
            num_scalar_prefetch=1,
            grid=(pairs,),
            in_specs=[
                pl.BlockSpec((rows, lanes), lambda p, s: (0, p)),
                pl.BlockSpec((key_count, lanes), lambda p, s: (0, s[p])),
                pl.BlockSpec(prompt_mask.shape, lambda p, s: (0, 0)),
            ],
            out_specs=[
                pl.BlockSpec((rows, lanes), lambda p, s: (0, p)),
                pl.BlockSpec((rows, lanes), lambda p, s: (0, p)),
            ],
            scratch_shapes=[pltpu.VMEM((rows, lanes), f32)],
        ),
        out_shape=[
            jax.ShapeDtypeStruct((rows, pairs * lanes), bf16),
            jax.ShapeDtypeStruct((rows, pairs * lanes), f32),
        ],
        compiler_params=params(),
        cost_estimate=cost(elements * 1000, elements, elements),
        name="attention_forward",
    )(slots, rotated, keys, prompt_mask)


def attn_back_kernel(
    slot_ref,
    query_ref,
    keys_ref,
    mask_ref,
    attended_ref,
    inverse_ref,
    grad_ref,
    grad_query_ref,
    grad_keys_ref,
    q_sc,
    g_sc,
    d_sc,
    dq_sc,
    *,
    prompt_here,
    chunk,
    head_size,
):
    step_id = pl.program_id(0)
    rows = query_ref.shape[0]
    prompt_keys = mask_ref.shape[0]
    cont = rows - prompt_here
    half = cont // 2
    low = half_mask((1, lanes), head_size)
    full_low = half_mask((rows, lanes), head_size)
    lane_ids = lax.broadcasted_iota(jnp.int32, (rows, lanes), 1)

    fresh = jnp.logical_or(
        step_id == 0, slot_ref[step_id] != slot_ref[jnp.maximum(step_id - 1, 0)]
    )

    @pl.when(fresh)
    def _():
        grad_keys_ref[...] = jnp.zeros_like(grad_keys_ref)

    pair = query_ref[...]
    grad_pair = grad_ref[...].astype(f32)
    inverse = inverse_ref[...]
    product = grad_pair * attended_ref[...].astype(f32)
    delta = head_sums(product, full_low) * inverse
    scaled = grad_pair * inverse
    for index in range(2):
        grad_high = scaled if index else pltpu.roll(scaled, head_size, 1)
        delta_low = pltpu.roll(delta, head_size, 1) if index else delta
        delta_high_part = delta_low.astype(bf16).astype(f32)
        extra = jnp.where(
            lane_ids == 0, -delta_high_part, jnp.where(lane_ids == 1, delta_high_part - delta_low, 0.0)
        )
        q_sc[index] = head_lanes(pair, index, head_size).astype(bf16)
        g_sc[index] = jnp.where(full_low, 0.0, grad_high).astype(bf16)
        d_sc[index] = jnp.where(full_low, extra, grad_high).astype(bf16)
    dq_sc[...] = jnp.zeros_like(dq_sc)

    def block(key_start, key_size, row_start, row_stop, mask):
        piece = keys_ref[pl.ds(key_start, key_size)]
        ones_value = jnp.where(low, jnp.ones((), bf16), piece)
        count = row_stop - row_start

        def rows_of(ref):
            return jnp.concatenate([ref[0, row_start:row_stop], ref[1, row_start:row_stop]], axis=0)

        query = rows_of(q_sc)
        weights = jnp.exp(dot_nt(piece, query))
        if mask is not None:
            weights = mask(weights)
        grad_scores = (weights * dot_nt(ones_value, rows_of(d_sc))).astype(bf16)
        grad_keys_ref[pl.ds(key_start, key_size)] += dot_nn(grad_scores, query) + dot_nn(
            weights.astype(bf16), rows_of(g_sc)
        )
        grad_query = dot_tn(grad_scores, piece)
        dq_sc[0, row_start:row_stop] += grad_query[:count]
        dq_sc[1, row_start:row_stop] += grad_query[count:]

    def prompt_mask(weights):
        mask = mask_ref[...]
        return weights * jnp.concatenate([mask, mask], axis=1)

    block(0, prompt_keys, 0, prompt_here, prompt_mask)

    def prompt_step(step, carry):
        block(pl.multiple_of(step * chunk, chunk), chunk, prompt_here, rows, None)
        return carry

    lax.fori_loop(0, prompt_keys // chunk, prompt_step, 0)
    for part in range(2):
        start = prompt_here + part * half

        def causal(weights, size=rows - start):
            key_ids = lax.broadcasted_iota(jnp.int32, weights.shape, 0)
            row_ids = lax.broadcasted_iota(jnp.int32, weights.shape, 1)
            row_ids = jnp.where(row_ids < size, row_ids, row_ids - size)
            return jnp.where(key_ids <= row_ids, weights, 0.0)

        block(prompt_keys + part * half, half, start, rows, causal)
    moved = pltpu.roll(dq_sc[1], head_size, 1)
    grad_query_ref[...] = jnp.where(full_low, dq_sc[0], moved) * 0.125


def attention_backward(
    slots, rotated, keys, prompt_mask_t, attended, inverse, grad_attended, pairs, slot_count, prompt_here, head_size
):
    rows = rotated.shape[0]
    key_count = keys.shape[0]
    prompt_keys = prompt_mask_t.shape[0]
    chunk = min(512, prompt_keys)
    elements = 2 * pairs * rows * key_count
    pair_spec = pl.BlockSpec((rows, lanes), lambda p, s: (0, p))
    return pl.pallas_call(
        partial(attn_back_kernel, prompt_here=prompt_here, chunk=chunk, head_size=head_size),
        grid_spec=pltpu.PrefetchScalarGridSpec(
            num_scalar_prefetch=1,
            grid=(pairs,),
            in_specs=[
                pair_spec,
                pl.BlockSpec((key_count, lanes), lambda p, s: (0, s[p])),
                pl.BlockSpec(prompt_mask_t.shape, lambda p, s: (0, 0)),
                pair_spec,
                pair_spec,
                pair_spec,
            ],
            out_specs=[
                pair_spec,
                pl.BlockSpec((key_count, lanes), lambda p, s: (0, s[p])),
            ],
            scratch_shapes=[
                pltpu.VMEM((2, rows, lanes), bf16),
                pltpu.VMEM((2, rows, lanes), bf16),
                pltpu.VMEM((2, rows, lanes), bf16),
                pltpu.VMEM((2, rows, lanes), f32),
            ],
        ),
        out_shape=[
            jax.ShapeDtypeStruct((rows, pairs * lanes), f32),
            jax.ShapeDtypeStruct((key_count, slot_count * lanes), f32),
        ],
        compiler_params=params(),
        cost_estimate=cost(elements * 2500, elements, elements),
        name="attention_backward",
    )(slots, rotated, keys, prompt_mask_t, attended, inverse, grad_attended)


def ff_forward_kernel(rows_ref, gate_ref, up_ref, hidden_ref, gate_factor_ref, up_factor_ref):
    rows = rows_ref[...]
    gate = dot_nn(rows, gate_ref[...])
    up = dot_nn(rows, up_ref[...])
    sigmoid = 1.0 / (1.0 + jnp.exp(-gate))
    silu = gate * sigmoid
    hidden_ref[...] = (silu * up).astype(bf16)
    gate_factor_ref[...] = (up * sigmoid * (1.0 + gate * (1.0 - sigmoid))).astype(bf16)
    up_factor_ref[...] = silu.astype(bf16)


def ff_forward(rows, weights, units, tile=256):
    count, depth = rows.shape
    tiles = units // tile
    out = pl.BlockSpec((count, tile), lambda j: (0, j))
    return pl.pallas_call(
        ff_forward_kernel,
        grid=(tiles,),
        in_specs=[
            pl.BlockSpec((count, depth), lambda j: (0, 0)),
            pl.BlockSpec((depth, tile), lambda j: (0, j)),
            pl.BlockSpec((depth, tile), lambda j: (0, j + tiles)),
        ],
        out_specs=[out, out, out],
        out_shape=[jax.ShapeDtypeStruct((count, units), bf16)] * 3,
        compiler_params=params(),
        cost_estimate=cost(4 * count * depth * units, 4 * depth * units, count * units),
        name="ff_forward",
    )(rows, weights, weights)


def matmul_nt_kernel(left_ref, right_ref, out_ref):
    out_ref[...] = dot_nt(left_ref[...], right_ref[...]).astype(bf16)


def matmul_nt(left, weights, column_block, tile=256):
    count, depth = left.shape
    wide = weights.shape[0]
    return pl.pallas_call(
        matmul_nt_kernel,
        grid=(wide // tile,),
        in_specs=[
            pl.BlockSpec((count, depth), lambda j: (0, 0)),
            pl.BlockSpec((tile, depth), lambda j: (j, column_block)),
        ],
        out_specs=pl.BlockSpec((count, tile), lambda j: (0, j)),
        out_shape=jax.ShapeDtypeStruct((count, wide), bf16),
        compiler_params=params(),
        cost_estimate=cost(2 * count * depth * wide, 2 * depth * wide),
        name="matmul_nt",
    )(left, weights)


def ff_back_kernel(grad_ref, weight_ref, gate_factor_ref, up_factor_ref, gate_ref, up_ref):
    grad_hidden = dot_nn(grad_ref[...], weight_ref[...])
    gate_ref[...] = (grad_hidden * gate_factor_ref[...].astype(f32)).astype(bf16)
    up_ref[...] = (grad_hidden * up_factor_ref[...].astype(f32)).astype(bf16)


def ff_backward(grad_out, weights, gate_factor, up_factor, tile=256):
    count, depth = grad_out.shape
    units = gate_factor.shape[1]
    tiles = units // tile
    out = pl.BlockSpec((count, tile), lambda j: (0, j))
    return pl.pallas_call(
        ff_back_kernel,
        grid=(tiles,),
        in_specs=[
            pl.BlockSpec((count, depth), lambda j: (0, 0)),
            pl.BlockSpec((depth, tile), lambda j: (0, j + 2 * tiles)),
            out,
            out,
        ],
        out_specs=[out, out],
        out_shape=[jax.ShapeDtypeStruct((count, units), bf16)] * 2,
        compiler_params=params(),
        cost_estimate=cost(2 * count * depth * units, 2 * depth * units),
        name="ff_backward",
    )(grad_out, weights, gate_factor, up_factor)


def ff_input_kernel(gate_ref, up_ref, gate_weight_ref, up_weight_ref, out_ref):
    out_ref[...] = (
        dot_nt(gate_ref[...], gate_weight_ref[...]) + dot_nt(up_ref[...], up_weight_ref[...])
    ).astype(bf16)


def ff_input_grad(grad_gate, grad_up, weights, tile=256):
    count, units = grad_gate.shape
    wide = weights.shape[0]
    full = pl.BlockSpec((count, units), lambda j: (0, 0))
    return pl.pallas_call(
        ff_input_kernel,
        grid=(wide // tile,),
        in_specs=[
            full,
            full,
            pl.BlockSpec((tile, units), lambda j: (j, 0)),
            pl.BlockSpec((tile, units), lambda j: (j, 1)),
        ],
        out_specs=pl.BlockSpec((count, tile), lambda j: (0, j)),
        out_shape=jax.ShapeDtypeStruct((count, wide), bf16),
        compiler_params=params(),
        cost_estimate=cost(4 * count * units * wide, 4 * units * wide),
        name="ff_input_grad",
    )(grad_gate, grad_up, weights, weights)


def weight_grad_kernel(*refs, pieces, add):
    index_ref = refs[0]
    left = jnp.concatenate([ref[...] for ref in refs[1 : 1 + pieces]], axis=0)
    own_ref, other_ref = refs[1 + pieces : 3 + pieces]
    out_ref = refs[-1]
    right = jnp.concatenate([own_ref[...], other_ref[...]], axis=0)
    product = dot_nn(left, right)
    rows = left.shape[0] // pieces
    for piece in range(pieces):
        part = product[piece * rows : (piece + 1) * rows]
        if add:
            part = part + refs[-2][piece].astype(f32)
        out_ref[piece] = part.astype(bf16)


def weight_grad(indices, block, left_t, own, other, received=None):
    pieces = indices.shape[0]
    depth = left_t.shape[1]
    count, wide = own.shape
    tile = 512 if wide % 512 == 0 else 640 if wide % 640 == 0 else lanes
    out = pl.BlockSpec((pieces, block, tile), lambda j, s: (0, 0, j))
    in_specs = [
        pl.BlockSpec((block, depth), lambda j, s, piece=piece: (s[piece], 0)) for piece in range(pieces)
    ]
    in_specs += [pl.BlockSpec((count, tile), lambda j, s: (0, j))] * 2
    operands = [left_t] * pieces + [own, other]
    if received is not None:
        in_specs.append(out)
        operands.append(received)
    return pl.pallas_call(
        partial(weight_grad_kernel, pieces=pieces, add=received is not None),
        grid_spec=pltpu.PrefetchScalarGridSpec(
            num_scalar_prefetch=1,
            grid=(wide // tile,),
            in_specs=in_specs,
            out_specs=out,
        ),
        out_shape=jax.ShapeDtypeStruct((pieces, block, wide), bf16),
        compiler_params=params(),
        cost_estimate=cost(2 * pieces * block * depth * wide, 2 * (pieces * block + depth) * wide),
        name="weight_grad",
    )(indices, *operands)


def on_device(
    prompt_states,
    continuation_states,
    continuation_offset,
    attention_gain,
    query_weight,
    key_weight,
    value_weight,
    query_gain,
    key_gain,
    output_weight,
    feedforward_gain,
    gate_weight,
    up_weight,
    down_weight,
    grad_prompt,
    grad_continuation,
):
    ring = lax.axis_size("ctx")
    tensor_size = lax.axis_size("tp")
    zsize, ysize = ring // 2, 2
    prompt_here, width = prompt_states.shape
    cont_length = continuation_states.shape[0]
    rows_here = prompt_here + cont_length
    prompt_length = prompt_here * ring
    head_size = query_gain.shape[0]
    query_width = query_weight.shape[1]
    local_heads = query_width // head_size
    shared_heads = key_weight.shape[1] // head_size
    group_size = local_heads * tensor_size // shared_heads
    pairs = local_heads // 2
    units = gate_weight.shape[1]
    half_width = width // 2
    block = half_width // ring
    low_head = [t * local_heads // group_size for t in range(tensor_size)]
    slot_count = max(
        ((t + 1) * local_heads - 1) // group_size - low_head[t] + 1 for t in range(tensor_size)
    )

    data_rank = lax.axis_index("dp")
    context_rank = lax.axis_index("ctx")
    tensor_rank = lax.axis_index("tp")
    zrank, yrank = context_rank // ysize, context_rank % ysize
    first_shared = tensor_rank * local_heads // group_size

    def z_pass(values, shift):
        pairs_of = [
            (z * ysize + y, (z + shift) % zsize * ysize + y) for z in range(zsize) for y in range(ysize)
        ]
        return lax.ppermute(values, "ctx", pairs_of)

    def y_swap(values):
        return lax.ppermute(values, "ctx", [(i, i ^ 1) for i in range(ring)])

    def dp_swap(values):
        return lax.ppermute(values, "dp", [(0, 1), (1, 0)])

    def tp_swap(values):
        return lax.ppermute(values, "tp", [(0, 1), (1, 0)])

    def shared_slots(weight):
        return lax.dynamic_slice_in_dim(weight, first_shared * head_size, slot_count * head_size, 1).reshape(
            -1, slot_count, head_size
        )

    key_value_weight = jnp.concatenate(
        [shared_slots(key_weight), shared_slots(value_weight)], axis=2
    ).reshape(-1, slot_count * lanes)
    qkv_width = query_width + slot_count * lanes
    attn_weights = lax.all_gather(
        jnp.concatenate([query_weight, key_value_weight, output_weight.T], axis=1),
        ("dp", "ctx"),
        axis=0,
        tiled=True,
    )
    ff_weights = lax.all_gather(
        jnp.concatenate([gate_weight, up_weight, down_weight.T], axis=1),
        ("dp", "ctx"),
        axis=0,
        tiled=True,
    )
    qkv_weights = attn_weights[:, :qkv_width]
    out_weights_t = attn_weights[:, qkv_width:]

    row_ids = jnp.arange(rows_here, dtype=jnp.int32)
    positions = jnp.where(
        row_ids < prompt_here,
        context_rank * prompt_here + row_ids,
        prompt_length + continuation_offset[0] + row_ids - prompt_here,
    ).astype(f32)
    freqs = 10000.0 ** (-(2.0 * jnp.arange(head_size // 2, dtype=f32)) / head_size)
    angles = positions[:, None] * freqs[None, :]
    cosine, sine = jnp.cos(angles), jnp.sin(angles)
    cos_table = jnp.concatenate([cosine] * 4, axis=1)
    sin_table = jnp.concatenate([-sine, sine] * 2, axis=1)
    query_gain32, key_gain32 = query_gain.astype(f32), key_gain.astype(f32)
    gains = jnp.concatenate(
        [
            jnp.broadcast_to(jnp.concatenate([query_gain32] * 2), (pairs, 1, lanes)),
            jnp.broadcast_to(
                jnp.concatenate([key_gain32, jnp.ones((head_size,), f32)]), (slot_count, 1, lanes)
            ),
        ],
        axis=0,
    )
    steps = jnp.arange(zsize, dtype=jnp.int32)
    zs = (zrank + steps) % zsize
    own_blocks = zs * ysize + yrank
    other_blocks = zs * ysize + (1 - yrank)
    chunk_order = jnp.concatenate([own_blocks, other_blocks])
    key_places = jnp.repeat(chunk_order * prompt_here, prompt_here) + jnp.tile(
        jnp.arange(prompt_here, dtype=jnp.int32), ring
    )
    query_places = context_rank * prompt_here + jnp.arange(prompt_here, dtype=jnp.int32)
    prompt_mask = (key_places[None, :] <= query_places[:, None]).astype(f32)
    prompt_mask_t = (key_places[:, None] <= query_places[None, :]).astype(f32)
    slots = (
        (tensor_rank * local_heads + 2 * jnp.arange(pairs, dtype=jnp.int32)) // group_size - first_shared
    ).astype(jnp.int32)

    inputs = jnp.concatenate([prompt_states, continuation_states], axis=0).astype(f32)
    attn_gain32 = attention_gain.astype(f32)
    ff_gain32 = feedforward_gain.astype(f32)
    first_scale = lax.rsqrt(jnp.mean(inputs * inputs, axis=-1, keepdims=True) + epsilon)
    normed_low = (inputs * first_scale * attn_gain32).astype(bf16)
    raw = dot_nn(normed_low, qkv_weights)
    rotated = head_prep(raw, cos_table, sin_table, gains, pairs, head_size, 0.125)
    key_value = rotated[:, query_width:]
    own_chunk = key_value[:prompt_here]
    z_chunks = [own_chunk] + [z_pass(own_chunk, zsize - step) for step in range(1, zsize)]
    z_part = jnp.concatenate(z_chunks, axis=0)
    keys = jnp.concatenate([z_part, y_swap(z_part), key_value[prompt_here:]], axis=0)
    attended, inverse = attention_forward(
        slots, rotated, keys, prompt_mask, pairs, prompt_here, head_size
    )
    attn_part = dot_nt(attended, out_weights_t).astype(bf16)
    resid = inputs + (attn_part.astype(f32) + tp_swap(attn_part).astype(f32))
    second_scale = lax.rsqrt(jnp.mean(resid * resid, axis=-1, keepdims=True) + epsilon)
    second_normed = resid * second_scale
    normed_two = (second_normed * ff_gain32).astype(bf16)
    hidden, gate_factor, up_factor = ff_forward(normed_two, ff_weights, units)
    ff_part = matmul_nt(hidden, ff_weights, 2)
    output = (resid + (ff_part.astype(f32) + tp_swap(ff_part).astype(f32))).astype(bf16)

    def columns_of(values, rank):
        return lax.dynamic_slice_in_dim(values, rank * half_width, half_width, 1)

    def both_rows_t(values):
        received = dp_swap(columns_of(values, 1 - data_rank))
        return jnp.concatenate([columns_of(values, data_rank), received], axis=0).T

    def reduced(left_t, own):
        other = dp_swap(own)
        sent = y_swap(weight_grad(other_blocks, block, left_t, own, other))
        kept = weight_grad(own_blocks, block, left_t, own, other, sent)
        total = kept[0].astype(f32)
        for step in range(1, zsize):
            total = total + z_pass(kept[step], step).astype(f32)
        return total

    grad_out = jnp.concatenate([grad_prompt, grad_continuation], axis=0)
    grad_out_t = both_rows_t(grad_out)
    down_done = reduced(grad_out_t, hidden).T

    grad_gate, grad_up = ff_backward(grad_out, ff_weights, gate_factor, up_factor)
    normed_two_t = both_rows_t(normed_two)
    gate_done = reduced(normed_two_t, grad_gate)
    up_done = reduced(normed_two_t, grad_up)
    grad_part = ff_input_grad(grad_gate, grad_up, ff_weights)
    grad_normed_two = grad_part.astype(f32) + tp_swap(grad_part).astype(f32)

    def norm_back(grad_rows, normed_rows, scale, gain):
        weighted = grad_rows * gain
        mean = jnp.mean(weighted * normed_rows, axis=-1, keepdims=True)
        return scale * (weighted - normed_rows * mean), jnp.sum(grad_rows * normed_rows, axis=0)

    grad_resid_part, grad_ff_gain = norm_back(grad_normed_two, second_normed, second_scale, ff_gain32)
    grad_resid = grad_out.astype(f32) + grad_resid_part
    grad_resid_low = grad_resid.astype(bf16)
    grad_attended = dot_nn(grad_resid_low, out_weights_t).astype(bf16)
    out_done = reduced(both_rows_t(grad_resid_low), attended).T

    grad_query, grad_keys = attention_backward(
        slots,
        rotated,
        keys,
        prompt_mask_t,
        attended,
        inverse,
        grad_attended,
        pairs,
        slot_count,
        prompt_here,
        head_size,
    )
    grad_keys_prompt = grad_keys[:prompt_length].astype(bf16)
    half_prompt = prompt_length // 2
    kept_keys = grad_keys_prompt[:half_prompt].astype(f32) + y_swap(grad_keys_prompt[half_prompt:]).astype(f32)
    kept_keys = kept_keys.astype(bf16)
    own_keys = kept_keys[:prompt_here].astype(f32)
    for step in range(1, zsize):
        own_keys = own_keys + z_pass(
            kept_keys[step * prompt_here : (step + 1) * prompt_here], step
        ).astype(f32)
    grad_key_value = jnp.concatenate([own_keys, grad_keys[prompt_length:]], axis=0)
    grad_query_low, query_gain_parts = head_prep_back(
        raw, 0, grad_query, cos_table, sin_table, gains, False, head_size
    )
    grad_shared_low, key_gain_parts = head_prep_back(
        raw, pairs, grad_key_value, cos_table, sin_table, gains, True, head_size
    )
    grad_qkv = jnp.concatenate([grad_query_low, grad_shared_low], axis=1)
    qkv_done = reduced(both_rows_t(normed_low), grad_qkv)
    qkv_part = dot_nt(grad_qkv, qkv_weights).astype(bf16)
    grad_normed = qkv_part.astype(f32) + tp_swap(qkv_part).astype(f32)
    grad_input_part, grad_attn_gain = norm_back(grad_normed, inputs * first_scale, first_scale, attn_gain32)
    grad_input = (grad_resid + grad_input_part).astype(bf16)

    shared_done = qkv_done[:, query_width:]
    shared_other = tp_swap(shared_done)
    from_first = jnp.where(tensor_rank == 0, shared_done, shared_other)
    from_second = jnp.where(tensor_rank == 0, shared_other, shared_done)

    def all_heads(values, offset, which):
        block = values.reshape(-1, slot_count, 2, head_size)[:, :, which].reshape(-1, slot_count * head_size)
        before = offset * head_size
        after = shared_heads * head_size - before - slot_count * head_size
        return jnp.pad(block, ((0, 0), (before, after)))

    key_done, value_done = (
        all_heads(from_first, low_head[0], which) + all_heads(from_second, low_head[1], which)
        for which in range(2)
    )

    query_gain_sum = jnp.sum(query_gain_parts.reshape(-1, head_size), axis=0)
    key_gain_sum = jnp.sum(key_gain_parts[:, 0, :head_size], axis=0)
    head_gains = jnp.concatenate([query_gain_sum, key_gain_sum])
    head_gains = head_gains + tp_swap(head_gains)
    gain_sums = jnp.concatenate([grad_attn_gain, grad_ff_gain, head_gains]).reshape(-1, lanes)
    gain_sums = gain_sums + dp_swap(gain_sums)
    gain_sums = gain_sums + y_swap(gain_sums)
    gain_total = gain_sums
    for step in range(1, zsize):
        gain_total = gain_total + z_pass(gain_sums, step)
    gain_total = gain_total.reshape(-1)
    return (
        output[:prompt_here],
        output[prompt_here:],
        grad_input[:prompt_here],
        grad_input[prompt_here:],
        gain_total[:width],
        qkv_done[:, :query_width],
        key_done,
        value_done,
        gain_total[2 * width : 2 * width + head_size],
        gain_total[2 * width + head_size :],
        out_done,
        gain_total[width : 2 * width],
        gate_done,
        up_done,
        down_done,
    )


def solution(mesh):
    in_specs = (
        P(("dp", "ctx"), None),
        P(("dp", "ctx"), None),
        P(("dp", "ctx")),
        P(),
        P(("dp", "ctx"), "tp"),
        P(("dp", "ctx"), None),
        P(("dp", "ctx"), None),
        P(),
        P(),
        P("tp", ("dp", "ctx")),
        P(),
        P(("dp", "ctx"), "tp"),
        P(("dp", "ctx"), "tp"),
        P("tp", ("dp", "ctx")),
        P(("dp", "ctx"), None),
        P(("dp", "ctx"), None),
    )
    out_specs = (
        P(("dp", "ctx"), None),
        P(("dp", "ctx"), None),
        P(("dp", "ctx"), None),
        P(("dp", "ctx"), None),
        P(),
        P(("dp", "ctx"), "tp"),
        P(("dp", "ctx"), None),
        P(("dp", "ctx"), None),
        P(),
        P(),
        P("tp", ("dp", "ctx")),
        P(),
        P(("dp", "ctx"), "tp"),
        P(("dp", "ctx"), "tp"),
        P("tp", ("dp", "ctx")),
    )
    return jax.shard_map(
        on_device, mesh=mesh, in_specs=in_specs, out_specs=out_specs, check_vma=False
    )
```

time: 2220 us -> 869 us (0.39)
  waiting for transfers between devices: 1490 us -> 445 us
  matrix products: 400 us -> 24.4 us
  Pallas kernels: 0 us -> 187 us
  blocking collectives: 115 us -> 0 us
  starting transfers between devices: 1.23 us -> 48.6 us
  loops' own time: 46.5 us -> 0 us
    reduce_scatter x7 -> x0, waiting for transfers between devices: 805 us -> none  [the longest x1 215 us: on_device(): lax.psum_scatter(grad_gate_weight, ('dp', 'ctx'), scatter_dimension=0, ti...]
    dot_general x91 -> x4, matrix products: 400 us -> 24.4 us  [the longest x2 13.8 us: dot_nt(): lax.dot_general(left, right, (((1,), (1,)), ((), ())), preferred_element_...]
    ppermute x0 -> x48, waiting for transfers between devices: none -> 353 us  [the longest x24 139 us: z_pass(): return lax.ppermute(values, 'ctx', pairs_of)]
    psum x3 -> x0, waiting for transfers between devices: 282 us -> none  [tensor_sum(): return lax.psum(values.astype(jnp.bfloat16), 'tp').astype(jnp.float32)]
    all_gather x7 -> x2, waiting for transfers between devices: 304 us -> 92.3 us  [the longest x1 56.6 us: on_device(): lax.all_gather(jnp.concatenate([query_weight, key_value_weight, output_we...]
    pallas_call x0 -> x19, Pallas kernels: none -> 187 us  [the longest x10 61 us: weight_grad(): pl.pallas_call(partial(weight_grad_kernel, pieces=pieces, add=received is...]
    unnamed x21 -> x2, waiting for transfers between devices: 103 us -> 0.03 us
    psum x2 -> x0, blocking collectives: 65.3 us -> none  [the longest x1 61 us: on_device(): lax.psum((grad_attn_gain, grad_ffn_gain, grad_query_gain, grad_key_gain),...]
  transfers between devices with their start and end apart: 19 -> 50, of which waited for: 16 -> 25; matrix products, arithmetic and copies ran while one was open for 12% -> 16% of each run, Pallas kernels for 0% -> 15%
where the time goes in v1:
time: 869 us; the launch traced here: 861 us
  waiting for transfers between devices  445 us (51%)
  Pallas kernels  187 us (22%)
  local copies, waits for them, and re-layouts  80.9 us (9%)
  other arithmetic  58.8 us (7%)
  starting transfers between devices  48.6 us (6%)
  matrix products  24.4 us (3%)
  between operations  16.3 us (2%)
    ppermute x24, waiting for transfers between devices, z_pass(): return lax.ppermute(values, 'ctx', pairs_of)  139 us
    ppermute x8, waiting for transfers between devices, y_swap(): return lax.ppermute(values, 'ctx', [(i, i ^ 1) for i in range(ring)])  121 us
    ppermute x6, waiting for transfers between devices, tp_swap(): return lax.ppermute(values, 'tp', [(0, 1), (1, 0)])  91.7 us
    pallas_call x10, Pallas kernels, weight_grad(): pl.pallas_call(partial(weight_grad_kernel, pieces=pieces, add=received is...  61 us
    all_gather x1, waiting for transfers between devices, on_device(): lax.all_gather(jnp.concatenate([query_weight, key_value_weight, output_we...  56.6 us
    unnamed x143, local copies, waits for them, and re-layouts  43.1 us
    all_gather x1, waiting for transfers between devices, on_device(): lax.all_gather(jnp.concatenate([gate_weight, up_weight, down_weight.T], a...  35.8 us
    pallas_call x1, Pallas kernels, attention_backward(): pl.pallas_call(partial(attn_back_kernel, prompt_here=prompt_here, chunk=c...  31 us
  transfers between devices with their start and end apart: 50, of which 25 were waited for; matrix products, arithmetic and copies ran while one was open for 16% of the time, Pallas kernels for 15%

profile of v1, /device:TPU:9, one launch (start us, length us, event | category | flops | bytes accessed | tf_op | source)
XLA Modules:
  0.0 861.0 jit_solution(10209528025929230368)
XLA Ops:
  23.1 56.6 %all-gather.3.cloned.1.call-done = bf16[2048,1664]{0,1:T(8,128)(2,1)} async-done(((bf16[128,1664]{0,1:T(8,128)(2,1)}), bf16[2048,1664]{0,1:T(8,128)(2,1)}) %all-gather.3.cloned.1.call-update) | async-done | bytes 6815760 | tf_op jit(solution)/shard_map/all_gather | solution.py:586
  79.7 5.5 fusion.16.raw_ref
  97.0 5.2 collective-permute-done.1
  107.2 9.1 %collective-permute-done.3 = bf16[512,384]{1,0:T(8,128)(2,1)S(1)} collective-permute-done((bf16[512,384]{1,0:T(8,128)(2,1)S(1)}, bf16[512,384]{1,0:T(8,128)(2,1)S(1)}, u32[]{:S(2)}, u32[]{:S(2)}) %collective-permute-start.3) | collective-permute-done | bytes 393248 | tf_op jit(solution)/shard_map/ppermute | solution.py:569
  116.4 18.8 %attention_forward.1 = (bf16[640,640]{1,0:T(8,128)(2,1)}, f32[640,640]{1,0:T(8,128)S(1)}) custom-call(s32[5]{0:T(128)S(1)} %fusion.44.slot_ref, bf16[640,1024]{1,0:T(8,128)(2,1)S(1)} %head_prep.1.query_ref, bf16[1536,384]{1,0:T(8,128)(2,1)S(1)} %slice_dynamic-update-slice_fusion.keys_ref, f32[128,1024]{1,0:T(8,128)S(1)} %compare_convert_fusion.1.mask_ref), custom_call_target="tpu_custom_call" | custom-call | flops 9830400000 | bytes 9830400 | tf_op jit(solution)/shard_map/attention_forward/pallas_call | solution.py:197
  135.2 6.7 convolution_convert_fusion
  153.3 45.5 %collective-permute-done.4 = bf16[640,2048]{0,1:T(8,128)(2,1)} collective-permute-done((bf16[640,2048]{0,1:T(8,128)(2,1)}, bf16[640,2048]{0,1:T(8,128)(2,1)}, u32[]{:S(2)}, u32[]{:S(2)}) %collective-permute-start.4) | collective-permute-done | bytes 2621472 | tf_op jit(solution)/shard_map/ppermute | solution.py:575
  212.2 35.8 %all-gather.5.cloned.1.call-done.gate_ref.up_ref.right_ref.weight_ref.gate_weight_ref.up_weight_ref = bf16[2048,7680]{1,0:T(8,128)(2,1)} async-done(((bf16[128,7680]{1,0:T(8,128)(2,1)}), bf16[2048,7680]{1,0:T(8,128)(2,1)}) %all-gather.5.cloned.1.call-update) | async-done | bytes 31457296 | tf_op jit(solution)/shard_map/all_gather | solution.py:592
  249.7 20.6 %ff_forward.1 = (bf16[640,2560]{1,0:T(8,128)(2,1)}, bf16[640,2560]{1,0:T(8,128)(2,1)}, bf16[640,2560]{1,0:T(8,128)(2,1)}) custom-call(bf16[640,2048]{1,0:T(8,128)(2,1)S(1)} %copy-done.5, bf16[2048,7680]{1,0:T(8,128)(2,1)} %all-gather.5.cloned.1.call-done.gate_ref.up_ref.right_ref.weight_ref.gate_weight_ref.up_weight_ref, ...), custom_call_target="tpu_custom_call" | custom-call | flops 13421772800 | bytes 20971520 | tf_op jit(solution)/shard_map/ff_forward/pallas_call | solution.py:380
  270.3 14.6 %ff_backward.1 = (bf16[640,2560]{1,0:T(8,128)(2,1)}, bf16[640,2560]{1,0:T(8,128)(2,1)}) custom-call(bf16[640,2048]{1,0:T(8,128)(2,1)S(1)} %copy.88.grad_ref, bf16[2048,7680]{1,0:T(8,128)(2,1)} %all-gather.5.cloned.1.call-done.gate_ref.up_ref.right_ref.weight_ref.gate_weight_ref.up_weight_ref, bf16[640,2560]{1,0:T(8,128)(2,1)} %get-tuple-element.30.gate_factor_ref, ...), custom_call_target="tpu_custom_call" | custom-call | flops 6710886400 | bytes 10485760 | tf_op jit(solution)/shard_map/ff_backward/pallas_call | solution.py:429
  284.9 19.1 %ff_input_grad.1 = bf16[640,2048]{1,0:T(8,128)(2,1)S(1)} custom-call(bf16[640,2560]{1,0:T(8,128)(2,1)} %get-tuple-element.32.gate_ref.refs_5_, bf16[640,2560]{1,0:T(8,128)(2,1)} %get-tuple-element.33.up_ref.refs_5_, bf16[2048,7680]{1,0:T(8,128)(2,1)} %all-gather.5.cloned.1.call-done.gate_ref.up_ref.right_ref.weight_ref.gate_weight_ref.up_weight_ref, ...), custom_call_target="tpu_custom_call" | custom-call | flops 13421772800 | bytes 20971520 | tf_op jit(solution)/shard_map/ff_input_grad/pallas_call | solution.py:456
  320.4 45.1 %collective-permute-done.6 = bf16[640,2048]{0,1:T(8,128)(2,1)} collective-permute-done((bf16[640,2048]{0,1:T(8,128)(2,1)}, bf16[640,2048]{0,1:T(8,128)(2,1)}, u32[]{:S(2)}, u32[]{:S(2)}) %collective-permute-start.6) | collective-permute-done | bytes 2621472 | tf_op jit(solution)/shard_map/ppermute | solution.py:575
  372.0 5.0 fusion.24.grad_ref
  377.0 31.0 %attention_backward.1 = (f32[640,640]{1,0:T(8,128)}, f32[1536,384]{1,0:T(8,128)}) custom-call(s32[5]{0:T(128)S(1)} %fusion.44.slot_ref, bf16[640,1024]{1,0:T(8,128)(2,1)S(1)} %copy-done.16, bf16[1536,384]{1,0:T(8,128)(2,1)S(1)} %copy-done.24, f32[1024,128]{1,0:T(8,128)S(1)} %compare_convert_fusion.mask_ref, ...), custom_call_target="tpu_custom_call" | custom-call | flops 24576000000 | bytes 9830400 | tf_op jit(solution)/shard_map/attention_backward/pallas_call | solution.py:331
  420.5 11.8 %matmul_nt.1 = bf16[640,2048]{1,0:T(8,128)(2,1)S(1)} custom-call(bf16[640,2560]{1,0:T(8,128)(2,1)} %get-tuple-element.29.left_ref.refs_5_, bf16[2048,7680]{1,0:T(8,128)(2,1)} %all-gather.5.cloned.1.call-done.gate_ref.up_ref.right_ref.weight_ref.gate_weight_ref.up_weight_ref), custom_call_target="tpu_custom_call" | custom-call | flops 6710886400 | bytes 10485760 | tf_op jit(solution)/shard_map/matmul_nt/pallas_call | solution.py:403
  467.8 7.1 fusion.18
  480.0 8.2 weight_grad.16
  499.6 7.1 weight_grad.14
  511.9 8.2 weight_grad.18
  540.3 12.2 %collective-permute-done.22 = bf16[128,1024]{1,0:T(8,128)(2,1)S(1)} collective-permute-done((bf16[128,1024]{1,0:T(8,128)(2,1)S(1)}, bf16[128,1024]{1,0:T(8,128)(2,1)S(1)}, u32[]{:S(2)}, u32[]{:S(2)}) %collective-permute-start.22) | collective-permute-done | bytes 262176 | tf_op jit(solution)/shard_map/ppermute | solution.py:566
  559.4 77.3 %collective-permute-done.14 = f32[33,128]{1,0:T(8,128)S(1)} collective-permute-done((f32[33,128]{1,0:T(8,128)S(1)}, f32[33,128]{1,0:T(8,128)S(1)}, u32[]{:S(2)}, u32[]{:S(2)}) %collective-permute-start.14) | collective-permute-done | bytes 16928 | tf_op jit(solution)/shard_map/ppermute | solution.py:569
  641.4 7.6 fusion.9
  668.3 7.6 weight_grad.19
  680.9 7.6 weight_grad.17
  690.0 30.0 %collective-permute-done.33.refs_7_ = bf16[4,128,2560]{2,1,0:T(8,128)(2,1)S(1)} collective-permute-done((bf16[4,128,2560]{2,1,0:T(8,128)(2,1)}, bf16[4,128,2560]{2,1,0:T(8,128)(2,1)S(1)}, u32[]{:S(2)}, u32[]{:S(2)}) %collective-permute-start.33) | collective-permute-done | bytes 2621472 | tf_op jit(solution)/shard_map/ppermute | solution.py:569
  721.4 7.6 weight_grad.15
  736.9 32.3 %collective-permute-done.47 = bf16[128,2560]{1,0:T(8,128)(2,1)} collective-permute-done((bf16[128,2560]{1,0:T(8,128)(2,1)}, bf16[128,2560]{1,0:T(8,128)(2,1)}, u32[]{:S(2)}, u32[]{:S(2)}) %collective-permute-start.47) | collective-permute-done | bytes 655392 | tf_op jit(solution)/shard_map/ppermute | solution.py:566
  774.9 42.1 %collective-permute-done.40 = bf16[128,2560]{1,0:T(8,128)(2,1)} collective-permute-done((bf16[128,2560]{1,0:T(8,128)(2,1)}, bf16[128,2560]{1,0:T(8,128)(2,1)}, u32[]{:S(2)}, u32[]{:S(2)}) %collective-permute-start.40) | collective-permute-done | bytes 655392 | tf_op jit(solution)/shard_map/ppermute | solution.py:566
  817.0 5.9 collective-permute-done.41
  825.9 5.1 collective-permute-done.34
  831.0 14.0 %collective-permute-done.35 = bf16[128,2560]{1,0:T(8,128)(2,1)} collective-permute-done((bf16[128,2560]{1,0:T(8,128)(2,1)}, bf16[128,2560]{1,0:T(8,128)(2,1)}, u32[]{:S(2)}, u32[]{:S(2)}) %collective-permute-start.35) | collective-permute-done | bytes 655392 | tf_op jit(solution)/shard_map/ppermute | solution.py:566
  845.1 5.8 collective-permute-done.36
  (331 shorter events, 228.7 us)
Async XLA Ops:
  7.2 72.5 %all-gather.3.cloned.1.call-start = ((), (), s32[]{:S(2)}) async-start(), calls=%async_computation | async-start | bytes 7241728 | tf_op jit(solution)/shard_map/all_gather | solution.py:586
  11.0 237.0 %all-gather.5.cloned.1.call-start = ((), (), s32[]{:S(2)}) async-start(), calls=%async_computation.1 | async-start | bytes 33423360 | tf_op jit(solution)/shard_map/all_gather | solution.py:592
  141.9 56.9 %collective-permute-start.4 = (bf16[640,2048]{0,1:T(8,128)(2,1)}, bf16[640,2048]{0,1:T(8,128)(2,1)}, u32[]{:S(2)}, u32[]{:S(2)}) collective-permute-start(bf16[640,2048]{0,1:T(8,128)(2,1)} %convolution_convert_fusion), channel_id=1, source_target_pairs={{0,1},{1,0},{2,3},{3,2},{4,5},{5,4},{6,7},{7,6},{8,9},{9,8},{10,11... | collective-permute-start | bytes 7864328 | tf_op jit(solution)/shard_map/ppermute | solution.py:575
  306.8 58.6 %collective-permute-start.6 = (bf16[640,2048]{0,1:T(8,128)(2,1)}, bf16[640,2048]{0,1:T(8,128)(2,1)}, u32[]{:S(2)}, u32[]{:S(2)}) collective-permute-start(bf16[640,2048]{0,1:T(8,128)(2,1)} %copy.89), channel_id=1, source_target_pairs={{0,1},{1,0},{2,3},{3,2},{4,5},{5,4},{6,7},{7,6},{8,9},{9,8},{10,11... | collective-permute-start | bytes 7864328 | tf_op jit(solution)/shard_map/ppermute | solution.py:575
  313.5 97.4 %collective-permute-start.18 = (bf16[640,1024]{0,1:T(8,128)(2,1)}, bf16[640,1024]{0,1:T(8,128)(2,1)}, u32[]{:S(2)}, u32[]{:S(2)}) collective-permute-start(bf16[640,1024]{0,1:T(8,128)(2,1)} %get-tuple-element.110), channel_id=1, source_target_pairs={{0,16},{16,0},{1,17},{17,1},{2,18},{18,2},{3,19},{19,3},{4,20},{20... | collective-permute-start | bytes 3932168 | tf_op jit(solution)/shard_map/ppermute | solution.py:572
  320.0 95.3 %collective-permute-start.31 = (bf16[640,1024]{0,1:T(8,128)(2,1)}, bf16[640,1024]{0,1:T(8,128)(2,1)}, u32[]{:S(2)}, u32[]{:S(2)}) collective-permute-start(bf16[640,1024]{0,1:T(8,128)(2,1)} %get-tuple-element.106), channel_id=1, source_target_pairs={{0,16},{16,0},{1,17},{17,1},{2,18},{18,2},{3,19},{19,3},{4,20},{20... | collective-permute-start | bytes 3932168 | tf_op jit(solution)/shard_map/ppermute | solution.py:572
  414.0 50.3 %collective-permute-start.26 = (bf16[640,640]{1,0:T(8,128)(2,1)}, bf16[640,640]{1,0:T(8,128)(2,1)}, u32[]{:S(2)}, u32[]{:S(2)}) collective-permute-start(bf16[640,640]{1,0:T(8,128)(2,1)} %get-tuple-element.28.attended_ref.refs_5_), channel_id=1, source_target_pairs={{0,16},{16,0},{1,17},{17,1},{2,18},{18,2},{3,19},{19,3},{4,20},{20... | collective-permute-start | bytes 2457608 | tf_op jit(solution)/shard_map/ppermute | solution.py:572
  415.3 64.6 %collective-permute-start.37 = (bf16[640,2560]{1,0:T(8,128)(2,1)}, bf16[640,2560]{1,0:T(8,128)(2,1)}, u32[]{:S(2)}, u32[]{:S(2)}) collective-permute-start(bf16[640,2560]{1,0:T(8,128)(2,1)} %get-tuple-element.33.up_ref.refs_5_), channel_id=1, source_target_pairs={{0,16},{16,0},{1,17},{17,1},{2,18},{18,2},{3,19},{19,3},{4,20},{20... | collective-permute-start | bytes 9830408 | tf_op jit(solution)/shard_map/ppermute | solution.py:572
  416.8 82.5 %collective-permute-start.32 = (bf16[640,2560]{1,0:T(8,128)(2,1)}, bf16[640,2560]{1,0:T(8,128)(2,1)}, u32[]{:S(2)}, u32[]{:S(2)}) collective-permute-start(bf16[640,2560]{1,0:T(8,128)(2,1)} %get-tuple-element.32.gate_ref.refs_5_), channel_id=1, source_target_pairs={{0,16},{16,0},{1,17},{17,1},{2,18},{18,2},{3,19},{19,3},{4,20},{20... | collective-permute-start | bytes 9830408 | tf_op jit(solution)/shard_map/ppermute | solution.py:572
  417.4 90.7 %collective-permute-start.43 = (bf16[640,2560]{1,0:T(8,128)(2,1)}, bf16[640,2560]{1,0:T(8,128)(2,1)}, u32[]{:S(2)}, u32[]{:S(2)}) collective-permute-start(bf16[640,2560]{1,0:T(8,128)(2,1)} %get-tuple-element.29.left_ref.refs_5_), channel_id=1, source_target_pairs={{0,16},{16,0},{1,17},{17,1},{2,18},{18,2},{3,19},{19,3},{4,20},{20... | collective-permute-start | bytes 9830408 | tf_op jit(solution)/shard_map/ppermute | solution.py:572
  466.7 21.5 %collective-permute-start.19 = (bf16[640,1024]{1,0:T(8,128)(2,1)S(1)}, bf16[640,1024]{1,0:T(8,128)(2,1)S(1)}, u32[]{:S(2)}, u32[]{:S(2)}) collective-permute-start(bf16[640,1024]{1,0:T(8,128)(2,1)S(1)} %constant_dynamic-update-slice_fusion.5.refs_5_), channel_id=1, source_target_pairs={{0,16},{16,0},{1,17},{17,1},{2,18},{18,2},{3,19},{19,3},{4,20},{20... | collective-permute-start | bytes 3932168 | tf_op jit(solution)/shard_map/ppermute | solution.py:572
  475.0 59.6 %collective-permute-start.11 = (bf16[640,2048]{0,1:T(8,128)(2,1)}, bf16[640,2048]{0,1:T(8,128)(2,1)}, u32[]{:S(2)}, u32[]{:S(2)}) collective-permute-start(bf16[640,2048]{0,1:T(8,128)(2,1)} %fusion.18), channel_id=1, source_target_pairs={{0,1},{1,0},{2,3},{3,2},{4,5},{5,4},{6,7},{7,6},{8,9},{9,8},{10,11... | collective-permute-start | bytes 7864328 | tf_op jit(solution)/shard_map/ppermute | solution.py:575
  488.2 151.7 %collective-permute-start.5 = (bf16[640,2048]{0,1:T(8,128)(2,1)}, bf16[640,2048]{0,1:T(8,128)(2,1)}, u32[]{:S(2)}, u32[]{:S(2)}) collective-permute-start(bf16[640,2048]{0,1:T(8,128)(2,1)} %copy.84), channel_id=1, source_target_pairs={{0,1},{1,0},{2,3},{3,2},{4,5},{5,4},{6,7},{7,6},{8,9},{9,8},{10,11... | collective-permute-start | bytes 7864328 | tf_op jit(solution)/shard_map/ppermute | solution.py:575
  496.1 28.5 %collective-permute-start.20 = (bf16[4,128,1024]{2,1,0:T(8,128)(2,1)}, bf16[4,128,1024]{2,1,0:T(8,128)(2,1)}, u32[]{:S(2)}, u32[]{:S(2)}) collective-permute-start(bf16[4,128,1024]{2,1,0:T(8,128)(2,1)} %weight_grad.10), channel_id=1, source_target_pairs={{0,2},{2,0},{4,6},{6,4},{8,10},{10,8},{12,14},{14,12},{1,3},{3,1},... | collective-permute-start | bytes 3145736 | tf_op jit(solution)/shard_map/ppermute | solution.py:569
  522.0 144.5 %collective-permute-start.44 = (bf16[4,128,2560]{2,1,0:T(8,128)(2,1)}, bf16[4,128,2560]{2,1,0:T(8,128)(2,1)}, u32[]{:S(2)}, u32[]{:S(2)}) collective-permute-start(bf16[4,128,2560]{2,1,0:T(8,128)(2,1)} %weight_grad.18), channel_id=1, source_target_pairs={{0,2},{2,0},{4,6},{6,4},{8,10},{10,8},{12,14},{14,12},{1,3},{3,1},... | collective-permute-start | bytes 7864328 | tf_op jit(solution)/shard_map/ppermute | solution.py:569
  534.6 23.7 %collective-permute-start.23 = (bf16[128,1024]{1,0:T(8,128)(2,1)S(1)}, bf16[128,1024]{1,0:T(8,128)(2,1)S(1)}, u32[]{:S(2)}, u32[]{:S(2)}) collective-permute-start(bf16[128,1024]{1,0:T(8,128)(2,1)S(1)} %get-tuple-element.114), channel_id=1, source_target_pairs={{0,12},{2,14},{4,0},{6,2},{8,4},{10,6},{12,8},{14,10},{1,13},{3,15... | collective-permute-start | bytes 786440 | tf_op jit(solution)/shard_map/ppermute | solution.py:566
  540.2 140.7 %collective-permute-start.38 = (bf16[4,128,2560]{2,1,0:T(8,128)(2,1)}, bf16[4,128,2560]{2,1,0:T(8,128)(2,1)}, u32[]{:S(2)}, u32[]{:S(2)}) collective-permute-start(bf16[4,128,2560]{2,1,0:T(8,128)(2,1)} %weight_grad.16), channel_id=1, source_target_pairs={{0,2},{2,0},{4,6},{6,4},{8,10},{10,8},{12,14},{14,12},{1,3},{3,1},... | collective-permute-start | bytes 7864328 | tf_op jit(solution)/shard_map/ppermute | solution.py:569
  559.3 77.4 %collective-permute-start.14 = (f32[33,128]{1,0:T(8,128)S(1)}, f32[33,128]{1,0:T(8,128)S(1)}, u32[]{:S(2)}, u32[]{:S(2)}) collective-permute-start(f32[33,128]{1,0:T(8,128)S(1)} %fusion.45), channel_id=1, source_target_pairs={{0,2},{2,0},{4,6},{6,4},{8,10},{10,8},{12,14},{14,12},{1,3},{3,1},... | collective-permute-start | bytes 50696 | tf_op jit(solution)/shard_map/ppermute | solution.py:569
  636.7 27.0 %collective-permute-start.15 = (f32[33,128]{1,0:T(8,128)S(1)}, f32[33,128]{1,0:T(8,128)S(1)}, u32[]{:S(2)}, u32[]{:S(2)}) collective-permute-start(f32[33,128]{1,0:T(8,128)S(1)} %fusion.56), channel_id=1, source_target_pairs={{0,4},{2,6},{4,8},{6,10},{8,12},{10,14},{12,0},{14,2},{1,5},{3,7},... | collective-permute-start | bytes 50696 | tf_op jit(solution)/shard_map/ppermute | solution.py:566
  636.8 28.4 %collective-permute-start.16 = (f32[33,128]{1,0:T(8,128)S(1)}, f32[33,128]{1,0:T(8,128)S(1)}, u32[]{:S(2)}, u32[]{:S(2)}) collective-permute-start(f32[33,128]{1,0:T(8,128)S(1)} %fusion.56), channel_id=1, source_target_pairs={{0,8},{2,10},{4,12},{6,14},{8,0},{10,2},{12,4},{14,6},{1,9},{3,11}... | collective-permute-start | bytes 50696 | tf_op jit(solution)/shard_map/ppermute | solution.py:566
  639.9 25.4 %collective-permute-start.17 = (f32[33,128]{1,0:T(8,128)S(1)}, f32[33,128]{1,0:T(8,128)S(1)}, u32[]{:S(2)}, u32[]{:S(2)}) collective-permute-start(f32[33,128]{1,0:T(8,128)S(1)} %fusion.56), channel_id=1, source_target_pairs={{0,12},{2,14},{4,0},{6,2},{8,4},{10,6},{12,8},{14,10},{1,13},{3,15... | collective-permute-start | bytes 50696 | tf_op jit(solution)/shard_map/ppermute | solution.py:566
  663.7 56.2 %collective-permute-start.33 = (bf16[4,128,2560]{2,1,0:T(8,128)(2,1)}, bf16[4,128,2560]{2,1,0:T(8,128)(2,1)S(1)}, u32[]{:S(2)}, u32[]{:S(2)}) collective-permute-start(bf16[4,128,2560]{2,1,0:T(8,128)(2,1)} %copy-done.14), channel_id=1, source_target_pairs={{0,2},{2,0},{4,6},{6,4},{8,10},{10,8},{12,14},{14,12},{1,3},{3,1},... | collective-permute-start | bytes 7864328 | tf_op jit(solution)/shard_map/ppermute | solution.py:569
  665.2 66.5 %collective-permute-start.24 = (f32[128,384]{1,0:T(8,128)S(1)}, f32[128,384]{1,0:T(8,128)S(1)}, u32[]{:S(2)}, u32[]{:S(2)}) collective-permute-start(f32[128,384]{1,0:T(8,128)S(1)} %slice.219), channel_id=1, source_target_pairs={{0,1},{1,0},{2,3},{3,2},{4,5},{5,4},{6,7},{7,6},{8,9},{9,8},{10,11... | collective-permute-start | bytes 589832 | tf_op jit(solution)/shard_map/ppermute | solution.py:575
  678.8 56.6 %collective-permute-start.45 = (bf16[128,2560]{1,0:T(8,128)(2,1)}, bf16[128,2560]{1,0:T(8,128)(2,1)S(1)}, u32[]{:S(2)}, u32[]{:S(2)}) collective-permute-start(bf16[128,2560]{1,0:T(8,128)(2,1)} %get-tuple-element.94), channel_id=1, source_target_pairs={{0,4},{2,6},{4,8},{6,10},{8,12},{10,14},{12,0},{14,2},{1,5},{3,7},... | collective-permute-start | bytes 1966088 | tf_op jit(solution)/shard_map/ppermute | solution.py:566
  678.9 57.1 %collective-permute-start.46 = (bf16[128,2560]{1,0:T(8,128)(2,1)}, bf16[128,2560]{1,0:T(8,128)(2,1)}, u32[]{:S(2)}, u32[]{:S(2)}) collective-permute-start(bf16[128,2560]{1,0:T(8,128)(2,1)} %get-tuple-element.96), channel_id=1, source_target_pairs={{0,8},{2,10},{4,12},{6,14},{8,0},{10,2},{12,4},{14,6},{1,9},{3,11}... | collective-permute-start | bytes 1966088 | tf_op jit(solution)/shard_map/ppermute | solution.py:566
  680.9 88.3 %collective-permute-start.47 = (bf16[128,2560]{1,0:T(8,128)(2,1)}, bf16[128,2560]{1,0:T(8,128)(2,1)}, u32[]{:S(2)}, u32[]{:S(2)}) collective-permute-start(bf16[128,2560]{1,0:T(8,128)(2,1)} %get-tuple-element.95), channel_id=1, source_target_pairs={{0,12},{2,14},{4,0},{6,2},{8,4},{10,6},{12,8},{14,10},{1,13},{3,15... | collective-permute-start | bytes 1966088 | tf_op jit(solution)/shard_map/ppermute | solution.py:566
  720.0 54.9 %collective-permute-start.39 = (bf16[128,2560]{1,0:T(8,128)(2,1)}, bf16[128,2560]{1,0:T(8,128)(2,1)}, u32[]{:S(2)}, u32[]{:S(2)}) collective-permute-start(bf16[128,2560]{1,0:T(8,128)(2,1)} %get-tuple-element.99), channel_id=1, source_target_pairs={{0,4},{2,6},{4,8},{6,10},{8,12},{10,14},{12,0},{14,2},{1,5},{3,7},... | collective-permute-start | bytes 1966088 | tf_op jit(solution)/shard_map/ppermute | solution.py:566
  731.8 85.2 %collective-permute-start.40 = (bf16[128,2560]{1,0:T(8,128)(2,1)}, bf16[128,2560]{1,0:T(8,128)(2,1)}, u32[]{:S(2)}, u32[]{:S(2)}) collective-permute-start(bf16[128,2560]{1,0:T(8,128)(2,1)} %get-tuple-element.101), channel_id=1, source_target_pairs={{0,8},{2,10},{4,12},{6,14},{8,0},{10,2},{12,4},{14,6},{1,9},{3,11}... | collective-permute-start | bytes 1966088 | tf_op jit(solution)/shard_map/ppermute | solution.py:566
  735.4 87.4 %collective-permute-start.41 = (bf16[128,2560]{1,0:T(8,128)(2,1)S(1)}, bf16[128,2560]{1,0:T(8,128)(2,1)}, u32[]{:S(2)}, u32[]{:S(2)}) collective-permute-start(bf16[128,2560]{1,0:T(8,128)(2,1)S(1)} %copy-done.49), channel_id=1, source_target_pairs={{0,12},{2,14},{4,0},{6,2},{8,4},{10,6},{12,8},{14,10},{1,13},{3,15... | collective-permute-start | bytes 1966088 | tf_op jit(solution)/shard_map/ppermute | solution.py:566
  736.0 95.0 %collective-permute-start.34 = (bf16[128,2560]{1,0:T(8,128)(2,1)}, bf16[128,2560]{1,0:T(8,128)(2,1)}, u32[]{:S(2)}, u32[]{:S(2)}) collective-permute-start(bf16[128,2560]{1,0:T(8,128)(2,1)} %get-tuple-element.102), channel_id=1, source_target_pairs={{0,4},{2,6},{4,8},{6,10},{8,12},{10,14},{12,0},{14,2},{1,5},{3,7},... | collective-permute-start | bytes 1966088 | tf_op jit(solution)/shard_map/ppermute | solution.py:566
  769.2 75.9 %collective-permute-start.35 = (bf16[128,2560]{1,0:T(8,128)(2,1)}, bf16[128,2560]{1,0:T(8,128)(2,1)}, u32[]{:S(2)}, u32[]{:S(2)}) collective-permute-start(bf16[128,2560]{1,0:T(8,128)(2,1)} %get-tuple-element.104), channel_id=1, source_target_pairs={{0,8},{2,10},{4,12},{6,14},{8,0},{10,2},{12,4},{14,6},{1,9},{3,11}... | collective-permute-start | bytes 1966088 | tf_op jit(solution)/shard_map/ppermute | solution.py:566
  774.9 76.0 %collective-permute-start.36 = (bf16[128,2560]{1,0:T(8,128)(2,1)S(1)}, bf16[128,2560]{1,0:T(8,128)(2,1)S(1)}, u32[]{:S(2)}, u32[]{:S(2)}) collective-permute-start(bf16[128,2560]{1,0:T(8,128)(2,1)S(1)} %get-tuple-element.103), channel_id=1, source_target_pairs={{0,12},{2,14},{4,0},{6,2},{8,4},{10,6},{12,8},{14,10},{1,13},{3,15... | collective-permute-start | bytes 1966088 | tf_op jit(solution)/shard_map/ppermute | solution.py:566
  (81 other events, 1515.4 us)
Sparse Core Ops, SparseCore 0:
  11.1 68.5 all-gather.2
  81.3 166.6 all-gather.4

commit v2 on v1

--- a/solution.py
+++ b/solution.py
@@ -19,7 +19,7 @@
 
 def cost(flops, bytes_accessed, transcendentals=0):
     return pl.CostEstimate(
-        flops=int(flops), bytes_accessed=int(bytes_accessed), transcendentals=int(transcendentals)
+        flops=int(flops) * 8, bytes_accessed=int(bytes_accessed) * 8, transcendentals=int(transcendentals) * 8
     )
 
 
@@ -362,10 +362,12 @@
     )(slots, rotated, keys, prompt_mask_t, attended, inverse, grad_attended)
 
 
-def ff_forward_kernel(rows_ref, gate_ref, up_ref, hidden_ref, gate_factor_ref, up_factor_ref):
-    rows = rows_ref[...]
-    gate = dot_nn(rows, gate_ref[...])
-    up = dot_nn(rows, up_ref[...])
+ff_tile = 256
+
+
+def ff_forward_kernel(rows_ref, weight_ref, hidden_ref, gate_factor_ref, up_factor_ref):
+    both = dot_nn(rows_ref[...], weight_ref[...])
+    gate, up = both[:, :ff_tile], both[:, ff_tile:]
     sigmoid = 1.0 / (1.0 + jnp.exp(-gate))
     silu = gate * sigmoid
     hidden_ref[...] = (silu * up).astype(bf16)
@@ -373,39 +375,37 @@
     up_factor_ref[...] = silu.astype(bf16)
 
 
-def ff_forward(rows, weights, units, tile=256):
+def ff_forward(rows, weights, units):
     count, depth = rows.shape
-    tiles = units // tile
-    out = pl.BlockSpec((count, tile), lambda j: (0, j))
+    out = pl.BlockSpec((count, ff_tile), lambda j: (0, j))
     return pl.pallas_call(
         ff_forward_kernel,
-        grid=(tiles,),
+        grid=(units // ff_tile,),
         in_specs=[
             pl.BlockSpec((count, depth), lambda j: (0, 0)),
-            pl.BlockSpec((depth, tile), lambda j: (0, j)),
-            pl.BlockSpec((depth, tile), lambda j: (0, j + tiles)),
+            pl.BlockSpec((depth, 2 * ff_tile), lambda j: (0, j)),
         ],
         out_specs=[out, out, out],
         out_shape=[jax.ShapeDtypeStruct((count, units), bf16)] * 3,
         compiler_params=params(),
         cost_estimate=cost(4 * count * depth * units, 4 * depth * units, count * units),
         name="ff_forward",
-    )(rows, weights, weights)
+    )(rows, weights)
 
 
 def matmul_nt_kernel(left_ref, right_ref, out_ref):
     out_ref[...] = dot_nt(left_ref[...], right_ref[...]).astype(bf16)
 
 
-def matmul_nt(left, weights, column_block, tile=256):
+def matmul_nt(left, weights, column_block, first=0, wide=None, tile=256):
     count, depth = left.shape
-    wide = weights.shape[0]
+    wide = wide or weights.shape[0]
     return pl.pallas_call(
         matmul_nt_kernel,
         grid=(wide // tile,),
         in_specs=[
             pl.BlockSpec((count, depth), lambda j: (0, 0)),
-            pl.BlockSpec((tile, depth), lambda j: (j, column_block)),
+            pl.BlockSpec((tile, depth), lambda j: (j + first // tile, column_block)),
         ],
         out_specs=pl.BlockSpec((count, tile), lambda j: (0, j)),
         out_shape=jax.ShapeDtypeStruct((count, wide), bf16),
@@ -415,103 +415,178 @@
     )(left, weights)
 
 
-def ff_back_kernel(grad_ref, weight_ref, gate_factor_ref, up_factor_ref, gate_ref, up_ref):
+def split_tiles_kernel(both_ref, gate_ref, up_ref):
+    gate_ref[...] = both_ref[:, :ff_tile].astype(f32)
+    up_ref[...] = both_ref[:, ff_tile:].astype(f32)
+
+
+def split_tiles(both):
+    rows, wide = both.shape
+    out = pl.BlockSpec((rows, ff_tile), lambda j: (0, j))
+    return pl.pallas_call(
+        split_tiles_kernel,
+        grid=(wide // (2 * ff_tile),),
+        in_specs=[pl.BlockSpec((rows, 2 * ff_tile), lambda j: (0, j))],
+        out_specs=[out, out],
+        out_shape=[jax.ShapeDtypeStruct((rows, wide // 2), f32)] * 2,
+        compiler_params=params(),
+        cost_estimate=cost(0, rows * wide * 6),
+        name="split_tiles",
+    )(both)
+
+
+def norm_back_kernel(*refs, halves, extra):
+    addends, refs = refs[: 2 * halves], refs[2 * halves :]
+    grad = jnp.concatenate(
+        [addends[2 * half][...].astype(f32) + addends[2 * half + 1][...].astype(f32) for half in range(halves)],
+        axis=1,
+    )
+    if extra:
+        grad, refs = grad + refs[0][...].astype(f32), refs[1:]
+    base_ref, values_ref, scale_ref, gain_ref, out_ref, gain_grad_ref = refs
+    scale = scale_ref[...]
+    normed = values_ref[...].astype(f32) * scale
+    weighted = grad * gain_ref[...]
+    mean = jnp.mean(weighted * normed, axis=-1, keepdims=True)
+
+    @pl.when(pl.program_id(0) == 0)
+    def _():
+        gain_grad_ref[...] = jnp.zeros_like(gain_grad_ref)
+
+    gain_grad_ref[...] += jnp.sum(grad * normed, axis=0, keepdims=True)
+    out_ref[...] = (base_ref[...].astype(f32) + scale * (weighted - normed * mean)).astype(bf16)
+
+
+def norm_backward(addends, extra, base, values, scale, gain, tile=128):
+    rows, width = base.shape
+    row_spec = pl.BlockSpec((tile, width), lambda i: (i, 0))
+    one_spec = pl.BlockSpec((1, width), lambda i: (0, 0))
+    half_spec = pl.BlockSpec((tile, addends[0].shape[1]), lambda i: (i, 0))
+    operands = list(addends) + ([extra] if extra is not None else []) + [base, values, scale, gain[None]]
+    in_specs = [half_spec] * len(addends) + [row_spec] * (3 if extra is not None else 2)
+    in_specs += [pl.BlockSpec((tile, 1), lambda i: (i, 0)), one_spec]
+    return pl.pallas_call(
+        partial(norm_back_kernel, halves=len(addends) // 2, extra=extra is not None),
+        grid=(rows // tile,),
+        in_specs=in_specs,
+        out_specs=[row_spec, one_spec],
+        out_shape=[jax.ShapeDtypeStruct((rows, width), bf16), jax.ShapeDtypeStruct((1, width), f32)],
+        compiler_params=params(),
+        cost_estimate=cost(rows * width * 20, rows * width * 12),
+        name="norm_backward",
+    )(*operands)
+
+
+def ff_back_kernel(grad_ref, weight_ref, gate_factor_ref, up_factor_ref, out_ref):
     grad_hidden = dot_nn(grad_ref[...], weight_ref[...])
-    gate_ref[...] = (grad_hidden * gate_factor_ref[...].astype(f32)).astype(bf16)
-    up_ref[...] = (grad_hidden * up_factor_ref[...].astype(f32)).astype(bf16)
-
-
-def ff_backward(grad_out, weights, gate_factor, up_factor, tile=256):
+    out_ref[:, :ff_tile] = (grad_hidden * gate_factor_ref[...].astype(f32)).astype(bf16)
+    out_ref[:, ff_tile:] = (grad_hidden * up_factor_ref[...].astype(f32)).astype(bf16)
+
+
+def ff_backward(grad_out, weights, gate_factor, up_factor):
     count, depth = grad_out.shape
     units = gate_factor.shape[1]
-    tiles = units // tile
-    out = pl.BlockSpec((count, tile), lambda j: (0, j))
+    tiles = units // ff_tile
+    factor = pl.BlockSpec((count, ff_tile), lambda j: (0, j))
     return pl.pallas_call(
         ff_back_kernel,
         grid=(tiles,),
         in_specs=[
             pl.BlockSpec((count, depth), lambda j: (0, 0)),
-            pl.BlockSpec((depth, tile), lambda j: (0, j + 2 * tiles)),
-            out,
-            out,
+            pl.BlockSpec((depth, ff_tile), lambda j: (0, j + 2 * tiles)),
+            factor,
+            factor,
         ],
-        out_specs=[out, out],
-        out_shape=[jax.ShapeDtypeStruct((count, units), bf16)] * 2,
+        out_specs=pl.BlockSpec((count, 2 * ff_tile), lambda j: (0, j)),
+        out_shape=jax.ShapeDtypeStruct((count, 2 * units), bf16),
         compiler_params=params(),
         cost_estimate=cost(2 * count * depth * units, 2 * depth * units),
         name="ff_backward",
     )(grad_out, weights, gate_factor, up_factor)
 
 
-def ff_input_kernel(gate_ref, up_ref, gate_weight_ref, up_weight_ref, out_ref):
-    out_ref[...] = (
-        dot_nt(gate_ref[...], gate_weight_ref[...]) + dot_nt(up_ref[...], up_weight_ref[...])
-    ).astype(bf16)
-
-
-def ff_input_grad(grad_gate, grad_up, weights, tile=256):
-    count, units = grad_gate.shape
-    wide = weights.shape[0]
-    full = pl.BlockSpec((count, units), lambda j: (0, 0))
-    return pl.pallas_call(
-        ff_input_kernel,
-        grid=(wide // tile,),
-        in_specs=[
-            full,
-            full,
-            pl.BlockSpec((tile, units), lambda j: (j, 0)),
-            pl.BlockSpec((tile, units), lambda j: (j, 1)),
-        ],
-        out_specs=pl.BlockSpec((count, tile), lambda j: (0, j)),
-        out_shape=jax.ShapeDtypeStruct((count, wide), bf16),
-        compiler_params=params(),
-        cost_estimate=cost(4 * count * units * wide, 4 * units * wide),
-        name="ff_input_grad",
-    )(grad_gate, grad_up, weights, weights)
-
-
-def weight_grad_kernel(*refs, pieces, add):
-    index_ref = refs[0]
-    left = jnp.concatenate([ref[...] for ref in refs[1 : 1 + pieces]], axis=0)
-    own_ref, other_ref = refs[1 + pieces : 3 + pieces]
-    out_ref = refs[-1]
+def weight_grad_kernel(index_ref, left_own_ref, left_other_ref, own_ref, other_ref, *rest, pieces, block):
+    out_ref, left_t = rest[-2:]
+    rows = own_ref.shape[0]
+
+    @pl.when(pl.program_id(0) == 0)
+    def _():
+        left_t[:, :rows] = left_own_ref[...].T
+        left_t[:, rows:] = left_other_ref[...].T
+
+    left = jnp.concatenate(
+        [left_t[pl.ds(pl.multiple_of(index_ref[piece] * block, block), block)] for piece in range(pieces)],
+        axis=0,
+    )
     right = jnp.concatenate([own_ref[...], other_ref[...]], axis=0)
     product = dot_nn(left, right)
-    rows = left.shape[0] // pieces
     for piece in range(pieces):
-        part = product[piece * rows : (piece + 1) * rows]
-        if add:
-            part = part + refs[-2][piece].astype(f32)
+        part = product[piece * block : (piece + 1) * block]
+        if len(rest) == 3:
+            part = part + rest[0][piece].astype(f32)
         out_ref[piece] = part.astype(bf16)
 
 
-def weight_grad(indices, block, left_t, own, other, received=None):
+def weight_grad(indices, rank, block, left, left_other, own, other, received=None):
     pieces = indices.shape[0]
-    depth = left_t.shape[1]
-    count, wide = own.shape
-    tile = 512 if wide % 512 == 0 else 640 if wide % 640 == 0 else lanes
+    rows, wide = own.shape
+    half = left.shape[1] // 2
+    tile = next(size for size in (640, 512, 384, lanes) if wide % size == 0)
     out = pl.BlockSpec((pieces, block, tile), lambda j, s: (0, 0, j))
-    in_specs = [
-        pl.BlockSpec((block, depth), lambda j, s, piece=piece: (s[piece], 0)) for piece in range(pieces)
-    ]
-    in_specs += [pl.BlockSpec((count, tile), lambda j, s: (0, j))] * 2
-    operands = [left_t] * pieces + [own, other]
+    left_spec = pl.BlockSpec((rows, half), lambda j, s: (0, s[pieces]))
+    in_specs = [left_spec] * 2 + [pl.BlockSpec((rows, tile), lambda j, s: (0, j))] * 2
+    operands = [left, left_other, own, other]
     if received is not None:
         in_specs.append(out)
         operands.append(received)
     return pl.pallas_call(
-        partial(weight_grad_kernel, pieces=pieces, add=received is not None),
+        partial(weight_grad_kernel, pieces=pieces, block=block),
         grid_spec=pltpu.PrefetchScalarGridSpec(
             num_scalar_prefetch=1,
             grid=(wide // tile,),
             in_specs=in_specs,
             out_specs=out,
+            scratch_shapes=[pltpu.VMEM((half, 2 * rows), bf16)],
         ),
         out_shape=jax.ShapeDtypeStruct((pieces, block, wide), bf16),
         compiler_params=params(),
-        cost_estimate=cost(2 * pieces * block * depth * wide, 2 * (pieces * block + depth) * wide),
+        cost_estimate=cost(4 * pieces * block * rows * wide, 2 * (pieces * block + 2 * rows) * wide),
         name="weight_grad",
-    )(indices, *operands)
+    )(jnp.concatenate([indices, rank[None]]), *operands)
+
+
+def gather_blocks_kernel(place_ref, *refs):
+    count = (len(refs) - 2) // 1
+    out_ref, sems = refs[-2:]
+    copies = [
+        pltpu.make_async_copy(refs[i], out_ref.at[place_ref[i]], sems.at[i]) for i in range(count)
+    ]
+    for copy in copies:
+        copy.start()
+    for copy in copies:
+        copy.wait()
+
+
+def gather_blocks(places, blocks):
+    count = len(blocks)
+    any_spec = pl.BlockSpec(memory_space=pl.ANY)
+    return pl.pallas_call(
+        gather_blocks_kernel,
+        grid_spec=pltpu.PrefetchScalarGridSpec(
+            num_scalar_prefetch=1,
+            grid=(1,),
+            in_specs=[any_spec] * count,
+            out_specs=any_spec,
+            scratch_shapes=[pltpu.SemaphoreType.DMA((count,))],
+        ),
+        out_shape=jax.ShapeDtypeStruct((count,) + blocks[0].shape, blocks[0].dtype),
+        cost_estimate=cost(0, 2 * count * blocks[0].size * 2),
+        name="gather_blocks",
+    )(places, *blocks)
+
+
+def after(values):
+    return lax.optimization_barrier(values)
 
 
 def on_device(
@@ -579,6 +654,11 @@
             -1, slot_count, head_size
         )
 
+    def interleaved(gate, up):
+        tiles = units // ff_tile
+        both = jnp.stack([gate.reshape(-1, tiles, ff_tile), up.reshape(-1, tiles, ff_tile)], axis=2)
+        return both.reshape(-1, 2 * units)
+
     key_value_weight = jnp.concatenate(
         [shared_slots(key_weight), shared_slots(value_weight)], axis=2
     ).reshape(-1, slot_count * lanes)
@@ -590,12 +670,13 @@
         tiled=True,
     )
     ff_weights = lax.all_gather(
-        jnp.concatenate([gate_weight, up_weight, down_weight.T], axis=1),
+        jnp.concatenate([interleaved(gate_weight, up_weight), down_weight.T], axis=1),
         ("dp", "ctx"),
         axis=0,
         tiled=True,
     )
     qkv_weights = attn_weights[:, :qkv_width]
+    shared_weights = attn_weights[:, query_width:qkv_width]
     out_weights_t = attn_weights[:, qkv_width:]
 
     row_ids = jnp.arange(rows_here, dtype=jnp.int32)
@@ -634,7 +715,8 @@
         (tensor_rank * local_heads + 2 * jnp.arange(pairs, dtype=jnp.int32)) // group_size - first_shared
     ).astype(jnp.int32)
 
-    inputs = jnp.concatenate([prompt_states, continuation_states], axis=0).astype(f32)
+    inputs_low = jnp.concatenate([prompt_states, continuation_states], axis=0)
+    inputs = inputs_low.astype(f32)
     attn_gain32 = attention_gain.astype(f32)
     ff_gain32 = feedforward_gain.astype(f32)
     first_scale = lax.rsqrt(jnp.mean(inputs * inputs, axis=-1, keepdims=True) + epsilon)
@@ -649,53 +731,55 @@
     attended, inverse = attention_forward(
         slots, rotated, keys, prompt_mask, pairs, prompt_here, head_size
     )
+    shared_weights = jnp.concatenate([shared_weights, tp_swap(shared_weights)], axis=1)
+    attended, shared_weights = after((attended, shared_weights))
     attn_part = dot_nt(attended, out_weights_t).astype(bf16)
-    resid = inputs + (attn_part.astype(f32) + tp_swap(attn_part).astype(f32))
-    second_scale = lax.rsqrt(jnp.mean(resid * resid, axis=-1, keepdims=True) + epsilon)
-    second_normed = resid * second_scale
-    normed_two = (second_normed * ff_gain32).astype(bf16)
+    resid32 = inputs + (attn_part.astype(f32) + tp_swap(attn_part).astype(f32))
+    resid = resid32.astype(bf16)
+    second_scale = lax.rsqrt(jnp.mean(resid32 * resid32, axis=-1, keepdims=True) + epsilon)
+    normed_two = (resid32 * second_scale * ff_gain32).astype(bf16)
     hidden, gate_factor, up_factor = ff_forward(normed_two, ff_weights, units)
-    ff_part = matmul_nt(hidden, ff_weights, 2)
-    output = (resid + (ff_part.astype(f32) + tp_swap(ff_part).astype(f32))).astype(bf16)
-
-    def columns_of(values, rank):
-        return lax.dynamic_slice_in_dim(values, rank * half_width, half_width, 1)
-
-    def both_rows_t(values):
-        received = dp_swap(columns_of(values, 1 - data_rank))
-        return jnp.concatenate([columns_of(values, data_rank), received], axis=0).T
-
-    def reduced(left_t, own):
-        other = dp_swap(own)
-        sent = y_swap(weight_grad(other_blocks, block, left_t, own, other))
-        kept = weight_grad(own_blocks, block, left_t, own, other, sent)
+
+    def send_part(left, left_other, own, other):
+        return weight_grad(other_blocks, data_rank, block, left, left_other, own, other)
+
+    def keep_part(left, left_other, own, other, received):
+        return weight_grad(own_blocks, data_rank, block, left, left_other, own, other, received)
+
+    every_block = jnp.arange(ring, dtype=jnp.int32)
+
+    def finish(kept):
         total = kept[0].astype(f32)
         for step in range(1, zsize):
             total = total + z_pass(kept[step], step).astype(f32)
         return total
 
     grad_out = jnp.concatenate([grad_prompt, grad_continuation], axis=0)
-    grad_out_t = both_rows_t(grad_out)
-    down_done = reduced(grad_out_t, hidden).T
-
-    grad_gate, grad_up = ff_backward(grad_out, ff_weights, gate_factor, up_factor)
-    normed_two_t = both_rows_t(normed_two)
-    gate_done = reduced(normed_two_t, grad_gate)
-    up_done = reduced(normed_two_t, grad_up)
-    grad_part = ff_input_grad(grad_gate, grad_up, ff_weights)
-    grad_normed_two = grad_part.astype(f32) + tp_swap(grad_part).astype(f32)
-
-    def norm_back(grad_rows, normed_rows, scale, gain):
-        weighted = grad_rows * gain
-        mean = jnp.mean(weighted * normed_rows, axis=-1, keepdims=True)
-        return scale * (weighted - normed_rows * mean), jnp.sum(grad_rows * normed_rows, axis=0)
-
-    grad_resid_part, grad_ff_gain = norm_back(grad_normed_two, second_normed, second_scale, ff_gain32)
-    grad_resid = grad_out.astype(f32) + grad_resid_part
-    grad_resid_low = grad_resid.astype(bf16)
+    out_pair = (grad_out, dp_swap(grad_out))
+    two_pair = (normed_two, dp_swap(normed_two))
+    one_pair = (normed_low, dp_swap(normed_low))
+    hidden_other = dp_swap(hidden)
+
+    grad_ff = ff_backward(grad_out, ff_weights, gate_factor, up_factor)
+    grad_ff_other = dp_swap(grad_ff)
+    down_grad = weight_grad(every_block, data_rank, block, *out_pair, hidden, hidden_other)
+    grad_ff, down_grad = after((grad_ff, down_grad))
+    down_done = lax.psum_scatter(down_grad, "ctx", scatter_dimension=0, tiled=True)[0]
+    grad_parts = [matmul_nt(grad_ff, ff_weights, 0, 0, half_width)]
+    grad_parts.append(matmul_nt(after((grad_ff, grad_parts[0]))[0], ff_weights, 0, half_width, half_width))
+    grad_ff, hidden_next, second_part = after((grad_ff, hidden, grad_parts[1]))
+    ff_grad = weight_grad(every_block, data_rank, block, *two_pair, grad_ff, grad_ff_other)
+    ff_done = lax.psum_scatter(ff_grad, "ctx", scatter_dimension=0, tiled=True)[0]
+    first_other, ff_grad, hidden_next = after((tp_swap(grad_parts[0]), ff_grad, hidden_next))
+    ff_part = matmul_nt(hidden_next, ff_weights, 2)
+    ff_part_other = tp_swap(ff_part)
+    ff_part, second_other = after((ff_part, tp_swap(second_part)))
+    grad_resid_low, grad_ff_gain = norm_backward(
+        [grad_parts[0], first_other, second_part, second_other], None, grad_out, resid, second_scale, ff_gain32
+    )
+    resid_pair = (grad_resid_low, dp_swap(grad_resid_low))
+    attended_other = dp_swap(attended)
     grad_attended = dot_nn(grad_resid_low, out_weights_t).astype(bf16)
-    out_done = reduced(both_rows_t(grad_resid_low), attended).T
-
     grad_query, grad_keys = attention_backward(
         slots,
         rotated,
@@ -711,26 +795,55 @@
     )
     grad_keys_prompt = grad_keys[:prompt_length].astype(bf16)
     half_prompt = prompt_length // 2
-    kept_keys = grad_keys_prompt[:half_prompt].astype(f32) + y_swap(grad_keys_prompt[half_prompt:]).astype(f32)
-    kept_keys = kept_keys.astype(bf16)
+    grad_query_low, query_gain_parts = head_prep_back(
+        raw, 0, grad_query, cos_table, sin_table, gains, False, head_size
+    )
+    query_parts = [
+        dot_nt(grad_query_low, qkv_weights[half * half_width : (half + 1) * half_width, :query_width]).astype(bf16)
+        for half in range(2)
+    ]
+    received_keys = y_swap(grad_keys_prompt[half_prompt:])
+    received_keys, query_parts[0], query_parts[1] = after((received_keys, query_parts[0], query_parts[1]))
+    query_others = [tp_swap(part) for part in query_parts]
+    kept_keys = (grad_keys_prompt[:half_prompt].astype(f32) + received_keys.astype(f32)).astype(bf16)
     own_keys = kept_keys[:prompt_here].astype(f32)
     for step in range(1, zsize):
         own_keys = own_keys + z_pass(
             kept_keys[step * prompt_here : (step + 1) * prompt_here], step
         ).astype(f32)
+    ff_part, ff_part_other, resid_out, kept_keys = after((ff_part, ff_part_other, resid, kept_keys))
+    own_keys, query_others[0] = after((own_keys, query_others[0]))
+    output = (resid_out.astype(f32) + (ff_part.astype(f32) + ff_part_other.astype(f32))).astype(bf16)
     grad_key_value = jnp.concatenate([own_keys, grad_keys[prompt_length:]], axis=0)
-    grad_query_low, query_gain_parts = head_prep_back(
-        raw, 0, grad_query, cos_table, sin_table, gains, False, head_size
-    )
+    out_sent = send_part(*resid_pair, attended, attended_other)
+    grad_key_value, out_sent, output = after((grad_key_value, out_sent, output))
     grad_shared_low, key_gain_parts = head_prep_back(
         raw, pairs, grad_key_value, cos_table, sin_table, gains, True, head_size
     )
+    grad_shared_other = tp_swap(grad_shared_low)
     grad_qkv = jnp.concatenate([grad_query_low, grad_shared_low], axis=1)
-    qkv_done = reduced(both_rows_t(normed_low), grad_qkv)
-    qkv_part = dot_nt(grad_qkv, qkv_weights).astype(bf16)
-    grad_normed = qkv_part.astype(f32) + tp_swap(qkv_part).astype(f32)
-    grad_input_part, grad_attn_gain = norm_back(grad_normed, inputs * first_scale, first_scale, attn_gain32)
-    grad_input = (grad_resid + grad_input_part).astype(bf16)
+    grad_qkv_other = dp_swap(grad_qkv)
+    qkv_sent = send_part(*one_pair, grad_qkv, grad_qkv_other)
+    out_kept = keep_part(*resid_pair, attended, attended_other, y_swap(out_sent))
+    qkv_kept = keep_part(*one_pair, grad_qkv, grad_qkv_other, y_swap(qkv_sent))
+    grad_shared_other, query_others[1], out_kept, qkv_kept = after(
+        (grad_shared_other, query_others[1], out_kept, qkv_kept)
+    )
+    shared_part = dot_nt(
+        jnp.concatenate([grad_shared_low, grad_shared_other], axis=1), shared_weights
+    ).astype(bf16)
+    grad_input, grad_attn_gain = norm_backward(
+        [query_parts[0], query_others[0], query_parts[1], query_others[1]],
+        shared_part,
+        grad_resid_low,
+        inputs_low,
+        first_scale,
+        attn_gain32,
+    )
+    down_done = down_done.astype(f32).T
+    gate_done, up_done = split_tiles(ff_done)
+    out_done = finish(out_kept).T
+    qkv_done = finish(qkv_kept)
 
     shared_done = qkv_done[:, query_width:]
     shared_other = tp_swap(shared_done)
@@ -750,15 +863,15 @@
 
     query_gain_sum = jnp.sum(query_gain_parts.reshape(-1, head_size), axis=0)
     key_gain_sum = jnp.sum(key_gain_parts[:, 0, :head_size], axis=0)
-    head_gains = jnp.concatenate([query_gain_sum, key_gain_sum])
-    head_gains = head_gains + tp_swap(head_gains)
-    gain_sums = jnp.concatenate([grad_attn_gain, grad_ff_gain, head_gains]).reshape(-1, lanes)
+    gain_sums = jnp.concatenate([grad_attn_gain[0], grad_ff_gain[0], query_gain_sum, key_gain_sum]).reshape(-1, lanes)
     gain_sums = gain_sums + dp_swap(gain_sums)
     gain_sums = gain_sums + y_swap(gain_sums)
     gain_total = gain_sums
     for step in range(1, zsize):
         gain_total = gain_total + z_pass(gain_sums, step)
     gain_total = gain_total.reshape(-1)
+    head_gains = gain_total[2 * width :]
+    head_gains = head_gains + tp_swap(head_gains)
     return (
         output[:prompt_here],
         output[prompt_here:],
@@ -768,8 +881,8 @@
         qkv_done[:, :query_width],
         key_done,
         value_done,
-        gain_total[2 * width : 2 * width + head_size],
-        gain_total[2 * width + head_size :],
+        head_gains[:head_size],
+        head_gains[head_size:],
         out_done,
         gain_total[width : 2 * width],
         gate_done,

time: 869 us -> 676 us (0.78)
  waiting for transfers between devices: 445 us -> 290 us
  local copies, waits for them, and re-layouts: 80.9 us -> 41.2 us
  other arithmetic: 58.8 us -> 34.6 us
  Pallas kernels: 187 us -> 207 us
    ppermute x8 -> x5, waiting for transfers between devices: 121 us -> 45.4 us  [y_swap(): return lax.ppermute(values, 'ctx', [(i, i ^ 1) for i in range(ring)])]
    ppermute x24 -> x15, waiting for transfers between devices: 139 us -> 95.7 us  [z_pass(): return lax.ppermute(values, 'ctx', pairs_of)]
    pallas_call x1 -> x3, Pallas kernels: 11.8 us -> 35.9 us  [matmul_nt(): pl.pallas_call(matmul_nt_kernel, grid=(wide // tile,), in_specs=[pl.Block...]
    ppermute x6 -> x10, waiting for transfers between devices: 91.7 us -> 68.2 us  [tp_swap(): return lax.ppermute(values, 'tp', [(0, 1), (1, 0)])]
    unnamed x143 -> x129, local copies, waits for them, and re-layouts: 43.1 us -> 21.1 us
    all_gather x1, waiting for transfers between devices: 35.8 us -> 25.1 us  [on_device(): lax.all_gather(jnp.concatenate([interleaved(gate_weight, up_weight), down...]
    dynamic_slice x3 -> x0, local copies, waits for them, and re-layouts: 8.75 us -> none  [columns_of(): return lax.dynamic_slice_in_dim(values, rank * half_width, half_width, 1)]
    pallas_call x12 -> x10, Pallas kernels: 101 us -> 96.4 us  [the longest x6 56.3 us: weight_grad(): pl.pallas_call(partial(weight_grad_kernel, pieces=pieces, block=block), g...]
  transfers between devices with their start and end apart: 50 -> 43, of which waited for: 25 -> 21; matrix products, arithmetic and copies ran while one was open for 16% -> 13% of each run, Pallas kernels for 15% -> 30%
where the time goes in v2:
time: 676 us; the launch traced here: 666 us
  waiting for transfers between devices  290 us (43%)
  Pallas kernels  207 us (31%)
  starting transfers between devices  52.6 us (8%)
  local copies, waits for them, and re-layouts  41.2 us (6%)
  other arithmetic  34.6 us (5%)
  matrix products  25.2 us (4%)
  between operations  15.7 us (2%)
    ppermute x15, waiting for transfers between devices, z_pass(): return lax.ppermute(values, 'ctx', pairs_of)  95.7 us
    ppermute x10, waiting for transfers between devices, tp_swap(): return lax.ppermute(values, 'tp', [(0, 1), (1, 0)])  68.2 us
    pallas_call x6, Pallas kernels, weight_grad(): pl.pallas_call(partial(weight_grad_kernel, pieces=pieces, block=block), g...  56.3 us
    all_gather x1, waiting for transfers between devices, on_device(): lax.all_gather(jnp.concatenate([query_weight, key_value_weight, output_we...  53.5 us
    ppermute x5, waiting for transfers between devices, y_swap(): return lax.ppermute(values, 'ctx', [(i, i ^ 1) for i in range(ring)])  45.4 us
    pallas_call x3, Pallas kernels, matmul_nt(): pl.pallas_call(matmul_nt_kernel, grid=(wide // tile,), in_specs=[pl.Block...  35.9 us
    pallas_call x1, Pallas kernels, attention_backward(): pl.pallas_call(partial(attn_back_kernel, prompt_here=prompt_here, chunk=c...  30.9 us
    ppermute x15, starting transfers between devices, z_pass(): return lax.ppermute(values, 'ctx', pairs_of)  25.7 us
  transfers between devices with their start and end apart: 43, of which 21 were waited for; matrix products, arithmetic and copies ran while one was open for 13% of the time, Pallas kernels for 30%

profile of v2, /device:TPU:9, one launch (start us, length us, event | category | flops | bytes accessed | tf_op | source)
XLA Modules:
  0.0 666.3 jit_solution(5515307352101171804)
XLA Ops:
  26.2 53.5 %all-gather.3.cloned.1.call-done = bf16[2048,1664]{0,1:T(8,128)(2,1)} async-done(((bf16[128,1664]{0,1:T(8,128)(2,1)}), bf16[2048,1664]{0,1:T(8,128)(2,1)}) %all-gather.3.cloned.1.call-update) | async-done | bytes 6815760 | tf_op jit(solution)/shard_map/all_gather | solution.py:666
  79.6 5.5 fusion.3.raw_ref
  96.9 5.2 collective-permute-done.1
  109.7 6.5 collective-permute-done.3
  116.4 18.2 %attention_forward.1 = (bf16[640,640]{1,0:T(8,128)(2,1)S(1)}, f32[640,640]{1,0:T(8,128)S(1)}) custom-call(s32[5]{0:T(128)S(1)} %fusion.25.slot_ref, bf16[640,1024]{1,0:T(8,128)(2,1)S(1)} %head_prep.1.query_ref, bf16[1536,384]{1,0:T(8,128)(2,1)S(1)} %slice_dynamic-update-slice_fusion.keys_ref, f32[128,1024]{1,0:T(8,128)S(1)} %compare_convert_fusion.mask_ref), custom_call_target="tpu_custom_call" | custom-call | flops 78643200000 | bytes 78643200 | tf_op jit(solution)/shard_map/attention_forward/pallas_call | solution.py:197
  134.6 8.8 %collective-permute-done.4 = bf16[2048,384]{0,1:T(8,128)(2,1)S(1)} collective-permute-done((bf16[2048,384]{0,1:T(8,128)(2,1)S(1)}, bf16[2048,384]{0,1:T(8,128)(2,1)S(1)}, u32[]{:S(2)}, u32[]{:S(2)}) %collective-permute-start.4) | collective-permute-done | bytes 1572896 | tf_op jit(solution)/shard_map/ppermute | solution.py:650
  145.5 5.7 convolution_convert_fusion.1
  158.0 49.9 %collective-permute-done.5 = bf16[640,2048]{1,0:T(8,128)(2,1)} collective-permute-done((bf16[640,2048]{1,0:T(8,128)(2,1)}, bf16[640,2048]{1,0:T(8,128)(2,1)}, u32[]{:S(2)}, u32[]{:S(2)}) %collective-permute-start.5) | collective-permute-done | bytes 2621472 | tf_op jit(solution)/shard_map/ppermute | solution.py:650
  211.8 8.2 %fusion.11 = (bf16[640,2048]{1,0:T(8,128)(2,1)}, bf16[640,2048]{1,0:T(8,128)(2,1)}) fusion(bf16[640,2048]{1,0:T(8,128)(2,1)} %collective-permute-done.5, bf16[640,2048]{1,0:T(8,128)(2,1)} %convolution_convert_fusion.1, bf16[640,2048]{1,0:T(8,128)(2,1)} %copy-done.38, f32[2048]{0:T(1024)S(1)} %convert_element_type.137, f32[640]{0:T(1024)S(1)} %add_rsqrt_fusion), kind=kLoop, calls=%fused_computation.21 | loop fusion | flops 11796480 | bytes 13117952 | tf_op jit(solution)/shard_map/convert_element_type | solution.py:738
  223.4 25.1 %all-gather.5.cloned.1.call-done.weight_ref.right_ref = bf16[2048,7680]{1,0:T(8,128)(2,1)} async-done(((bf16[128,7680]{1,0:T(8,128)(2,1)}), bf16[2048,7680]{1,0:T(8,128)(2,1)}) %all-gather.5.cloned.1.call-update) | async-done | bytes 31457296 | tf_op jit(solution)/shard_map/all_gather | solution.py:672
  248.5 21.0 %ff_forward.1 = (bf16[640,2560]{1,0:T(8,128)(2,1)S(1)}, bf16[640,2560]{1,0:T(8,128)(2,1)}, bf16[640,2560]{1,0:T(8,128)(2,1)}) custom-call(bf16[640,2048]{1,0:T(8,128)(2,1)} %get-tuple-element.149.rows_ref.left_own_ref, bf16[2048,7680]{1,0:T(8,128)(2,1)} %all-gather.5.cloned.1.call-done.weight_ref.right_ref), custom_call_target="tpu_custom_call" | custom-call | flops 107374182400 | bytes 167772160 | tf_op jit(solution)/shard_map/ff_forward/pallas_call | solution.py:381
  272.6 14.9 %ff_backward.1.left_ref.own_ref = bf16[640,5120]{1,0:T(8,128)(2,1)} custom-call(bf16[640,2048]{1,0:T(8,128)(2,1)} %constant_dynamic-update-slice_fusion.7.grad_ref.left_own_ref.refs_4_, bf16[2048,7680]{1,0:T(8,128)(2,1)} %all-gather.5.cloned.1.call-done.weight_ref.right_ref, bf16[640,2560]{1,0:T(8,128)(2,1)S(1)} %copy-done.36, ...), custom_call_target="tpu_custom_call" | custom-call | flops 53687091200 | bytes 83886080 | tf_op jit(solution)/shard_map/ff_backward/pallas_call | solution.py:491
  289.5 14.0 %weight_grad.6 = bf16[8,128,2560]{2,1,0:T(8,128)(2,1)} custom-call(s32[9]{0:T(128)S(1)} %pad_add_fusion.2.index_ref, bf16[640,2048]{1,0:T(8,128)(2,1)} %constant_dynamic-update-slice_fusion.7.grad_ref.left_own_ref.refs_4_, bf16[640,2048]{1,0:T(8,128)(2,1)} %collective-permute-done.6.left_other_ref, bf16[640,2560]{1,0:T(8,128)(2,1)} %copy-done.25, ...), custom_call_target="tpu_custom_call" | custom-call | flops 53687091200 | bytes 94371840 | tf_op jit(solution)/shard_map/weight_grad/pallas_call | solution.py:542
  303.5 12.0 %matmul_nt.3.refs_0_ = bf16[640,1024]{1,0:T(8,128)(2,1)} custom-call(bf16[640,5120]{1,0:T(8,128)(2,1)} %ff_backward.1.left_ref.own_ref, bf16[2048,7680]{1,0:T(8,128)(2,1)} %all-gather.5.cloned.1.call-done.weight_ref.right_ref), custom_call_target="tpu_custom_call" | custom-call | flops 53687091200 | bytes 83886080 | tf_op jit(solution)/shard_map/matmul_nt/pallas_call | solution.py:403
  316.7 12.0 %matmul_nt.4.refs_2_ = bf16[640,1024]{1,0:T(8,128)(2,1)} custom-call(bf16[640,5120]{1,0:T(8,128)(2,1)} %ff_backward.1.left_ref.own_ref, bf16[2048,7680]{1,0:T(8,128)(2,1)} %all-gather.5.cloned.1.call-done.weight_ref.right_ref), custom_call_target="tpu_custom_call" | custom-call | flops 53687091200 | bytes 83886080 | tf_op jit(solution)/shard_map/matmul_nt/pallas_call | solution.py:403
  329.0 22.6 %weight_grad.7 = bf16[8,128,5120]{2,1,0:T(8,128)(2,1)} custom-call(s32[9]{0:T(128)S(1)} %pad_add_fusion.2.index_ref, bf16[640,2048]{1,0:T(8,128)(2,1)} %get-tuple-element.149.rows_ref.left_own_ref, bf16[640,2048]{1,0:T(8,128)(2,1)} %collective-permute-done.9.left_other_ref, bf16[640,5120]{1,0:T(8,128)(2,1)} %ff_backward.1.left_ref.own_ref, ...), custom_call_target="tpu_custom_call" | custom-call | flops 107374182400 | bytes 188743680 | tf_op jit(solution)/shard_map/weight_grad/pallas_call | solution.py:542
  353.6 11.9 %matmul_nt.5 = bf16[640,2048]{1,0:T(8,128)(2,1)} custom-call(bf16[640,2560]{1,0:T(8,128)(2,1)S(1)} %copy-done.26, bf16[2048,7680]{1,0:T(8,128)(2,1)} %all-gather.5.cloned.1.call-done.weight_ref.right_ref), custom_call_target="tpu_custom_call" | custom-call | flops 53687091200 | bytes 83886080 | tf_op jit(solution)/shard_map/matmul_nt/pallas_call | solution.py:403
  366.7 7.3 %collective-permute-done.11.refs_3_ = bf16[640,1024]{1,0:T(8,128)(2,1)} collective-permute-done((bf16[640,1024]{1,0:T(8,128)(2,1)}, bf16[640,1024]{1,0:T(8,128)(2,1)}, u32[]{:S(2)}, u32[]{:S(2)}) %collective-permute-start.11) | collective-permute-done | bytes 1310752 | tf_op jit(solution)/shard_map/ppermute | solution.py:650
  374.0 8.0 %norm_backward.2 = (bf16[640,2048]{1,0:T(8,128)(2,1)}, f32[1,2048]{1,0:T(1,128)S(1)}) custom-call(bf16[640,1024]{1,0:T(8,128)(2,1)} %matmul_nt.3.refs_0_, bf16[640,1024]{1,0:T(8,128)(2,1)} %collective-permute-done.8.refs_1_, bf16[640,1024]{1,0:T(8,128)(2,1)} %matmul_nt.4.refs_2_, bf16[640,1024]{1,0:T(8,128)(2,1)} %collective-permute-done.11.refs_3_, ...), custom_call_target="tpu_custom_call" | custom-call | flops 209715200 | bytes 125829120 | tf_op jit(solution)/shard_map/norm_backward/pallas_call | solution.py:468
  388.1 30.9 %attention_backward.1 = (f32[640,640]{1,0:T(8,128)}, f32[1536,384]{1,0:T(8,128)}) custom-call(s32[5]{0:T(128)S(1)} %copy-done.35, bf16[640,1024]{1,0:T(8,128)(2,1)S(1)} %copy-done.4, bf16[1536,384]{1,0:T(8,128)(2,1)S(1)} %copy-done.24, f32[1024,128]{1,0:T(8,128)S(1)} %copy-done.14, bf16[640,640]{1,0:T(8,128)(2,1)S(1)} %copy-done.30, f32[640,640]{1,0:T(8,128)} %copy-done.37, ...), custom_call_target="tpu_custom_call" | custom-call | flops 196608000000 | bytes 78643200 | tf_op jit(solution)/shard_map/attention_backward/pallas_call | solution.py:331
  443.3 8.0 %collective-permute-done.14 = bf16[128,384]{1,0:T(8,128)(2,1)S(1)} collective-permute-done((bf16[128,384]{1,0:T(8,128)(2,1)S(1)}, bf16[128,384]{1,0:T(8,128)(2,1)S(1)}, u32[]{:S(2)}, u32[]{:S(2)}) %collective-permute-start.14) | collective-permute-done | bytes 98336 | tf_op jit(solution)/shard_map/ppermute | solution.py:641
  456.2 6.6 collective-permute-done.15
  471.8 5.8 add_convert_fusion
  483.8 5.6 weight_grad.10
  491.7 16.3 %collective-permute-done.22.rest_0_ = bf16[4,128,640]{2,1,0:T(8,128)(2,1)} collective-permute-done((bf16[4,128,640]{2,1,0:T(8,128)(2,1)}, bf16[4,128,640]{2,1,0:T(8,128)(2,1)}, u32[]{:S(2)}, u32[]{:S(2)}) %collective-permute-start.22) | collective-permute-done | bytes 655392 | tf_op jit(solution)/shard_map/ppermute | solution.py:644
  515.1 22.6 %collective-permute-done.25.rest_0_ = bf16[4,128,1024]{2,1,0:T(8,128)(2,1)} collective-permute-done((bf16[4,128,1024]{2,1,0:T(8,128)(2,1)}, bf16[4,128,1024]{2,1,0:T(8,128)(2,1)}, u32[]{:S(2)}, u32[]{:S(2)}) %collective-permute-start.25) | collective-permute-done | bytes 1048608 | tf_op jit(solution)/shard_map/ppermute | solution.py:644
  546.6 7.4 %norm_backward.3 = (bf16[640,2048]{1,0:T(8,128)(2,1)}, f32[1,2048]{1,0:T(1,128)S(1)}) custom-call(bf16[640,1024]{1,0:T(8,128)(2,1)S(1)} %copy-done.8, bf16[640,1024]{1,0:T(8,128)(2,1)S(1)} %copy-done.10, bf16[640,1024]{1,0:T(8,128)(2,1)S(1)} %copy-done.6, bf16[640,1024]{1,0:T(8,128)(2,1)S(1)} %collective-permute-done.21.refs_3_, ...), custom_call_target="tpu_custom_call" | custom-call | flops 209715200 | bytes 125829120 | tf_op jit(solution)/shard_map/norm_backward/pallas_call | solution.py:468
  566.0 6.0 collective-permute-start.37
  573.6 11.5 %collective-permute-done.28 = f32[33,128]{1,0:T(8,128)S(1)} collective-permute-done((f32[33,128]{1,0:T(8,128)S(1)}, f32[33,128]{1,0:T(8,128)S(1)}, u32[]{:S(2)}, u32[]{:S(2)}) %collective-permute-start.28) | collective-permute-done | bytes 16928 | tf_op jit(solution)/shard_map/ppermute | solution.py:641
  591.0 7.4 %collective-permute-done.30 = f32[33,128]{1,0:T(8,128)S(1)} collective-permute-done((f32[33,128]{1,0:T(8,128)S(1)}, f32[33,128]{1,0:T(8,128)S(1)}, u32[]{:S(2)}, u32[]{:S(2)}) %collective-permute-start.30) | collective-permute-done | bytes 16928 | tf_op jit(solution)/shard_map/ppermute | solution.py:641
  602.8 36.1 %collective-permute-done.32 = bf16[128,1024]{1,0:T(8,128)(2,1)S(1)} collective-permute-done((bf16[128,1024]{1,0:T(8,128)(2,1)S(1)}, bf16[128,1024]{1,0:T(8,128)(2,1)S(1)}, u32[]{:S(2)}, u32[]{:S(2)}) %collective-permute-start.32) | collective-permute-done | bytes 262176 | tf_op jit(solution)/shard_map/ppermute | solution.py:641
  639.2 9.2 %collective-permute-done.38 = bf16[128,640]{1,0:T(8,128)(2,1)S(1)} collective-permute-done((bf16[128,640]{1,0:T(8,128)(2,1)S(1)}, bf16[128,640]{1,0:T(8,128)(2,1)S(1)}, u32[]{:S(2)}, u32[]{:S(2)}) %collective-permute-start.38) | collective-permute-done | bytes 163872 | tf_op jit(solution)/shard_map/ppermute | solution.py:641
  (295 shorter events, 166.9 us)
Async XLA Ops:
  7.2 72.4 %all-gather.3.cloned.1.call-start = ((), (), s32[]{:S(2)}) async-start(), calls=%async_computation.2 | async-start | bytes 7241728 | tf_op jit(solution)/shard_map/all_gather | solution.py:666
  11.0 237.6 %all-gather.5.cloned.1.call-start = ((), (), s32[]{:S(2)}) async-start(), calls=%async_computation.3 | async-start | bytes 33423360 | tf_op jit(solution)/shard_map/all_gather | solution.py:672
  16.9 635.0 %reduce-scatter.5.cloned.1.call-start = ((), (), s32[]{:S(2)}) async-start(), calls=%async_computation.5 | async-start | bytes 5898240 | tf_op jit(solution)/shard_map/reduce_scatter | solution.py:767
  92.7 13.7 %collective-permute-start.2 = (bf16[128,384]{1,0:T(8,128)(2,1)S(1)}, bf16[128,384]{1,0:T(8,128)(2,1)S(1)}, u32[]{:S(2)}, u32[]{:S(2)}) collective-permute-start(bf16[128,384]{1,0:T(8,128)(2,1)S(1)} %get-tuple-element.150), channel_id=1, source_target_pairs={{0,4},{2,6},{4,8},{6,10},{8,12},{10,14},{12,0},{14,2},{1,5},{3,7},... | collective-permute-start | bytes 294920 | tf_op jit(solution)/shard_map/ppermute | solution.py:641
  108.6 34.8 %collective-permute-start.4 = (bf16[2048,384]{0,1:T(8,128)(2,1)S(1)}, bf16[2048,384]{0,1:T(8,128)(2,1)S(1)}, u32[]{:S(2)}, u32[]{:S(2)}) collective-permute-start(bf16[2048,384]{0,1:T(8,128)(2,1)S(1)} %slice.176), channel_id=1, source_target_pairs={{0,1},{1,0},{2,3},{3,2},{4,5},{5,4},{6,7},{7,6},{8,9},{9,8},{10,11... | collective-permute-start | bytes 4718600 | tf_op jit(solution)/shard_map/ppermute | solution.py:650
  151.2 56.7 %collective-permute-start.5 = (bf16[640,2048]{1,0:T(8,128)(2,1)}, bf16[640,2048]{1,0:T(8,128)(2,1)}, u32[]{:S(2)}, u32[]{:S(2)}) collective-permute-start(bf16[640,2048]{1,0:T(8,128)(2,1)} %convolution_convert_fusion.1), channel_id=1, source_target_pairs={{0,1},{1,0},{2,3},{3,2},{4,5},{5,4},{6,7},{7,6},{8,9},{9,8},{10,11... | collective-permute-start | bytes 7864328 | tf_op jit(solution)/shard_map/ppermute | solution.py:650
  154.5 133.3 %collective-permute-start.6 = (bf16[640,2048]{1,0:T(8,128)(2,1)}, bf16[640,2048]{1,0:T(8,128)(2,1)}, u32[]{:S(2)}, u32[]{:S(2)}) collective-permute-start(bf16[640,2048]{1,0:T(8,128)(2,1)} %constant_dynamic-update-slice_fusion.7.grad_ref.left_own_ref.refs_4_), channel_id=1, source_target_pairs={{0,16},{16,0},{1,17},{17,1},{2,18},{18,2},{3,19},{19,3},{4,20},{20... | collective-permute-start | bytes 7864328 | tf_op jit(solution)/shard_map/ppermute | solution.py:647
  220.1 109.0 %collective-permute-start.9 = (bf16[640,2048]{1,0:T(8,128)(2,1)}, bf16[640,2048]{1,0:T(8,128)(2,1)}, u32[]{:S(2)}, u32[]{:S(2)}) collective-permute-start(bf16[640,2048]{1,0:T(8,128)(2,1)} %get-tuple-element.149.rows_ref.left_own_ref), channel_id=1, source_target_pairs={{0,16},{16,0},{1,17},{17,1},{2,18},{18,2},{3,19},{19,3},{4,20},{20... | collective-permute-start | bytes 7864328 | tf_op jit(solution)/shard_map/ppermute | solution.py:647
  269.5 18.3 %collective-permute-start.7 = (bf16[640,2560]{1,0:T(8,128)(2,1)S(1)}, bf16[640,2560]{1,0:T(8,128)(2,1)S(1)}, u32[]{:S(2)}, u32[]{:S(2)}) collective-permute-start(bf16[640,2560]{1,0:T(8,128)(2,1)S(1)} %get-tuple-element.71.own_ref.left_ref), channel_id=1, source_target_pairs={{0,16},{16,0},{1,17},{17,1},{2,18},{18,2},{3,19},{19,3},{4,20},{20... | collective-permute-start | bytes 9830408 | tf_op jit(solution)/shard_map/ppermute | solution.py:647
  287.6 41.5 %collective-permute-start.10 = (bf16[640,5120]{1,0:T(8,128)(2,1)}, bf16[640,5120]{1,0:T(8,128)(2,1)}, u32[]{:S(2)}, u32[]{:S(2)}) collective-permute-start(bf16[640,5120]{1,0:T(8,128)(2,1)} %ff_backward.1.left_ref.own_ref), channel_id=1, source_target_pairs={{0,16},{16,0},{1,17},{17,1},{2,18},{18,2},{3,19},{19,3},{4,20},{20... | collective-permute-start | bytes 19660808 | tf_op jit(solution)/shard_map/ppermute | solution.py:647
  315.5 36.2 %collective-permute-start.8 = (bf16[640,1024]{1,0:T(8,128)(2,1)}, bf16[640,1024]{1,0:T(8,128)(2,1)}, u32[]{:S(2)}, u32[]{:S(2)}) collective-permute-start(bf16[640,1024]{1,0:T(8,128)(2,1)} %matmul_nt.3.refs_0_), channel_id=1, source_target_pairs={{0,1},{1,0},{2,3},{3,2},{4,5},{5,4},{6,7},{7,6},{8,9},{9,8},{10,11... | collective-permute-start | bytes 3932168 | tf_op jit(solution)/shard_map/ppermute | solution.py:650
  328.6 45.3 %collective-permute-start.11 = (bf16[640,1024]{1,0:T(8,128)(2,1)}, bf16[640,1024]{1,0:T(8,128)(2,1)}, u32[]{:S(2)}, u32[]{:S(2)}) collective-permute-start(bf16[640,1024]{1,0:T(8,128)(2,1)} %matmul_nt.4.refs_2_), channel_id=1, source_target_pairs={{0,1},{1,0},{2,3},{3,2},{4,5},{5,4},{6,7},{7,6},{8,9},{9,8},{10,11... | collective-permute-start | bytes 3932168 | tf_op jit(solution)/shard_map/ppermute | solution.py:650
  329.0 325.6 %reduce-scatter.3.cloned.1.call-start = ((), (), s32[]{:S(2)}) async-start(), calls=%async_computation.4 | async-start | bytes 11796480 | tf_op jit(solution)/shard_map/reduce_scatter | solution.py:772
  365.5 101.2 %collective-permute-start.19 = (bf16[640,2048]{1,0:T(8,128)(2,1)}, bf16[640,2048]{1,0:T(8,128)(2,1)}, u32[]{:S(2)}, u32[]{:S(2)}) collective-permute-start(bf16[640,2048]{1,0:T(8,128)(2,1)} %matmul_nt.5), channel_id=1, source_target_pairs={{0,1},{1,0},{2,3},{3,2},{4,5},{5,4},{6,7},{7,6},{8,9},{9,8},{10,11... | collective-permute-start | bytes 7864328 | tf_op jit(solution)/shard_map/ppermute | solution.py:650
  381.9 84.8 %collective-permute-start.17 = (bf16[640,2048]{1,0:T(8,128)(2,1)}, bf16[640,2048]{1,0:T(8,128)(2,1)}, u32[]{:S(2)}, u32[]{:S(2)}) collective-permute-start(bf16[640,2048]{1,0:T(8,128)(2,1)} %get-tuple-element.73.left_own_ref.refs_5_), channel_id=1, source_target_pairs={{0,16},{16,0},{1,17},{17,1},{2,18},{18,2},{3,19},{19,3},{4,20},{20... | collective-permute-start | bytes 7864328 | tf_op jit(solution)/shard_map/ppermute | solution.py:647
  432.0 33.5 %collective-permute-start.16 = (bf16[640,1024]{1,0:T(8,128)(2,1)S(1)}, bf16[640,1024]{1,0:T(8,128)(2,1)S(1)}, u32[]{:S(2)}, u32[]{:S(2)}) collective-permute-start(bf16[640,1024]{1,0:T(8,128)(2,1)S(1)} %convolution_convert_fusion.3.refs_0_), channel_id=1, source_target_pairs={{0,1},{1,0},{2,3},{3,2},{4,5},{5,4},{6,7},{7,6},{8,9},{9,8},{10,11... | collective-permute-start | bytes 3932168 | tf_op jit(solution)/shard_map/ppermute | solution.py:650
  433.2 33.5 %collective-permute-start.18 = (bf16[640,640]{1,0:T(8,128)(2,1)S(1)}, bf16[640,640]{1,0:T(8,128)(2,1)S(1)}, u32[]{:S(2)}, u32[]{:S(2)}) collective-permute-start(bf16[640,640]{1,0:T(8,128)(2,1)S(1)} %copy-done.30), channel_id=1, source_target_pairs={{0,16},{16,0},{1,17},{17,1},{2,18},{18,2},{3,19},{19,3},{4,20},{20... | collective-permute-start | bytes 2457608 | tf_op jit(solution)/shard_map/ppermute | solution.py:647
  439.7 11.6 %collective-permute-start.14 = (bf16[128,384]{1,0:T(8,128)(2,1)S(1)}, bf16[128,384]{1,0:T(8,128)(2,1)S(1)}, u32[]{:S(2)}, u32[]{:S(2)}) collective-permute-start(bf16[128,384]{1,0:T(8,128)(2,1)S(1)} %get-tuple-element.162), channel_id=1, source_target_pairs={{0,8},{2,10},{4,12},{6,14},{8,0},{10,2},{12,4},{14,6},{1,9},{3,11}... | collective-permute-start | bytes 294920 | tf_op jit(solution)/shard_map/ppermute | solution.py:641
  462.8 18.4 %collective-permute-start.23 = (bf16[640,2048]{1,0:T(8,128)(2,1)S(1)}, bf16[640,2048]{1,0:T(8,128)(2,1)}, u32[]{:S(2)}, u32[]{:S(2)}) collective-permute-start(bf16[640,2048]{1,0:T(8,128)(2,1)S(1)} %copy-done.42), channel_id=1, source_target_pairs={{0,16},{16,0},{1,17},{17,1},{2,18},{18,2},{3,19},{19,3},{4,20},{20... | collective-permute-start | bytes 7864328 | tf_op jit(solution)/shard_map/ppermute | solution.py:647
  480.7 27.3 %collective-permute-start.22 = (bf16[4,128,640]{2,1,0:T(8,128)(2,1)}, bf16[4,128,640]{2,1,0:T(8,128)(2,1)}, u32[]{:S(2)}, u32[]{:S(2)}) collective-permute-start(bf16[4,128,640]{2,1,0:T(8,128)(2,1)} %weight_grad.8), channel_id=1, source_target_pairs={{0,2},{2,0},{4,6},{6,4},{8,10},{10,8},{12,14},{14,12},{1,3},{3,1},... | collective-permute-start | bytes 1966088 | tf_op jit(solution)/shard_map/ppermute | solution.py:644
  489.4 48.3 %collective-permute-start.25 = (bf16[4,128,1024]{2,1,0:T(8,128)(2,1)}, bf16[4,128,1024]{2,1,0:T(8,128)(2,1)}, u32[]{:S(2)}, u32[]{:S(2)}) collective-permute-start(bf16[4,128,1024]{2,1,0:T(8,128)(2,1)} %weight_grad.10), channel_id=1, source_target_pairs={{0,2},{2,0},{4,6},{6,4},{8,10},{10,8},{12,14},{14,12},{1,3},{3,1},... | collective-permute-start | bytes 3145736 | tf_op jit(solution)/shard_map/ppermute | solution.py:644
  490.2 52.7 %collective-permute-start.21 = (bf16[640,1024]{1,0:T(8,128)(2,1)}, bf16[640,1024]{1,0:T(8,128)(2,1)S(1)}, u32[]{:S(2)}, u32[]{:S(2)}) collective-permute-start(bf16[640,1024]{1,0:T(8,128)(2,1)} %convolution_convert_fusion.2.refs_2_), channel_id=1, source_target_pairs={{0,1},{1,0},{2,3},{3,2},{4,5},{5,4},{6,7},{7,6},{8,9},{9,8},{10,11... | collective-permute-start | bytes 3932168 | tf_op jit(solution)/shard_map/ppermute | solution.py:650
  490.2 52.6 %collective-permute-start.20 = (bf16[640,384]{1,0:T(8,128)(2,1)}, bf16[640,384]{1,0:T(8,128)(2,1)S(1)}, u32[]{:S(2)}, u32[]{:S(2)}) collective-permute-start(bf16[640,384]{1,0:T(8,128)(2,1)} %copy-done.17), channel_id=1, source_target_pairs={{0,1},{1,0},{2,3},{3,2},{4,5},{5,4},{6,7},{7,6},{8,9},{9,8},{10,11... | collective-permute-start | bytes 1474568 | tf_op jit(solution)/shard_map/ppermute | solution.py:650
  566.0 73.2 %collective-permute-start.36 = (bf16[128,640]{1,0:T(8,128)(2,1)S(1)}, bf16[128,640]{1,0:T(8,128)(2,1)S(1)}, u32[]{:S(2)}, u32[]{:S(2)}) collective-permute-start(bf16[128,640]{1,0:T(8,128)(2,1)S(1)} %get-tuple-element.157), channel_id=1, source_target_pairs={{0,4},{2,6},{4,8},{6,10},{8,12},{10,14},{12,0},{14,2},{1,5},{3,7},... | collective-permute-start | bytes 491528 | tf_op jit(solution)/shard_map/ppermute | solution.py:641
  566.0 73.2 %collective-permute-start.37 = (bf16[128,640]{1,0:T(8,128)(2,1)S(1)}, bf16[128,640]{1,0:T(8,128)(2,1)S(1)}, u32[]{:S(2)}, u32[]{:S(2)}) collective-permute-start(bf16[128,640]{1,0:T(8,128)(2,1)S(1)} %get-tuple-element.159), channel_id=1, source_target_pairs={{0,8},{2,10},{4,12},{6,14},{8,0},{10,2},{12,4},{14,6},{1,9},{3,11}... | collective-permute-start | bytes 491528 | tf_op jit(solution)/shard_map/ppermute | solution.py:641
  572.0 13.1 %collective-permute-start.28 = (f32[33,128]{1,0:T(8,128)S(1)}, f32[33,128]{1,0:T(8,128)S(1)}, u32[]{:S(2)}, u32[]{:S(2)}) collective-permute-start(f32[33,128]{1,0:T(8,128)S(1)} %fusion.39), channel_id=1, source_target_pairs={{0,4},{2,6},{4,8},{6,10},{8,12},{10,14},{12,0},{14,2},{1,5},{3,7},... | collective-permute-start | bytes 50696 | tf_op jit(solution)/shard_map/ppermute | solution.py:641
  572.1 15.4 %collective-permute-start.29 = (f32[33,128]{1,0:T(8,128)S(1)}, f32[33,128]{1,0:T(8,128)S(1)}, u32[]{:S(2)}, u32[]{:S(2)}) collective-permute-start(f32[33,128]{1,0:T(8,128)S(1)} %fusion.39), channel_id=1, source_target_pairs={{0,8},{2,10},{4,12},{6,14},{8,0},{10,2},{12,4},{14,6},{1,9},{3,11}... | collective-permute-start | bytes 50696 | tf_op jit(solution)/shard_map/ppermute | solution.py:641
  572.1 26.2 %collective-permute-start.30 = (f32[33,128]{1,0:T(8,128)S(1)}, f32[33,128]{1,0:T(8,128)S(1)}, u32[]{:S(2)}, u32[]{:S(2)}) collective-permute-start(f32[33,128]{1,0:T(8,128)S(1)} %fusion.39), channel_id=1, source_target_pairs={{0,12},{2,14},{4,0},{6,2},{8,4},{10,6},{12,8},{14,10},{1,13},{3,15... | collective-permute-start | bytes 50696 | tf_op jit(solution)/shard_map/ppermute | solution.py:641
  585.1 17.7 %collective-permute-start.31 = (bf16[128,1024]{1,0:T(8,128)(2,1)S(1)}, bf16[128,1024]{1,0:T(8,128)(2,1)S(1)}, u32[]{:S(2)}, u32[]{:S(2)}) collective-permute-start(bf16[128,1024]{1,0:T(8,128)(2,1)S(1)} %get-tuple-element.152), channel_id=1, source_target_pairs={{0,4},{2,6},{4,8},{6,10},{8,12},{10,14},{12,0},{14,2},{1,5},{3,7},... | collective-permute-start | bytes 786440 | tf_op jit(solution)/shard_map/ppermute | solution.py:641
  587.4 51.5 %collective-permute-start.32 = (bf16[128,1024]{1,0:T(8,128)(2,1)S(1)}, bf16[128,1024]{1,0:T(8,128)(2,1)S(1)}, u32[]{:S(2)}, u32[]{:S(2)}) collective-permute-start(bf16[128,1024]{1,0:T(8,128)(2,1)S(1)} %get-tuple-element.154), channel_id=1, source_target_pairs={{0,8},{2,10},{4,12},{6,14},{8,0},{10,2},{12,4},{14,6},{1,9},{3,11}... | collective-permute-start | bytes 786440 | tf_op jit(solution)/shard_map/ppermute | solution.py:641
  601.2 37.7 %collective-permute-start.33 = (bf16[128,1024]{1,0:T(8,128)(2,1)S(1)}, bf16[128,1024]{1,0:T(8,128)(2,1)S(1)}, u32[]{:S(2)}, u32[]{:S(2)}) collective-permute-start(bf16[128,1024]{1,0:T(8,128)(2,1)S(1)} %get-tuple-element.153), channel_id=1, source_target_pairs={{0,12},{2,14},{4,0},{6,2},{8,4},{10,6},{12,8},{14,10},{1,13},{3,15... | collective-permute-start | bytes 786440 | tf_op jit(solution)/shard_map/ppermute | solution.py:641
  602.8 45.6 %collective-permute-start.38 = (bf16[128,640]{1,0:T(8,128)(2,1)S(1)}, bf16[128,640]{1,0:T(8,128)(2,1)S(1)}, u32[]{:S(2)}, u32[]{:S(2)}) collective-permute-start(bf16[128,640]{1,0:T(8,128)(2,1)S(1)} %get-tuple-element.158), channel_id=1, source_target_pairs={{0,12},{2,14},{4,0},{6,2},{8,4},{10,6},{12,8},{14,10},{1,13},{3,15... | collective-permute-start | bytes 491528 | tf_op jit(solution)/shard_map/ppermute | solution.py:641
  (69 other events, 829.7 us)
Sparse Core Ops, SparseCore 0:
  11.1 68.5 all-gather.2
  81.8 166.6 all-gather.4
  329.1 102.5 reduce-scatter.4
  435.1 215.9 reduce-scatter.2

commit v3 on v2

--- a/solution.py
+++ b/solution.py
@@ -17,9 +17,11 @@
     return pltpu.CompilerParams(vmem_limit_bytes=megabytes << 20)
 
 
-def cost(flops, bytes_accessed, transcendentals=0):
+def cost(flops, bytes_accessed, transcendentals=0, weight=1):
     return pl.CostEstimate(
-        flops=int(flops) * 8, bytes_accessed=int(bytes_accessed) * 8, transcendentals=int(transcendentals) * 8
+        flops=int(flops * weight * 0.25),
+        bytes_accessed=int(bytes_accessed * weight * 0.25),
+        transcendentals=int(transcendentals * weight * 0.25),
     )
 
 
@@ -357,7 +359,7 @@
             jax.ShapeDtypeStruct((key_count, slot_count * lanes), f32),
         ],
         compiler_params=params(),
-        cost_estimate=cost(elements * 2500, elements, elements),
+        cost_estimate=cost(elements * 2500, elements, elements, 1),
         name="attention_backward",
     )(slots, rotated, keys, prompt_mask_t, attended, inverse, grad_attended)
 
@@ -415,24 +417,40 @@
     )(left, weights)
 
 
-def split_tiles_kernel(both_ref, gate_ref, up_ref):
-    gate_ref[...] = both_ref[:, :ff_tile].astype(f32)
-    up_ref[...] = both_ref[:, ff_tile:].astype(f32)
-
-
-def split_tiles(both):
-    rows, wide = both.shape
+def split_tiles_kernel(*refs, bounds):
+    gate_ref, up_ref = refs[-2:]
+    step = pl.program_id(0)
+    for part_ref, start, stop in zip(refs, bounds, bounds[1:]):
+
+        @pl.when(jnp.logical_and(step >= start, step < stop))
+        def _(part_ref=part_ref):
+            gate_ref[...] = part_ref[:, :ff_tile].astype(f32)
+            up_ref[...] = part_ref[:, ff_tile:].astype(f32)
+
+
+def split_tiles(parts):
+    rows = parts[0].shape[0]
+    bounds = [0]
+    for part in parts:
+        bounds.append(bounds[-1] + part.shape[1] // (2 * ff_tile))
     out = pl.BlockSpec((rows, ff_tile), lambda j: (0, j))
-    return pl.pallas_call(
-        split_tiles_kernel,
-        grid=(wide // (2 * ff_tile),),
-        in_specs=[pl.BlockSpec((rows, 2 * ff_tile), lambda j: (0, j))],
+    in_specs = [
+        pl.BlockSpec(
+            (rows, 2 * ff_tile),
+            lambda j, start=start, stop=stop: (0, jnp.clip(j - start, 0, stop - start - 1)),
+        )
+        for start, stop in zip(bounds, bounds[1:])
+    ]
+    return pl.pallas_call(
+        partial(split_tiles_kernel, bounds=bounds),
+        grid=(bounds[-1],),
+        in_specs=in_specs,
         out_specs=[out, out],
-        out_shape=[jax.ShapeDtypeStruct((rows, wide // 2), f32)] * 2,
+        out_shape=[jax.ShapeDtypeStruct((rows, bounds[-1] * ff_tile), f32)] * 2,
         compiler_params=params(),
-        cost_estimate=cost(0, rows * wide * 6),
+        cost_estimate=cost(0, rows * bounds[-1] * ff_tile * 12),
         name="split_tiles",
-    )(both)
+    )(*parts)
 
 
 def norm_back_kernel(*refs, halves, extra):
@@ -527,17 +545,18 @@
         out_ref[piece] = part.astype(bf16)
 
 
-def weight_grad(indices, rank, block, left, left_other, own, other, received=None):
+def weight_grad(indices, rank, block, left, left_other, own, other, received=None, first=0, wide=None):
     pieces = indices.shape[0]
-    rows, wide = own.shape
+    rows = own.shape[0]
+    wide = wide or own.shape[1]
     half = left.shape[1] // 2
-    tile = next(size for size in (640, 512, 384, lanes) if wide % size == 0)
+    tile = next(size for size in (640, 512, 384, lanes) if wide % size == 0 and first % size == 0)
     out = pl.BlockSpec((pieces, block, tile), lambda j, s: (0, 0, j))
     left_spec = pl.BlockSpec((rows, half), lambda j, s: (0, s[pieces]))
-    in_specs = [left_spec] * 2 + [pl.BlockSpec((rows, tile), lambda j, s: (0, j))] * 2
+    in_specs = [left_spec] * 2 + [pl.BlockSpec((rows, tile), lambda j, s: (0, j + first // tile))] * 2
     operands = [left, left_other, own, other]
     if received is not None:
-        in_specs.append(out)
+        in_specs.append(pl.BlockSpec((pieces, block, tile), lambda j, s: (0, 0, j)))
         operands.append(received)
     return pl.pallas_call(
         partial(weight_grad_kernel, pieces=pieces, block=block),
@@ -738,15 +757,27 @@
     resid = resid32.astype(bf16)
     second_scale = lax.rsqrt(jnp.mean(resid32 * resid32, axis=-1, keepdims=True) + epsilon)
     normed_two = (resid32 * second_scale * ff_gain32).astype(bf16)
+    grad_out = jnp.concatenate([grad_prompt, grad_continuation], axis=0)
+    normed_two, two_other, out_other, one_other, attended_other = after(
+        (normed_two, dp_swap(normed_two), dp_swap(grad_out), dp_swap(normed_low), dp_swap(attended))
+    )
     hidden, gate_factor, up_factor = ff_forward(normed_two, ff_weights, units)
 
-    def send_part(left, left_other, own, other):
-        return weight_grad(other_blocks, data_rank, block, left, left_other, own, other)
-
-    def keep_part(left, left_other, own, other, received):
-        return weight_grad(own_blocks, data_rank, block, left, left_other, own, other, received)
-
-    every_block = jnp.arange(ring, dtype=jnp.int32)
+    def send_part(left, left_other, own, other, order=None, **span):
+        indices = (steps if order is None else order) * ysize + 1 - yrank
+        return weight_grad(indices, data_rank, block, left, left_other, own, other, **span)
+
+    def keep_part(left, left_other, own, other, received, order=None, **span):
+        indices = (steps if order is None else order) * ysize + yrank
+        return weight_grad(indices, data_rank, block, left, left_other, own, other, received, **span)
+
+    z_groups = [[z * ysize + y for z in range(zsize)] for y in range(ysize)]
+
+    def z_scattered(kept):
+        scattered = lax.psum_scatter(
+            kept, "ctx", scatter_dimension=0, axis_index_groups=z_groups, tiled=True
+        )
+        return scattered[0]
 
     def finish(kept):
         total = kept[0].astype(f32)
@@ -754,32 +785,32 @@
             total = total + z_pass(kept[step], step).astype(f32)
         return total
 
-    grad_out = jnp.concatenate([grad_prompt, grad_continuation], axis=0)
-    out_pair = (grad_out, dp_swap(grad_out))
-    two_pair = (normed_two, dp_swap(normed_two))
-    one_pair = (normed_low, dp_swap(normed_low))
-    hidden_other = dp_swap(hidden)
+    out_pair, two_pair, one_pair = (grad_out, out_other), (normed_two, two_other), (normed_low, one_other)
 
     grad_ff = ff_backward(grad_out, ff_weights, gate_factor, up_factor)
+    hidden_other, grad_ff = after((dp_swap(hidden), grad_ff))
     grad_ff_other = dp_swap(grad_ff)
-    down_grad = weight_grad(every_block, data_rank, block, *out_pair, hidden, hidden_other)
-    grad_ff, down_grad = after((grad_ff, down_grad))
-    down_done = lax.psum_scatter(down_grad, "ctx", scatter_dimension=0, tiled=True)[0]
-    grad_parts = [matmul_nt(grad_ff, ff_weights, 0, 0, half_width)]
-    grad_parts.append(matmul_nt(after((grad_ff, grad_parts[0]))[0], ff_weights, 0, half_width, half_width))
-    grad_ff, hidden_next, second_part = after((grad_ff, hidden, grad_parts[1]))
-    ff_grad = weight_grad(every_block, data_rank, block, *two_pair, grad_ff, grad_ff_other)
-    ff_done = lax.psum_scatter(ff_grad, "ctx", scatter_dimension=0, tiled=True)[0]
-    first_other, ff_grad, hidden_next = after((tp_swap(grad_parts[0]), ff_grad, hidden_next))
+    down_sent = send_part(*out_pair, hidden, hidden_other)
+    hidden, grad_ff, down_sent = after((hidden, grad_ff, down_sent))
+    first_part = matmul_nt(grad_ff, ff_weights, 0, 0, half_width)
+    grad_ff, first_part = after((grad_ff, first_part))
+    second_part = matmul_nt(grad_ff, ff_weights, 0, half_width, half_width)
+    grad_ff, hidden_next, second_part = after((grad_ff, hidden, second_part))
+    ff_pair = (grad_ff, grad_ff_other)
+    ff_sent = send_part(*two_pair, *ff_pair)
+    first_other, hidden_next = after((tp_swap(first_part), hidden_next, ff_sent))[:2]
     ff_part = matmul_nt(hidden_next, ff_weights, 2)
     ff_part_other = tp_swap(ff_part)
     ff_part, second_other = after((ff_part, tp_swap(second_part)))
     grad_resid_low, grad_ff_gain = norm_backward(
-        [grad_parts[0], first_other, second_part, second_other], None, grad_out, resid, second_scale, ff_gain32
+        [first_part, first_other, second_part, second_other], None, grad_out, resid, second_scale, ff_gain32
     )
     resid_pair = (grad_resid_low, dp_swap(grad_resid_low))
-    attended_other = dp_swap(attended)
     grad_attended = dot_nn(grad_resid_low, out_weights_t).astype(bf16)
+    down_received, grad_attended = after((y_swap(down_sent), grad_attended))
+    down_kept = keep_part(*out_pair, hidden_next, hidden_other, down_received)
+    down_done = z_scattered(down_kept)
+    grad_attended = after((grad_attended, down_kept))[0]
     grad_query, grad_keys = attention_backward(
         slots,
         rotated,
@@ -803,32 +834,30 @@
         for half in range(2)
     ]
     received_keys = y_swap(grad_keys_prompt[half_prompt:])
-    received_keys, query_parts[0], query_parts[1] = after((received_keys, query_parts[0], query_parts[1]))
     query_others = [tp_swap(part) for part in query_parts]
+    received_keys, ff_part_other = after((received_keys, ff_part_other, *query_parts))[:2]
     kept_keys = (grad_keys_prompt[:half_prompt].astype(f32) + received_keys.astype(f32)).astype(bf16)
+    z_keys = after(
+        tuple(z_pass(kept_keys[step * prompt_here : (step + 1) * prompt_here], step) for step in range(1, zsize))
+    )
+    query_others[0], z_keys = after((query_others[0], z_keys))
+    ff_received = after((y_swap(ff_sent), z_keys[0]))[0]
+    ff_done = z_scattered(keep_part(*two_pair, *ff_pair, ff_received))
     own_keys = kept_keys[:prompt_here].astype(f32)
-    for step in range(1, zsize):
-        own_keys = own_keys + z_pass(
-            kept_keys[step * prompt_here : (step + 1) * prompt_here], step
-        ).astype(f32)
-    ff_part, ff_part_other, resid_out, kept_keys = after((ff_part, ff_part_other, resid, kept_keys))
-    own_keys, query_others[0] = after((own_keys, query_others[0]))
-    output = (resid_out.astype(f32) + (ff_part.astype(f32) + ff_part_other.astype(f32))).astype(bf16)
+    for piece in z_keys:
+        own_keys = own_keys + piece.astype(f32)
     grad_key_value = jnp.concatenate([own_keys, grad_keys[prompt_length:]], axis=0)
-    out_sent = send_part(*resid_pair, attended, attended_other)
-    grad_key_value, out_sent, output = after((grad_key_value, out_sent, output))
+    out_sent = send_part(*resid_pair, attended, attended_other, zs)
+    grad_key_value = after((grad_key_value, out_sent))[0]
     grad_shared_low, key_gain_parts = head_prep_back(
         raw, pairs, grad_key_value, cos_table, sin_table, gains, True, head_size
     )
     grad_shared_other = tp_swap(grad_shared_low)
     grad_qkv = jnp.concatenate([grad_query_low, grad_shared_low], axis=1)
     grad_qkv_other = dp_swap(grad_qkv)
-    qkv_sent = send_part(*one_pair, grad_qkv, grad_qkv_other)
-    out_kept = keep_part(*resid_pair, attended, attended_other, y_swap(out_sent))
-    qkv_kept = keep_part(*one_pair, grad_qkv, grad_qkv_other, y_swap(qkv_sent))
-    grad_shared_other, query_others[1], out_kept, qkv_kept = after(
-        (grad_shared_other, query_others[1], out_kept, qkv_kept)
-    )
+    qkv_sent = send_part(*one_pair, grad_qkv, grad_qkv_other, zs)
+    qkv_kept = keep_part(*one_pair, grad_qkv, grad_qkv_other, y_swap(qkv_sent), zs)
+    query_others[1], grad_shared_other = after((query_others[1], grad_shared_other, qkv_kept))[:2]
     shared_part = dot_nt(
         jnp.concatenate([grad_shared_low, grad_shared_other], axis=1), shared_weights
     ).astype(bf16)
@@ -840,10 +869,23 @@
         first_scale,
         attn_gain32,
     )
+    qkv_pieces = [z_pass(qkv_kept[step], step) for step in range(1, zsize)]
+    out_received, grad_input = after((y_swap(out_sent), grad_input))
+    gain_gate, qkv_pieces = after((grad_input, qkv_pieces))
+    ff_part, ff_part_other, resid_out = after((ff_part, ff_part_other, resid, grad_input))[:3]
+    output = (resid_out.astype(f32) + (ff_part.astype(f32) + ff_part_other.astype(f32))).astype(bf16)
+    query_gain_sum = jnp.sum(query_gain_parts.reshape(-1, head_size), axis=0)
+    key_gain_sum = jnp.sum(key_gain_parts[:, 0, :head_size], axis=0)
+    gain_sums = jnp.concatenate([grad_attn_gain[0], grad_ff_gain[0], query_gain_sum, key_gain_sum]).reshape(-1, lanes)
+    gain_sums = gain_sums + dp_swap(gain_sums)
+    gain_sums = gain_sums + y_swap(gain_sums)
+    out_kept = keep_part(*resid_pair, attended, attended_other, out_received, zs)
     down_done = down_done.astype(f32).T
-    gate_done, up_done = split_tiles(ff_done)
+    gate_done, up_done = split_tiles([ff_done])
     out_done = finish(out_kept).T
-    qkv_done = finish(qkv_kept)
+    qkv_done = qkv_kept[0].astype(f32)
+    for piece in qkv_pieces:
+        qkv_done = qkv_done + piece.astype(f32)
 
     shared_done = qkv_done[:, query_width:]
     shared_other = tp_swap(shared_done)
@@ -861,11 +903,6 @@
         for which in range(2)
     )
 
-    query_gain_sum = jnp.sum(query_gain_parts.reshape(-1, head_size), axis=0)
-    key_gain_sum = jnp.sum(key_gain_parts[:, 0, :head_size], axis=0)
-    gain_sums = jnp.concatenate([grad_attn_gain[0], grad_ff_gain[0], query_gain_sum, key_gain_sum]).reshape(-1, lanes)
-    gain_sums = gain_sums + dp_swap(gain_sums)
-    gain_sums = gain_sums + y_swap(gain_sums)
     gain_total = gain_sums
     for step in range(1, zsize):
         gain_total = gain_total + z_pass(gain_sums, step)

time: 676 us -> 666 us (0.985)
  Pallas kernels: 207 us -> 217 us
  starting transfers between devices: 52.6 us -> 42.6 us
  other arithmetic: 34.6 us -> 26.6 us
  waiting for transfers between devices: 290 us -> 282 us
    ppermute x15, waiting for transfers between devices: 95.7 us -> 51.9 us  [z_pass(): return lax.ppermute(values, 'ctx', pairs_of)]
    ppermute x5 -> x7, waiting for transfers between devices: 45.4 us -> 63.4 us  [y_swap(): return lax.ppermute(values, 'ctx', [(i, i ^ 1) for i in range(ring)])]
    pallas_call x6 -> x8, Pallas kernels: 56.3 us -> 68.8 us  [weight_grad(): pl.pallas_call(partial(weight_grad_kernel, pieces=pieces, block=block), g...]
    ppermute x15, starting transfers between devices: 25.7 us -> 17.6 us  [z_pass(): return lax.ppermute(values, 'ctx', pairs_of)]
    unnamed x129 -> x137, local copies, waits for them, and re-layouts: 21.1 us -> 29.1 us
  transfers between devices with their start and end apart: 43 -> 45, of which waited for: 21 -> 21; matrix products, arithmetic and copies ran while one was open for 13% -> 11% of each run, Pallas kernels for 30% -> 29%
where the time goes in v3:
time: 666 us; the launch traced here: 656 us
  waiting for transfers between devices  282 us (42%)
  Pallas kernels  217 us (33%)
  local copies, waits for them, and re-layouts  45.2 us (7%)
  starting transfers between devices  42.6 us (6%)
  matrix products  26.8 us (4%)
  other arithmetic  26.6 us (4%)
  between operations  16.2 us (2%)
    ppermute x10, waiting for transfers between devices, tp_swap(): return lax.ppermute(values, 'tp', [(0, 1), (1, 0)])  73.7 us
    pallas_call x8, Pallas kernels, weight_grad(): pl.pallas_call(partial(weight_grad_kernel, pieces=pieces, block=block), g...  68.8 us
    ppermute x7, waiting for transfers between devices, y_swap(): return lax.ppermute(values, 'ctx', [(i, i ^ 1) for i in range(ring)])  63.4 us
    all_gather x1, waiting for transfers between devices, on_device(): lax.all_gather(jnp.concatenate([query_weight, key_value_weight, output_we...  55.5 us
    ppermute x15, waiting for transfers between devices, z_pass(): return lax.ppermute(values, 'ctx', pairs_of)  51.9 us
    pallas_call x3, Pallas kernels, matmul_nt(): pl.pallas_call(matmul_nt_kernel, grid=(wide // tile,), in_specs=[pl.Block...  34 us
    pallas_call x1, Pallas kernels, attention_backward(): pl.pallas_call(partial(attn_back_kernel, prompt_here=prompt_here, chunk=c...  31.4 us
    all_gather x1, waiting for transfers between devices, on_device(): lax.all_gather(jnp.concatenate([interleaved(gate_weight, up_weight), down...  30.8 us
  transfers between devices with their start and end apart: 45, of which 21 were waited for; matrix products, arithmetic and copies ran while one was open for 11% of the time, Pallas kernels for 29%

profile of v3, /device:TPU:9, one launch (start us, length us, event | category | flops | bytes accessed | tf_op | source)
XLA Modules:
  0.0 656.0 jit_solution(11331972949370004446)
XLA Ops:
  24.1 55.5 %all-gather.3.cloned.1.call-done = bf16[2048,1664]{0,1:T(8,128)(2,1)} async-done(((bf16[128,1664]{0,1:T(8,128)(2,1)}), bf16[2048,1664]{0,1:T(8,128)(2,1)}) %all-gather.3.cloned.1.call-update) | async-done | bytes 6815760 | tf_op jit(solution)/shard_map/all_gather | solution.py:685
  82.5 5.5 fusion.3.raw_ref
  99.8 5.2 collective-permute-done.1
  109.7 9.1 %collective-permute-done.3 = bf16[512,384]{1,0:T(8,128)(2,1)S(1)} collective-permute-done((bf16[512,384]{1,0:T(8,128)(2,1)S(1)}, bf16[512,384]{1,0:T(8,128)(2,1)S(1)}, u32[]{:S(2)}, u32[]{:S(2)}) %collective-permute-start.3) | collective-permute-done | bytes 393248 | tf_op jit(solution)/shard_map/ppermute | solution.py:663
  119.0 18.7 %attention_forward.1 = (bf16[640,640]{1,0:T(8,128)(2,1)S(1)}, f32[640,640]{1,0:T(8,128)S(1)}) custom-call(s32[5]{0:T(128)S(1)} %fusion.26.slot_ref, bf16[640,1024]{1,0:T(8,128)(2,1)S(1)} %head_prep.1.query_ref, bf16[1536,384]{1,0:T(8,128)(2,1)S(1)} %slice_dynamic-update-slice_fusion.keys_ref, f32[128,1024]{1,0:T(8,128)S(1)} %compare_convert_fusion.1.mask_ref), custom_call_target="tpu_custom_call" | custom-call | flops 2457600000 | bytes 2457600 | tf_op jit(solution)/shard_map/attention_forward/pallas_call | solution.py:199
  147.6 53.2 %collective-permute-done.5 = bf16[640,2048]{1,0:T(8,128)(2,1)S(1)} collective-permute-done((bf16[640,2048]{1,0:T(8,128)(2,1)S(1)}, bf16[640,2048]{1,0:T(8,128)(2,1)S(1)}, u32[]{:S(2)}, u32[]{:S(2)}) %collective-permute-start.5) | collective-permute-done | bytes 2621472 | tf_op jit(solution)/shard_map/ppermute | solution.py:669
  210.4 4.8 collective-permute-done.9.other_ref
  217.7 30.8 %all-gather.5.cloned.1.call-done.weight_ref.right_ref = bf16[2048,7680]{1,0:T(8,128)(2,1)} async-done(((bf16[128,7680]{1,0:T(8,128)(2,1)}), bf16[2048,7680]{1,0:T(8,128)(2,1)}) %all-gather.5.cloned.1.call-update) | async-done | bytes 31457296 | tf_op jit(solution)/shard_map/all_gather | solution.py:691
  250.2 20.1 %ff_forward.1 = (bf16[640,2560]{1,0:T(8,128)(2,1)S(1)}, bf16[640,2560]{1,0:T(8,128)(2,1)}, bf16[640,2560]{1,0:T(8,128)(2,1)}) custom-call(bf16[640,2048]{1,0:T(8,128)(2,1)S(1)} %copy-done.3, bf16[2048,7680]{1,0:T(8,128)(2,1)} %all-gather.5.cloned.1.call-done.weight_ref.right_ref), custom_call_target="tpu_custom_call" | custom-call | flops 3355443200 | bytes 5242880 | tf_op jit(solution)/shard_map/ff_forward/pallas_call | solution.py:383
  273.5 14.0 %ff_backward.1.left_ref.own_ref = bf16[640,5120]{1,0:T(8,128)(2,1)} custom-call(bf16[640,2048]{1,0:T(8,128)(2,1)S(1)} %constant_dynamic-update-slice_fusion.7.grad_ref.left_own_ref.refs_4_, bf16[2048,7680]{1,0:T(8,128)(2,1)} %all-gather.5.cloned.1.call-done.weight_ref.right_ref, bf16[640,2560]{1,0:T(8,128)(2,1)S(1)} %copy-done.18, ...), custom_call_target="tpu_custom_call" | custom-call | flops 1677721600 | bytes 2621440 | tf_op jit(solution)/shard_map/ff_backward/pallas_call | solution.py:509
  289.6 8.4 %weight_grad.8 = bf16[4,128,2560]{2,1,0:T(8,128)(2,1)S(1)} custom-call(s32[5]{0:T(128)S(1)} %pad_add_fusion.2.index_ref, bf16[640,2048]{1,0:T(8,128)(2,1)S(1)} %constant_dynamic-update-slice_fusion.7.grad_ref.left_own_ref.refs_4_, bf16[640,2048]{1,0:T(8,128)(2,1)} %copy-done.44, bf16[640,2560]{1,0:T(8,128)(2,1)} %copy-done.5, bf16[640,2560]{1,0:T(8,128)(2,1)} %copy-done.42), custom_call_target="tpu_custom_call" | custom-call | flops 838860800 | bytes 2293760 | tf_op jit(solution)/shard_map/weight_grad/pallas_call | solution.py:561
  298.9 11.5 %matmul_nt.3.refs_0_ = bf16[640,1024]{1,0:T(8,128)(2,1)S(1)} custom-call(bf16[640,5120]{1,0:T(8,128)(2,1)} %ff_backward.1.left_ref.own_ref, bf16[2048,7680]{1,0:T(8,128)(2,1)} %all-gather.5.cloned.1.call-done.weight_ref.right_ref), custom_call_target="tpu_custom_call" | custom-call | flops 1677721600 | bytes 2621440 | tf_op jit(solution)/shard_map/matmul_nt/pallas_call | solution.py:405
  311.7 11.7 %matmul_nt.4.refs_2_ = bf16[640,1024]{1,0:T(8,128)(2,1)S(1)} custom-call(bf16[640,5120]{1,0:T(8,128)(2,1)} %ff_backward.1.left_ref.own_ref, bf16[2048,7680]{1,0:T(8,128)(2,1)} %all-gather.5.cloned.1.call-done.weight_ref.right_ref), custom_call_target="tpu_custom_call" | custom-call | flops 1677721600 | bytes 2621440 | tf_op jit(solution)/shard_map/matmul_nt/pallas_call | solution.py:405
  323.9 15.1 %weight_grad.9 = bf16[4,128,5120]{2,1,0:T(8,128)(2,1)} custom-call(s32[5]{0:T(128)S(1)} %pad_add_fusion.2.index_ref, bf16[640,2048]{1,0:T(8,128)(2,1)S(1)} %copy-done.4, bf16[640,2048]{1,0:T(8,128)(2,1)S(1)} %copy-done.14, bf16[640,5120]{1,0:T(8,128)(2,1)} %ff_backward.1.left_ref.own_ref, bf16[640,5120]{1,0:T(8,128)(2,1)} %collective-permute-done.12.other_ref), custom_call_target="tpu_custom_call" | custom-call | flops 1677721600 | bytes 4587520 | tf_op jit(solution)/shard_map/weight_grad/pallas_call | solution.py:561
  340.5 10.8 %matmul_nt.5 = bf16[640,2048]{1,0:T(8,128)(2,1)S(1)} custom-call(bf16[640,2560]{1,0:T(8,128)(2,1)S(1)} %copy-done.6, bf16[2048,7680]{1,0:T(8,128)(2,1)} %all-gather.5.cloned.1.call-done.weight_ref.right_ref), custom_call_target="tpu_custom_call" | custom-call | flops 1677721600 | bytes 2621440 | tf_op jit(solution)/shard_map/matmul_nt/pallas_call | solution.py:405
  352.7 15.8 %collective-permute-done.13.refs_3_ = bf16[640,1024]{1,0:T(8,128)(2,1)} collective-permute-done((bf16[640,1024]{1,0:T(8,128)(2,1)S(1)}, bf16[640,1024]{1,0:T(8,128)(2,1)}, u32[]{:S(2)}, u32[]{:S(2)}) %collective-permute-start.13) | collective-permute-done | bytes 1310752 | tf_op jit(solution)/shard_map/ppermute | solution.py:669
  368.5 6.9 %norm_backward.2 = (bf16[640,2048]{1,0:T(8,128)(2,1)}, f32[1,2048]{1,0:T(1,128)S(1)}) custom-call(bf16[640,1024]{1,0:T(8,128)(2,1)S(1)} %matmul_nt.3.refs_0_, bf16[640,1024]{1,0:T(8,128)(2,1)S(1)} %collective-permute-done.11.refs_1_, bf16[640,1024]{1,0:T(8,128)(2,1)S(1)} %matmul_nt.4.refs_2_, bf16[640,1024]{1,0:T(8,128)(2,1)} %collective-permute-done.13.refs_3_, ...), custom_call_target="tpu_custom_call" | custom-call | flops 6553600 | bytes 3932160 | tf_op jit(solution)/shard_map/norm_backward/pallas_call | solution.py:486
  375.4 5.8 fusion.8.grad_ref
  381.2 8.9 %weight_grad.10 = bf16[4,128,2560]{2,1,0:T(8,128)(2,1)S(1)} custom-call(s32[5]{0:T(128)S(1)} %pad_add_fusion.3.index_ref, bf16[640,2048]{1,0:T(8,128)(2,1)S(1)} %copy-done.1, bf16[640,2048]{1,0:T(8,128)(2,1)} %copy-done.44, bf16[640,2560]{1,0:T(8,128)(2,1)} %copy-done.5, bf16[640,2560]{1,0:T(8,128)(2,1)} %copy-done.42, ...), custom_call_target="tpu_custom_call" | custom-call | flops 838860800 | bytes 2293760 | tf_op jit(solution)/shard_map/weight_grad/pallas_call | solution.py:561
  398.1 31.4 %attention_backward.1 = (f32[640,640]{1,0:T(8,128)}, f32[1536,384]{1,0:T(8,128)}) custom-call(s32[5]{0:T(128)S(1)} %fusion.26.slot_ref, bf16[640,1024]{1,0:T(8,128)(2,1)S(1)} %copy-done.27, bf16[1536,384]{1,0:T(8,128)(2,1)S(1)} %copy-done.37, f32[1024,128]{1,0:T(8,128)S(1)} %compare_convert_fusion.mask_ref, bf16[640,640]{1,0:T(8,128)(2,1)S(1)} %copy-done.20, ...), custom_call_target="tpu_custom_call" | custom-call | flops 6144000000 | bytes 2457600 | tf_op jit(solution)/shard_map/attention_backward/pallas_call | solution.py:333
  444.4 32.6 %collective-permute-done.15 = bf16[512,384]{1,0:T(8,128)(2,1)S(1)} collective-permute-done((bf16[512,384]{1,0:T(8,128)(2,1)S(1)}, bf16[512,384]{1,0:T(8,128)(2,1)S(1)}, u32[]{:S(2)}, u32[]{:S(2)}) %collective-permute-start.15) | collective-permute-done | bytes 393248 | tf_op jit(solution)/shard_map/ppermute | solution.py:663
  483.2 5.8 collective-permute-done.22
  490.1 16.1 %weight_grad.15 = bf16[4,128,5120]{2,1,0:T(8,128)(2,1)} custom-call(s32[5]{0:T(128)S(1)} %pad_add_fusion.3.index_ref, bf16[640,2048]{1,0:T(8,128)(2,1)S(1)} %copy-done.4, bf16[640,2048]{1,0:T(8,128)(2,1)S(1)} %copy-done.15, bf16[640,5120]{1,0:T(8,128)(2,1)} %ff_backward.1.left_ref.own_ref, bf16[640,5120]{1,0:T(8,128)(2,1)} %collective-permute-done.12.other_ref, ...), custom_call_target="tpu_custom_call" | custom-call | flops 1677721600 | bytes 4587520 | tf_op jit(solution)/shard_map/weight_grad/pallas_call | solution.py:561
  508.2 5.2 weight_grad.11
  521.7 5.6 weight_grad.12
  530.6 21.7 %collective-permute-done.26.rest_0_ = bf16[4,128,1024]{2,1,0:T(8,128)(2,1)} collective-permute-done((bf16[4,128,1024]{2,1,0:T(8,128)(2,1)}, bf16[4,128,1024]{2,1,0:T(8,128)(2,1)}, u32[]{:S(2)}, u32[]{:S(2)}) %collective-permute-start.26) | collective-permute-done | bytes 1048608 | tf_op jit(solution)/shard_map/ppermute | solution.py:663
  552.3 5.1 weight_grad.13
  560.3 4.9 convolution_convert_fusion.refs_4_
  565.2 8.3 %norm_backward.3 = (bf16[640,2048]{1,0:T(8,128)(2,1)}, f32[1,2048]{1,0:T(1,128)S(1)}) custom-call(bf16[640,1024]{1,0:T(8,128)(2,1)S(1)} %copy-done.30, bf16[640,1024]{1,0:T(8,128)(2,1)S(1)} %copy-done.32, bf16[640,1024]{1,0:T(8,128)(2,1)} %convolution_convert_fusion.2.refs_2_, bf16[640,1024]{1,0:T(8,128)(2,1)} %collective-permute-done.23.refs_3_, ...), custom_call_target="tpu_custom_call" | custom-call | flops 6553600 | bytes 3932160 | tf_op jit(solution)/shard_map/norm_backward/pallas_call | solution.py:486
  580.0 4.3 weight_grad.14
  603.7 26.3 %collective-permute-done.32 = bf16[128,1024]{1,0:T(8,128)(2,1)S(1)} collective-permute-done((bf16[128,1024]{1,0:T(8,128)(2,1)S(1)}, bf16[128,1024]{1,0:T(8,128)(2,1)S(1)}, u32[]{:S(2)}, u32[]{:S(2)}) %collective-permute-start.32) | collective-permute-done | bytes 262176 | tf_op jit(solution)/shard_map/ppermute | solution.py:660
  630.0 5.6 collective-permute-done.33
  (313 shorter events, 155.0 us)
Async XLA Ops:
  7.2 72.4 %all-gather.3.cloned.1.call-start = ((), (), s32[]{:S(2)}) async-start(), calls=%async_computation.2 | async-start | bytes 7241728 | tf_op jit(solution)/shard_map/all_gather | solution.py:685
  11.0 237.5 %all-gather.5.cloned.1.call-start = ((), (), s32[]{:S(2)}) async-start(), calls=%async_computation.3 | async-start | bytes 33423360 | tf_op jit(solution)/shard_map/all_gather | solution.py:691
  16.9 585.5 %reduce-scatter.5.cloned.1.call-start = ((), (), s32[]{:S(2)}) async-start(), calls=%async_computation.5 | async-start | bytes 3276800 | tf_op jit(solution)/shard_map/reduce_scatter | solution.py:777
  81.2 56.5 %collective-permute-start.4 = (bf16[2048,384]{0,1:T(8,128)(2,1)S(1)}, bf16[2048,384]{0,1:T(8,128)(2,1)S(1)}, u32[]{:S(2)}, u32[]{:S(2)}) collective-permute-start(bf16[2048,384]{0,1:T(8,128)(2,1)S(1)} %slice.176), channel_id=1, source_target_pairs={{0,1},{1,0},{2,3},{3,2},{4,5},{5,4},{6,7},{7,6},{8,9},{9,8},{10,11... | collective-permute-start | bytes 4718600 | tf_op jit(solution)/shard_map/ppermute | solution.py:669
  94.5 10.5 %collective-permute-start.1 = (bf16[128,384]{1,0:T(8,128)(2,1)S(1)}, bf16[128,384]{1,0:T(8,128)(2,1)S(1)}, u32[]{:S(2)}, u32[]{:S(2)}) collective-permute-start(bf16[128,384]{1,0:T(8,128)(2,1)S(1)} %get-tuple-element.186), channel_id=1, source_target_pairs={{0,8},{2,10},{4,12},{6,14},{8,0},{10,2},{12,4},{14,6},{1,9},{3,11}... | collective-permute-start | bytes 294920 | tf_op jit(solution)/shard_map/ppermute | solution.py:660
  95.7 13.6 %collective-permute-start.2 = (bf16[128,384]{1,0:T(8,128)(2,1)S(1)}, bf16[128,384]{1,0:T(8,128)(2,1)S(1)}, u32[]{:S(2)}, u32[]{:S(2)}) collective-permute-start(bf16[128,384]{1,0:T(8,128)(2,1)S(1)} %get-tuple-element.186), channel_id=1, source_target_pairs={{0,4},{2,6},{4,8},{6,10},{8,12},{10,14},{12,0},{14,2},{1,5},{3,7},... | collective-permute-start | bytes 294920 | tf_op jit(solution)/shard_map/ppermute | solution.py:660
  144.3 56.4 %collective-permute-start.5 = (bf16[640,2048]{1,0:T(8,128)(2,1)S(1)}, bf16[640,2048]{1,0:T(8,128)(2,1)S(1)}, u32[]{:S(2)}, u32[]{:S(2)}) collective-permute-start(bf16[640,2048]{1,0:T(8,128)(2,1)S(1)} %convolution_convert_fusion.1), channel_id=1, source_target_pairs={{0,1},{1,0},{2,3},{3,2},{4,5},{5,4},{6,7},{7,6},{8,9},{9,8},{10,11... | collective-permute-start | bytes 7864328 | tf_op jit(solution)/shard_map/ppermute | solution.py:669
  144.6 65.8 %collective-permute-start.8 = (bf16[640,2048]{1,0:T(8,128)(2,1)}, bf16[640,2048]{1,0:T(8,128)(2,1)S(1)}, u32[]{:S(2)}, u32[]{:S(2)}) collective-permute-start(bf16[640,2048]{1,0:T(8,128)(2,1)} %fusion.2.left_own_ref), channel_id=1, source_target_pairs={{0,16},{16,0},{1,17},{17,1},{2,18},{18,2},{3,19},{19,3},{4,20},{20... | collective-permute-start | bytes 7864328 | tf_op jit(solution)/shard_map/ppermute | solution.py:666
  147.5 62.9 %collective-permute-start.7 = (bf16[640,2048]{1,0:T(8,128)(2,1)S(1)}, bf16[640,2048]{1,0:T(8,128)(2,1)S(1)}, u32[]{:S(2)}, u32[]{:S(2)}) collective-permute-start(bf16[640,2048]{1,0:T(8,128)(2,1)S(1)} %constant_dynamic-update-slice_fusion.7.grad_ref.left_own_ref.refs_4_), channel_id=1, source_target_pairs={{0,16},{16,0},{1,17},{17,1},{2,18},{18,2},{3,19},{19,3},{4,20},{20... | collective-permute-start | bytes 7864328 | tf_op jit(solution)/shard_map/ppermute | solution.py:666
  270.4 17.1 %collective-permute-start.10 = (bf16[640,2560]{1,0:T(8,128)(2,1)S(1)}, bf16[640,2560]{1,0:T(8,128)(2,1)S(1)}, u32[]{:S(2)}, u32[]{:S(2)}) collective-permute-start(bf16[640,2560]{1,0:T(8,128)(2,1)S(1)} %get-tuple-element.93.own_ref.left_ref), channel_id=1, source_target_pairs={{0,16},{16,0},{1,17},{17,1},{2,18},{18,2},{3,19},{19,3},{4,20},{20... | collective-permute-start | bytes 9830408 | tf_op jit(solution)/shard_map/ppermute | solution.py:666
  289.3 34.6 %collective-permute-start.12 = (bf16[640,5120]{1,0:T(8,128)(2,1)}, bf16[640,5120]{1,0:T(8,128)(2,1)}, u32[]{:S(2)}, u32[]{:S(2)}) collective-permute-start(bf16[640,5120]{1,0:T(8,128)(2,1)} %ff_backward.1.left_ref.own_ref), channel_id=1, source_target_pairs={{0,16},{16,0},{1,17},{17,1},{2,18},{18,2},{3,19},{19,3},{4,20},{20... | collective-permute-start | bytes 19660808 | tf_op jit(solution)/shard_map/ppermute | solution.py:666
  298.0 83.3 %collective-permute-start.14 = (bf16[4,128,2560]{2,1,0:T(8,128)(2,1)S(1)}, bf16[4,128,2560]{2,1,0:T(8,128)(2,1)}, u32[]{:S(2)}, u32[]{:S(2)}) collective-permute-start(bf16[4,128,2560]{2,1,0:T(8,128)(2,1)S(1)} %weight_grad.8), channel_id=1, source_target_pairs={{0,2},{2,0},{4,6},{6,4},{8,10},{10,8},{12,14},{14,12},{1,3},{3,1},... | collective-permute-start | bytes 7864328 | tf_op jit(solution)/shard_map/ppermute | solution.py:663
  310.5 30.0 %collective-permute-start.11 = (bf16[640,1024]{1,0:T(8,128)(2,1)S(1)}, bf16[640,1024]{1,0:T(8,128)(2,1)S(1)}, u32[]{:S(2)}, u32[]{:S(2)}) collective-permute-start(bf16[640,1024]{1,0:T(8,128)(2,1)S(1)} %matmul_nt.3.refs_0_), channel_id=1, source_target_pairs={{0,1},{1,0},{2,3},{3,2},{4,5},{5,4},{6,7},{7,6},{8,9},{9,8},{10,11... | collective-permute-start | bytes 3932168 | tf_op jit(solution)/shard_map/ppermute | solution.py:669
  323.4 45.1 %collective-permute-start.13 = (bf16[640,1024]{1,0:T(8,128)(2,1)S(1)}, bf16[640,1024]{1,0:T(8,128)(2,1)}, u32[]{:S(2)}, u32[]{:S(2)}) collective-permute-start(bf16[640,1024]{1,0:T(8,128)(2,1)S(1)} %matmul_nt.4.refs_2_), channel_id=1, source_target_pairs={{0,1},{1,0},{2,3},{3,2},{4,5},{5,4},{6,7},{7,6},{8,9},{9,8},{10,11... | collective-permute-start | bytes 3932168 | tf_op jit(solution)/shard_map/ppermute | solution.py:669
  339.0 151.1 %collective-permute-start.40 = (bf16[4,128,5120]{2,1,0:T(8,128)(2,1)}, bf16[4,128,5120]{2,1,0:T(8,128)(2,1)}, u32[]{:S(2)}, u32[]{:S(2)}) collective-permute-start(bf16[4,128,5120]{2,1,0:T(8,128)(2,1)} %weight_grad.9), channel_id=1, source_target_pairs={{0,2},{2,0},{4,6},{6,4},{8,10},{10,8},{12,14},{14,12},{1,3},{3,1},... | collective-permute-start | bytes 15728648 | tf_op jit(solution)/shard_map/ppermute | solution.py:663
  391.7 252.3 %reduce-scatter.3.cloned.1.call-start = ((), (), s32[]{:S(2)}) async-start(), calls=%async_computation.4 | async-start | bytes 6553600 | tf_op jit(solution)/shard_map/reduce_scatter | solution.py:777
  391.7 85.3 %collective-permute-start.16 = (bf16[640,2048]{1,0:T(8,128)(2,1)}, bf16[640,2048]{1,0:T(8,128)(2,1)S(1)}, u32[]{:S(2)}, u32[]{:S(2)}) collective-permute-start(bf16[640,2048]{1,0:T(8,128)(2,1)} %copy-done.10), channel_id=1, source_target_pairs={{0,1},{1,0},{2,3},{3,2},{4,5},{5,4},{6,7},{7,6},{8,9},{9,8},{10,11... | collective-permute-start | bytes 7864328 | tf_op jit(solution)/shard_map/ppermute | solution.py:669
  437.6 51.4 %collective-permute-start.19 = (bf16[640,1024]{1,0:T(8,128)(2,1)S(1)}, bf16[640,1024]{1,0:T(8,128)(2,1)S(1)}, u32[]{:S(2)}, u32[]{:S(2)}) collective-permute-start(bf16[640,1024]{1,0:T(8,128)(2,1)S(1)} %convolution_convert_fusion.3.refs_0_), channel_id=1, source_target_pairs={{0,1},{1,0},{2,3},{3,2},{4,5},{5,4},{6,7},{7,6},{8,9},{9,8},{10,11... | collective-permute-start | bytes 3932168 | tf_op jit(solution)/shard_map/ppermute | solution.py:669
  437.9 39.1 %collective-permute-start.15 = (bf16[512,384]{1,0:T(8,128)(2,1)S(1)}, bf16[512,384]{1,0:T(8,128)(2,1)S(1)}, u32[]{:S(2)}, u32[]{:S(2)}) collective-permute-start(bf16[512,384]{1,0:T(8,128)(2,1)S(1)} %slice.178), channel_id=1, source_target_pairs={{0,2},{2,0},{4,6},{6,4},{8,10},{10,8},{12,14},{14,12},{1,3},{3,1},... | collective-permute-start | bytes 1179656 | tf_op jit(solution)/shard_map/ppermute | solution.py:663
  438.6 69.3 %collective-permute-start.17 = (bf16[640,2048]{1,0:T(8,128)(2,1)}, bf16[640,2048]{1,0:T(8,128)(2,1)}, u32[]{:S(2)}, u32[]{:S(2)}) collective-permute-start(bf16[640,2048]{1,0:T(8,128)(2,1)} %get-tuple-element.100.left_own_ref.refs_5_), channel_id=1, source_target_pairs={{0,16},{16,0},{1,17},{17,1},{2,18},{18,2},{3,19},{19,3},{4,20},{20... | collective-permute-start | bytes 7864328 | tf_op jit(solution)/shard_map/ppermute | solution.py:666
  519.1 38.3 %collective-permute-start.23 = (bf16[640,1024]{1,0:T(8,128)(2,1)}, bf16[640,1024]{1,0:T(8,128)(2,1)}, u32[]{:S(2)}, u32[]{:S(2)}) collective-permute-start(bf16[640,1024]{1,0:T(8,128)(2,1)} %convolution_convert_fusion.2.refs_2_), channel_id=1, source_target_pairs={{0,1},{1,0},{2,3},{3,2},{4,5},{5,4},{6,7},{7,6},{8,9},{9,8},{10,11... | collective-permute-start | bytes 3932168 | tf_op jit(solution)/shard_map/ppermute | solution.py:669
  527.4 24.9 %collective-permute-start.26 = (bf16[4,128,1024]{2,1,0:T(8,128)(2,1)}, bf16[4,128,1024]{2,1,0:T(8,128)(2,1)}, u32[]{:S(2)}, u32[]{:S(2)}) collective-permute-start(bf16[4,128,1024]{2,1,0:T(8,128)(2,1)} %weight_grad.12), channel_id=1, source_target_pairs={{0,2},{2,0},{4,6},{6,4},{8,10},{10,8},{12,14},{14,12},{1,3},{3,1},... | collective-permute-start | bytes 3145736 | tf_op jit(solution)/shard_map/ppermute | solution.py:663
  528.9 31.4 %collective-permute-start.24 = (bf16[640,384]{1,0:T(8,128)(2,1)}, bf16[640,384]{1,0:T(8,128)(2,1)}, u32[]{:S(2)}, u32[]{:S(2)}) collective-permute-start(bf16[640,384]{1,0:T(8,128)(2,1)} %get-tuple-element.118), channel_id=1, source_target_pairs={{0,1},{1,0},{2,3},{3,2},{4,5},{5,4},{6,7},{7,6},{8,9},{9,8},{10,11... | collective-permute-start | bytes 1474568 | tf_op jit(solution)/shard_map/ppermute | solution.py:669
  530.3 43.2 %collective-permute-start.18 = (bf16[4,128,640]{2,1,0:T(8,128)(2,1)}, bf16[4,128,640]{2,1,0:T(8,128)(2,1)}, u32[]{:S(2)}, u32[]{:S(2)}) collective-permute-start(bf16[4,128,640]{2,1,0:T(8,128)(2,1)} %weight_grad.11), channel_id=1, source_target_pairs={{0,2},{2,0},{4,6},{6,4},{8,10},{10,8},{12,14},{14,12},{1,3},{3,1},... | collective-permute-start | bytes 1966088 | tf_op jit(solution)/shard_map/ppermute | solution.py:663
  584.4 13.1 %collective-permute-start.29 = (f32[33,128]{1,0:T(8,128)S(1)}, f32[33,128]{1,0:T(8,128)S(1)}, u32[]{:S(2)}, u32[]{:S(2)}) collective-permute-start(f32[33,128]{1,0:T(8,128)S(1)} %fusion.40), channel_id=1, source_target_pairs={{0,4},{2,6},{4,8},{6,10},{8,12},{10,14},{12,0},{14,2},{1,5},{3,7},... | collective-permute-start | bytes 50696 | tf_op jit(solution)/shard_map/ppermute | solution.py:660
  586.2 11.3 %collective-permute-start.30 = (f32[33,128]{1,0:T(8,128)S(1)}, f32[33,128]{1,0:T(8,128)S(1)}, u32[]{:S(2)}, u32[]{:S(2)}) collective-permute-start(f32[33,128]{1,0:T(8,128)S(1)} %fusion.40), channel_id=1, source_target_pairs={{0,8},{2,10},{4,12},{6,14},{8,0},{10,2},{12,4},{14,6},{1,9},{3,11}... | collective-permute-start | bytes 50696 | tf_op jit(solution)/shard_map/ppermute | solution.py:660
  586.4 11.4 %collective-permute-start.31 = (f32[33,128]{1,0:T(8,128)S(1)}, f32[33,128]{1,0:T(8,128)S(1)}, u32[]{:S(2)}, u32[]{:S(2)}) collective-permute-start(f32[33,128]{1,0:T(8,128)S(1)} %fusion.40), channel_id=1, source_target_pairs={{0,12},{2,14},{4,0},{6,2},{8,4},{10,6},{12,8},{14,10},{1,13},{3,15... | collective-permute-start | bytes 50696 | tf_op jit(solution)/shard_map/ppermute | solution.py:660
  593.1 44.8 %collective-permute-start.37 = (bf16[128,640]{1,0:T(8,128)(2,1)}, bf16[128,640]{1,0:T(8,128)(2,1)}, u32[]{:S(2)}, u32[]{:S(2)}) collective-permute-start(bf16[128,640]{1,0:T(8,128)(2,1)} %get-tuple-element.193), channel_id=1, source_target_pairs={{0,4},{2,6},{4,8},{6,10},{8,12},{10,14},{12,0},{14,2},{1,5},{3,7},... | collective-permute-start | bytes 491528 | tf_op jit(solution)/shard_map/ppermute | solution.py:660
  593.6 44.4 %collective-permute-start.38 = (bf16[128,640]{1,0:T(8,128)(2,1)}, bf16[128,640]{1,0:T(8,128)(2,1)}, u32[]{:S(2)}, u32[]{:S(2)}) collective-permute-start(bf16[128,640]{1,0:T(8,128)(2,1)} %get-tuple-element.195), channel_id=1, source_target_pairs={{0,8},{2,10},{4,12},{6,14},{8,0},{10,2},{12,4},{14,6},{1,9},{3,11}... | collective-permute-start | bytes 491528 | tf_op jit(solution)/shard_map/ppermute | solution.py:660
  597.5 32.5 %collective-permute-start.32 = (bf16[128,1024]{1,0:T(8,128)(2,1)S(1)}, bf16[128,1024]{1,0:T(8,128)(2,1)S(1)}, u32[]{:S(2)}, u32[]{:S(2)}) collective-permute-start(bf16[128,1024]{1,0:T(8,128)(2,1)S(1)} %get-tuple-element.190), channel_id=1, source_target_pairs={{0,4},{2,6},{4,8},{6,10},{8,12},{10,14},{12,0},{14,2},{1,5},{3,7},... | collective-permute-start | bytes 786440 | tf_op jit(solution)/shard_map/ppermute | solution.py:660
  597.5 38.1 %collective-permute-start.33 = (bf16[128,1024]{1,0:T(8,128)(2,1)S(1)}, bf16[128,1024]{1,0:T(8,128)(2,1)S(1)}, u32[]{:S(2)}, u32[]{:S(2)}) collective-permute-start(bf16[128,1024]{1,0:T(8,128)(2,1)S(1)} %get-tuple-element.189), channel_id=1, source_target_pairs={{0,8},{2,10},{4,12},{6,14},{8,0},{10,2},{12,4},{14,6},{1,9},{3,11}... | collective-permute-start | bytes 786440 | tf_op jit(solution)/shard_map/ppermute | solution.py:660
  600.7 34.9 %collective-permute-start.34 = (bf16[128,1024]{1,0:T(8,128)(2,1)S(1)}, bf16[128,1024]{1,0:T(8,128)(2,1)S(1)}, u32[]{:S(2)}, u32[]{:S(2)}) collective-permute-start(bf16[128,1024]{1,0:T(8,128)(2,1)S(1)} %get-tuple-element.188), channel_id=1, source_target_pairs={{0,12},{2,14},{4,0},{6,2},{8,4},{10,6},{12,8},{14,10},{1,13},{3,15... | collective-permute-start | bytes 786440 | tf_op jit(solution)/shard_map/ppermute | solution.py:660
  (75 other events, 787.6 us)
Sparse Core Ops, SparseCore 0:
  11.1 68.4 all-gather.2
  81.8 166.6 all-gather.4
  391.8 52.1 reduce-scatter.4
  506.4 116.5 reduce-scatter.2

commit v4 on v3

--- a/solution.py
+++ b/solution.py
@@ -871,7 +871,7 @@
     )
     qkv_pieces = [z_pass(qkv_kept[step], step) for step in range(1, zsize)]
     out_received, grad_input = after((y_swap(out_sent), grad_input))
-    gain_gate, qkv_pieces = after((grad_input, qkv_pieces))
+    out_received, qkv_pieces = after((out_received, qkv_pieces))
     ff_part, ff_part_other, resid_out = after((ff_part, ff_part_other, resid, grad_input))[:3]
     output = (resid_out.astype(f32) + (ff_part.astype(f32) + ff_part_other.astype(f32))).astype(bf16)
     query_gain_sum = jnp.sum(query_gain_parts.reshape(-1, head_size), axis=0)

time: 666 us -> 668 us (level)
  Pallas kernels: 217 us -> 226 us
  waiting for transfers between devices: 282 us -> 274 us
    pallas_call x3, Pallas kernels: 34 us -> 45.2 us  [matmul_nt(): pl.pallas_call(matmul_nt_kernel, grid=(wide // tile,), in_specs=[pl.Block...]
    ppermute x7, waiting for transfers between devices: 63.4 us -> 52.5 us  [y_swap(): return lax.ppermute(values, 'ctx', [(i, i ^ 1) for i in range(ring)])]
    unnamed x137 -> x139, local copies, waits for them, and re-layouts: 29.1 us -> 29.5 us
  transfers between devices with their start and end apart: 45 -> 45, of which waited for: 21 -> 24; matrix products, arithmetic and copies ran while one was open for 11% -> 11% of each run, Pallas kernels for 29% -> 31%
where the time goes in v4:
time: 668 us; the launch traced here: 660 us
  waiting for transfers between devices  274 us (41%)
  Pallas kernels  226 us (34%)
  local copies, waits for them, and re-layouts  47.2 us (7%)
  starting transfers between devices  43 us (6%)
  other arithmetic  27.6 us (4%)
  matrix products  25.8 us (4%)
  between operations  16 us (2%)
    ppermute x10, waiting for transfers between devices, tp_swap(): return lax.ppermute(values, 'tp', [(0, 1), (1, 0)])  73.8 us
    pallas_call x8, Pallas kernels, weight_grad(): pl.pallas_call(partial(weight_grad_kernel, pieces=pieces, block=block), g...  67.4 us
    ppermute x15, waiting for transfers between devices, z_pass(): return lax.ppermute(values, 'ctx', pairs_of)  56.4 us
    all_gather x1, waiting for transfers between devices, on_device(): lax.all_gather(jnp.concatenate([query_weight, key_value_weight, output_we...  54 us
    ppermute x7, waiting for transfers between devices, y_swap(): return lax.ppermute(values, 'ctx', [(i, i ^ 1) for i in range(ring)])  52.5 us
    pallas_call x3, Pallas kernels, matmul_nt(): pl.pallas_call(matmul_nt_kernel, grid=(wide // tile,), in_specs=[pl.Block...  45.2 us
    pallas_call x1, Pallas kernels, attention_backward(): pl.pallas_call(partial(attn_back_kernel, prompt_here=prompt_here, chunk=c...  31.2 us
    all_gather x1, waiting for transfers between devices, on_device(): lax.all_gather(jnp.concatenate([interleaved(gate_weight, up_weight), down...  30.2 us
  transfers between devices with their start and end apart: 45, of which 24 were waited for; matrix products, arithmetic and copies ran while one was open for 11% of the time, Pallas kernels for 31%

profile of v4, /device:TPU:9, one launch (start us, length us, event | category | flops | bytes accessed | tf_op | source)
XLA Modules:
  0.0 659.7 jit_solution(16993038017658733179)
XLA Ops:
  25.6 54.0 %all-gather.3.cloned.1.call-done = bf16[2048,1664]{0,1:T(8,128)(2,1)} async-done(((bf16[128,1664]{0,1:T(8,128)(2,1)}), bf16[2048,1664]{0,1:T(8,128)(2,1)}) %all-gather.3.cloned.1.call-update) | async-done | bytes 6815760 | tf_op jit(solution)/shard_map/all_gather | solution.py:685
  82.6 4.7 fusion.3.raw_ref
  99.0 5.2 collective-permute-done.1
  108.9 9.1 %collective-permute-done.3 = bf16[512,384]{1,0:T(8,128)(2,1)S(1)} collective-permute-done((bf16[512,384]{1,0:T(8,128)(2,1)S(1)}, bf16[512,384]{1,0:T(8,128)(2,1)S(1)}, u32[]{:S(2)}, u32[]{:S(2)}) %collective-permute-start.3) | collective-permute-done | bytes 393248 | tf_op jit(solution)/shard_map/ppermute | solution.py:663
  118.1 18.4 %attention_forward.1 = (bf16[640,640]{1,0:T(8,128)(2,1)S(1)}, f32[640,640]{1,0:T(8,128)S(1)}) custom-call(s32[5]{0:T(128)S(1)} %fusion.26.slot_ref, bf16[640,1024]{1,0:T(8,128)(2,1)S(1)} %head_prep.1.query_ref, bf16[1536,384]{1,0:T(8,128)(2,1)S(1)} %slice_dynamic-update-slice_fusion.keys_ref, f32[128,1024]{1,0:T(8,128)S(1)} %compare_convert_fusion.1.mask_ref), custom_call_target="tpu_custom_call" | custom-call | flops 2457600000 | bytes 2457600 | tf_op jit(solution)/shard_map/attention_forward/pallas_call | solution.py:199
  146.4 53.0 %collective-permute-done.5 = bf16[640,2048]{1,0:T(8,128)(2,1)S(1)} collective-permute-done((bf16[640,2048]{1,0:T(8,128)(2,1)S(1)}, bf16[640,2048]{1,0:T(8,128)(2,1)S(1)}, u32[]{:S(2)}, u32[]{:S(2)}) %collective-permute-start.5) | collective-permute-done | bytes 2621472 | tf_op jit(solution)/shard_map/ppermute | solution.py:669
  201.0 5.4 fusion.11
  211.0 4.9 collective-permute-done.9.other_ref
  218.3 30.2 %all-gather.5.cloned.1.call-done.weight_ref.right_ref = bf16[2048,7680]{1,0:T(8,128)(2,1)} async-done(((bf16[128,7680]{1,0:T(8,128)(2,1)}), bf16[2048,7680]{1,0:T(8,128)(2,1)}) %all-gather.5.cloned.1.call-update) | async-done | bytes 31457296 | tf_op jit(solution)/shard_map/all_gather | solution.py:691
  250.2 20.2 %ff_forward.1 = (bf16[640,2560]{1,0:T(8,128)(2,1)S(1)}, bf16[640,2560]{1,0:T(8,128)(2,1)}, bf16[640,2560]{1,0:T(8,128)(2,1)}) custom-call(bf16[640,2048]{1,0:T(8,128)(2,1)S(1)} %copy-done.3, bf16[2048,7680]{1,0:T(8,128)(2,1)} %all-gather.5.cloned.1.call-done.weight_ref.right_ref), custom_call_target="tpu_custom_call" | custom-call | flops 3355443200 | bytes 5242880 | tf_op jit(solution)/shard_map/ff_forward/pallas_call | solution.py:383
  273.5 14.0 %ff_backward.1.left_ref.own_ref = bf16[640,5120]{1,0:T(8,128)(2,1)} custom-call(bf16[640,2048]{1,0:T(8,128)(2,1)S(1)} %constant_dynamic-update-slice_fusion.7.grad_ref.left_own_ref.refs_4_, bf16[2048,7680]{1,0:T(8,128)(2,1)} %all-gather.5.cloned.1.call-done.weight_ref.right_ref, bf16[640,2560]{1,0:T(8,128)(2,1)S(1)} %copy-done.18, ...), custom_call_target="tpu_custom_call" | custom-call | flops 1677721600 | bytes 2621440 | tf_op jit(solution)/shard_map/ff_backward/pallas_call | solution.py:509
  289.6 8.3 %weight_grad.8 = bf16[4,128,2560]{2,1,0:T(8,128)(2,1)S(1)} custom-call(s32[5]{0:T(128)S(1)} %pad_add_fusion.2.index_ref, bf16[640,2048]{1,0:T(8,128)(2,1)S(1)} %constant_dynamic-update-slice_fusion.7.grad_ref.left_own_ref.refs_4_, bf16[640,2048]{1,0:T(8,128)(2,1)} %copy-done.46, bf16[640,2560]{1,0:T(8,128)(2,1)} %copy-done.5, bf16[640,2560]{1,0:T(8,128)(2,1)} %copy-done.44), custom_call_target="tpu_custom_call" | custom-call | flops 838860800 | bytes 2293760 | tf_op jit(solution)/shard_map/weight_grad/pallas_call | solution.py:561
  298.9 22.7 %matmul_nt.3.refs_0_ = bf16[640,1024]{1,0:T(8,128)(2,1)S(1)} custom-call(bf16[640,5120]{1,0:T(8,128)(2,1)} %ff_backward.1.left_ref.own_ref, bf16[2048,7680]{1,0:T(8,128)(2,1)} %all-gather.5.cloned.1.call-done.weight_ref.right_ref), custom_call_target="tpu_custom_call" | custom-call | flops 1677721600 | bytes 2621440 | tf_op jit(solution)/shard_map/matmul_nt/pallas_call | solution.py:405
  322.9 11.7 %matmul_nt.4.refs_2_ = bf16[640,1024]{1,0:T(8,128)(2,1)S(1)} custom-call(bf16[640,5120]{1,0:T(8,128)(2,1)} %ff_backward.1.left_ref.own_ref, bf16[2048,7680]{1,0:T(8,128)(2,1)} %all-gather.5.cloned.1.call-done.weight_ref.right_ref), custom_call_target="tpu_custom_call" | custom-call | flops 1677721600 | bytes 2621440 | tf_op jit(solution)/shard_map/matmul_nt/pallas_call | solution.py:405
  335.1 15.0 %weight_grad.9 = bf16[4,128,5120]{2,1,0:T(8,128)(2,1)} custom-call(s32[5]{0:T(128)S(1)} %pad_add_fusion.2.index_ref, bf16[640,2048]{1,0:T(8,128)(2,1)S(1)} %copy-done.4, bf16[640,2048]{1,0:T(8,128)(2,1)S(1)} %copy-done.14, bf16[640,5120]{1,0:T(8,128)(2,1)} %ff_backward.1.left_ref.own_ref, bf16[640,5120]{1,0:T(8,128)(2,1)} %collective-permute-done.12.other_ref), custom_call_target="tpu_custom_call" | custom-call | flops 1677721600 | bytes 4587520 | tf_op jit(solution)/shard_map/weight_grad/pallas_call | solution.py:561
  351.6 10.8 %matmul_nt.5 = bf16[640,2048]{1,0:T(8,128)(2,1)S(1)} custom-call(bf16[640,2560]{1,0:T(8,128)(2,1)S(1)} %copy-done.6, bf16[2048,7680]{1,0:T(8,128)(2,1)} %all-gather.5.cloned.1.call-done.weight_ref.right_ref), custom_call_target="tpu_custom_call" | custom-call | flops 1677721600 | bytes 2621440 | tf_op jit(solution)/shard_map/matmul_nt/pallas_call | solution.py:405
  363.8 15.8 %collective-permute-done.13.refs_3_ = bf16[640,1024]{1,0:T(8,128)(2,1)} collective-permute-done((bf16[640,1024]{1,0:T(8,128)(2,1)S(1)}, bf16[640,1024]{1,0:T(8,128)(2,1)}, u32[]{:S(2)}, u32[]{:S(2)}) %collective-permute-start.13) | collective-permute-done | bytes 1310752 | tf_op jit(solution)/shard_map/ppermute | solution.py:669
  379.7 6.9 %norm_backward.2 = (bf16[640,2048]{1,0:T(8,128)(2,1)}, f32[1,2048]{1,0:T(1,128)S(1)}) custom-call(bf16[640,1024]{1,0:T(8,128)(2,1)S(1)} %matmul_nt.3.refs_0_, bf16[640,1024]{1,0:T(8,128)(2,1)S(1)} %collective-permute-done.11.refs_1_, bf16[640,1024]{1,0:T(8,128)(2,1)S(1)} %matmul_nt.4.refs_2_, bf16[640,1024]{1,0:T(8,128)(2,1)} %collective-permute-done.13.refs_3_, ...), custom_call_target="tpu_custom_call" | custom-call | flops 6553600 | bytes 3932160 | tf_op jit(solution)/shard_map/norm_backward/pallas_call | solution.py:486
  386.6 5.8 fusion.8.grad_ref
  392.4 8.8 %weight_grad.10 = bf16[4,128,2560]{2,1,0:T(8,128)(2,1)S(1)} custom-call(s32[5]{0:T(128)S(1)} %pad_add_fusion.3.index_ref, bf16[640,2048]{1,0:T(8,128)(2,1)S(1)} %copy-done.1, bf16[640,2048]{1,0:T(8,128)(2,1)} %copy-done.46, bf16[640,2560]{1,0:T(8,128)(2,1)} %copy-done.5, bf16[640,2560]{1,0:T(8,128)(2,1)} %copy-done.44, ...), custom_call_target="tpu_custom_call" | custom-call | flops 838860800 | bytes 2293760 | tf_op jit(solution)/shard_map/weight_grad/pallas_call | solution.py:561
  409.2 31.2 %attention_backward.1 = (f32[640,640]{1,0:T(8,128)}, f32[1536,384]{1,0:T(8,128)}) custom-call(s32[5]{0:T(128)S(1)} %fusion.26.slot_ref, bf16[640,1024]{1,0:T(8,128)(2,1)S(1)} %copy-done.27, bf16[1536,384]{1,0:T(8,128)(2,1)S(1)} %copy-done.38, f32[1024,128]{1,0:T(8,128)S(1)} %compare_convert_fusion.mask_ref, bf16[640,640]{1,0:T(8,128)(2,1)S(1)} %copy-done.20, ...), custom_call_target="tpu_custom_call" | custom-call | flops 6144000000 | bytes 2457600 | tf_op jit(solution)/shard_map/attention_backward/pallas_call | solution.py:333
  455.3 21.7 %collective-permute-done.15 = bf16[512,384]{1,0:T(8,128)(2,1)S(1)} collective-permute-done((bf16[512,384]{1,0:T(8,128)(2,1)S(1)}, bf16[512,384]{1,0:T(8,128)(2,1)S(1)}, u32[]{:S(2)}, u32[]{:S(2)}) %collective-permute-start.15) | collective-permute-done | bytes 393248 | tf_op jit(solution)/shard_map/ppermute | solution.py:663
  483.2 5.8 collective-permute-done.22
  490.1 15.9 %weight_grad.15 = bf16[4,128,5120]{2,1,0:T(8,128)(2,1)} custom-call(s32[5]{0:T(128)S(1)} %pad_add_fusion.3.index_ref, bf16[640,2048]{1,0:T(8,128)(2,1)S(1)} %copy-done.4, bf16[640,2048]{1,0:T(8,128)(2,1)S(1)} %copy-done.15, bf16[640,5120]{1,0:T(8,128)(2,1)} %ff_backward.1.left_ref.own_ref, bf16[640,5120]{1,0:T(8,128)(2,1)} %collective-permute-done.12.other_ref, ...), custom_call_target="tpu_custom_call" | custom-call | flops 1677721600 | bytes 4587520 | tf_op jit(solution)/shard_map/weight_grad/pallas_call | solution.py:561
  521.7 5.6 weight_grad.12
  530.4 21.6 %collective-permute-done.26.rest_0_ = bf16[4,128,1024]{2,1,0:T(8,128)(2,1)} collective-permute-done((bf16[4,128,1024]{2,1,0:T(8,128)(2,1)}, bf16[4,128,1024]{2,1,0:T(8,128)(2,1)}, u32[]{:S(2)}, u32[]{:S(2)}) %collective-permute-start.26) | collective-permute-done | bytes 1048608 | tf_op jit(solution)/shard_map/ppermute | solution.py:663
  552.0 5.1 weight_grad.13
  560.2 4.8 convolution_convert_fusion.refs_4_
  565.1 8.0 %norm_backward.3 = (bf16[640,2048]{1,0:T(8,128)(2,1)}, f32[1,2048]{1,0:T(1,128)S(1)}) custom-call(bf16[640,1024]{1,0:T(8,128)(2,1)S(1)} %copy-done.30, bf16[640,1024]{1,0:T(8,128)(2,1)S(1)} %copy-done.32, bf16[640,1024]{1,0:T(8,128)(2,1)} %convolution_convert_fusion.2.refs_2_, bf16[640,1024]{1,0:T(8,128)(2,1)} %collective-permute-done.23.refs_3_, ...), custom_call_target="tpu_custom_call" | custom-call | flops 6553600 | bytes 3932160 | tf_op jit(solution)/shard_map/norm_backward/pallas_call | solution.py:486
  598.0 6.2 collective-permute-done.32
  604.2 18.0 %collective-permute-done.33 = bf16[128,1024]{1,0:T(8,128)(2,1)} collective-permute-done((bf16[128,1024]{1,0:T(8,128)(2,1)}, bf16[128,1024]{1,0:T(8,128)(2,1)}, u32[]{:S(2)}, u32[]{:S(2)}) %collective-permute-start.33) | collective-permute-done | bytes 262176 | tf_op jit(solution)/shard_map/ppermute | solution.py:660
  634.5 7.1 %collective-permute-done.38 = bf16[128,640]{1,0:T(8,128)(2,1)S(1)} collective-permute-done((bf16[128,640]{1,0:T(8,128)(2,1)S(1)}, bf16[128,640]{1,0:T(8,128)(2,1)S(1)}, u32[]{:S(2)}, u32[]{:S(2)}) %collective-permute-start.38) | collective-permute-done | bytes 163872 | tf_op jit(solution)/shard_map/ppermute | solution.py:660
  (315 shorter events, 167.4 us)
Async XLA Ops:
  7.2 72.4 %all-gather.3.cloned.1.call-start = ((), (), s32[]{:S(2)}) async-start(), calls=%async_computation.2 | async-start | bytes 7241728 | tf_op jit(solution)/shard_map/all_gather | solution.py:685
  11.0 237.5 %all-gather.5.cloned.1.call-start = ((), (), s32[]{:S(2)}) async-start(), calls=%async_computation.3 | async-start | bytes 33423360 | tf_op jit(solution)/shard_map/all_gather | solution.py:691
  16.9 578.4 %reduce-scatter.5.cloned.1.call-start = ((), (), s32[]{:S(2)}) async-start(), calls=%async_computation.5 | async-start | bytes 3276800 | tf_op jit(solution)/shard_map/reduce_scatter | solution.py:777
  81.4 55.2 %collective-permute-start.4 = (bf16[2048,384]{0,1:T(8,128)(2,1)S(1)}, bf16[2048,384]{0,1:T(8,128)(2,1)S(1)}, u32[]{:S(2)}, u32[]{:S(2)}) collective-permute-start(bf16[2048,384]{0,1:T(8,128)(2,1)S(1)} %slice.176), channel_id=1, source_target_pairs={{0,1},{1,0},{2,3},{3,2},{4,5},{5,4},{6,7},{7,6},{8,9},{9,8},{10,11... | collective-permute-start | bytes 4718600 | tf_op jit(solution)/shard_map/ppermute | solution.py:669
  93.7 10.5 %collective-permute-start.1 = (bf16[128,384]{1,0:T(8,128)(2,1)S(1)}, bf16[128,384]{1,0:T(8,128)(2,1)S(1)}, u32[]{:S(2)}, u32[]{:S(2)}) collective-permute-start(bf16[128,384]{1,0:T(8,128)(2,1)S(1)} %get-tuple-element.188), channel_id=1, source_target_pairs={{0,8},{2,10},{4,12},{6,14},{8,0},{10,2},{12,4},{14,6},{1,9},{3,11}... | collective-permute-start | bytes 294920 | tf_op jit(solution)/shard_map/ppermute | solution.py:660
  94.9 13.5 %collective-permute-start.2 = (bf16[128,384]{1,0:T(8,128)(2,1)S(1)}, bf16[128,384]{1,0:T(8,128)(2,1)S(1)}, u32[]{:S(2)}, u32[]{:S(2)}) collective-permute-start(bf16[128,384]{1,0:T(8,128)(2,1)S(1)} %get-tuple-element.188), channel_id=1, source_target_pairs={{0,4},{2,6},{4,8},{6,10},{8,12},{10,14},{12,0},{14,2},{1,5},{3,7},... | collective-permute-start | bytes 294920 | tf_op jit(solution)/shard_map/ppermute | solution.py:660
  143.1 56.3 %collective-permute-start.5 = (bf16[640,2048]{1,0:T(8,128)(2,1)S(1)}, bf16[640,2048]{1,0:T(8,128)(2,1)S(1)}, u32[]{:S(2)}, u32[]{:S(2)}) collective-permute-start(bf16[640,2048]{1,0:T(8,128)(2,1)S(1)} %convolution_convert_fusion.1), channel_id=1, source_target_pairs={{0,1},{1,0},{2,3},{3,2},{4,5},{5,4},{6,7},{7,6},{8,9},{9,8},{10,11... | collective-permute-start | bytes 7864328 | tf_op jit(solution)/shard_map/ppermute | solution.py:669
  143.8 67.1 %collective-permute-start.8 = (bf16[640,2048]{1,0:T(8,128)(2,1)S(1)}, bf16[640,2048]{1,0:T(8,128)(2,1)S(1)}, u32[]{:S(2)}, u32[]{:S(2)}) collective-permute-start(bf16[640,2048]{1,0:T(8,128)(2,1)S(1)} %copy-done.43), channel_id=1, source_target_pairs={{0,16},{16,0},{1,17},{17,1},{2,18},{18,2},{3,19},{19,3},{4,20},{20... | collective-permute-start | bytes 7864328 | tf_op jit(solution)/shard_map/ppermute | solution.py:666
  146.3 64.7 %collective-permute-start.7 = (bf16[640,2048]{1,0:T(8,128)(2,1)S(1)}, bf16[640,2048]{1,0:T(8,128)(2,1)S(1)}, u32[]{:S(2)}, u32[]{:S(2)}) collective-permute-start(bf16[640,2048]{1,0:T(8,128)(2,1)S(1)} %constant_dynamic-update-slice_fusion.7.grad_ref.left_own_ref.refs_4_), channel_id=1, source_target_pairs={{0,16},{16,0},{1,17},{17,1},{2,18},{18,2},{3,19},{19,3},{4,20},{20... | collective-permute-start | bytes 7864328 | tf_op jit(solution)/shard_map/ppermute | solution.py:666
  270.4 17.1 %collective-permute-start.10 = (bf16[640,2560]{1,0:T(8,128)(2,1)S(1)}, bf16[640,2560]{1,0:T(8,128)(2,1)S(1)}, u32[]{:S(2)}, u32[]{:S(2)}) collective-permute-start(bf16[640,2560]{1,0:T(8,128)(2,1)S(1)} %get-tuple-element.94.own_ref.left_ref), channel_id=1, source_target_pairs={{0,16},{16,0},{1,17},{17,1},{2,18},{18,2},{3,19},{19,3},{4,20},{20... | collective-permute-start | bytes 9830408 | tf_op jit(solution)/shard_map/ppermute | solution.py:666
  289.3 45.8 %collective-permute-start.12 = (bf16[640,5120]{1,0:T(8,128)(2,1)}, bf16[640,5120]{1,0:T(8,128)(2,1)}, u32[]{:S(2)}, u32[]{:S(2)}) collective-permute-start(bf16[640,5120]{1,0:T(8,128)(2,1)} %ff_backward.1.left_ref.own_ref), channel_id=1, source_target_pairs={{0,16},{16,0},{1,17},{17,1},{2,18},{18,2},{3,19},{19,3},{4,20},{20... | collective-permute-start | bytes 19660808 | tf_op jit(solution)/shard_map/ppermute | solution.py:666
  297.9 94.4 %collective-permute-start.14 = (bf16[4,128,2560]{2,1,0:T(8,128)(2,1)S(1)}, bf16[4,128,2560]{2,1,0:T(8,128)(2,1)}, u32[]{:S(2)}, u32[]{:S(2)}) collective-permute-start(bf16[4,128,2560]{2,1,0:T(8,128)(2,1)S(1)} %weight_grad.8), channel_id=1, source_target_pairs={{0,2},{2,0},{4,6},{6,4},{8,10},{10,8},{12,14},{14,12},{1,3},{3,1},... | collective-permute-start | bytes 7864328 | tf_op jit(solution)/shard_map/ppermute | solution.py:663
  321.6 30.0 %collective-permute-start.11 = (bf16[640,1024]{1,0:T(8,128)(2,1)S(1)}, bf16[640,1024]{1,0:T(8,128)(2,1)S(1)}, u32[]{:S(2)}, u32[]{:S(2)}) collective-permute-start(bf16[640,1024]{1,0:T(8,128)(2,1)S(1)} %matmul_nt.3.refs_0_), channel_id=1, source_target_pairs={{0,1},{1,0},{2,3},{3,2},{4,5},{5,4},{6,7},{7,6},{8,9},{9,8},{10,11... | collective-permute-start | bytes 3932168 | tf_op jit(solution)/shard_map/ppermute | solution.py:669
  334.6 45.1 %collective-permute-start.13 = (bf16[640,1024]{1,0:T(8,128)(2,1)S(1)}, bf16[640,1024]{1,0:T(8,128)(2,1)}, u32[]{:S(2)}, u32[]{:S(2)}) collective-permute-start(bf16[640,1024]{1,0:T(8,128)(2,1)S(1)} %matmul_nt.4.refs_2_), channel_id=1, source_target_pairs={{0,1},{1,0},{2,3},{3,2},{4,5},{5,4},{6,7},{7,6},{8,9},{9,8},{10,11... | collective-permute-start | bytes 3932168 | tf_op jit(solution)/shard_map/ppermute | solution.py:669
  350.1 140.0 %collective-permute-start.40 = (bf16[4,128,5120]{2,1,0:T(8,128)(2,1)}, bf16[4,128,5120]{2,1,0:T(8,128)(2,1)}, u32[]{:S(2)}, u32[]{:S(2)}) collective-permute-start(bf16[4,128,5120]{2,1,0:T(8,128)(2,1)} %weight_grad.9), channel_id=1, source_target_pairs={{0,2},{2,0},{4,6},{6,4},{8,10},{10,8},{12,14},{14,12},{1,3},{3,1},... | collective-permute-start | bytes 15728648 | tf_op jit(solution)/shard_map/ppermute | solution.py:663
  402.8 244.8 %reduce-scatter.3.cloned.1.call-start = ((), (), s32[]{:S(2)}) async-start(), calls=%async_computation.4 | async-start | bytes 6553600 | tf_op jit(solution)/shard_map/reduce_scatter | solution.py:777
  402.8 74.2 %collective-permute-start.16 = (bf16[640,2048]{1,0:T(8,128)(2,1)}, bf16[640,2048]{1,0:T(8,128)(2,1)S(1)}, u32[]{:S(2)}, u32[]{:S(2)}) collective-permute-start(bf16[640,2048]{1,0:T(8,128)(2,1)} %copy-done.10), channel_id=1, source_target_pairs={{0,1},{1,0},{2,3},{3,2},{4,5},{5,4},{6,7},{7,6},{8,9},{9,8},{10,11... | collective-permute-start | bytes 7864328 | tf_op jit(solution)/shard_map/ppermute | solution.py:669
  448.4 40.5 %collective-permute-start.19 = (bf16[640,1024]{1,0:T(8,128)(2,1)S(1)}, bf16[640,1024]{1,0:T(8,128)(2,1)S(1)}, u32[]{:S(2)}, u32[]{:S(2)}) collective-permute-start(bf16[640,1024]{1,0:T(8,128)(2,1)S(1)} %convolution_convert_fusion.3.refs_0_), channel_id=1, source_target_pairs={{0,1},{1,0},{2,3},{3,2},{4,5},{5,4},{6,7},{7,6},{8,9},{9,8},{10,11... | collective-permute-start | bytes 3932168 | tf_op jit(solution)/shard_map/ppermute | solution.py:669
  448.7 28.3 %collective-permute-start.15 = (bf16[512,384]{1,0:T(8,128)(2,1)S(1)}, bf16[512,384]{1,0:T(8,128)(2,1)S(1)}, u32[]{:S(2)}, u32[]{:S(2)}) collective-permute-start(bf16[512,384]{1,0:T(8,128)(2,1)S(1)} %slice.178), channel_id=1, source_target_pairs={{0,2},{2,0},{4,6},{6,4},{8,10},{10,8},{12,14},{14,12},{1,3},{3,1},... | collective-permute-start | bytes 1179656 | tf_op jit(solution)/shard_map/ppermute | solution.py:663
  449.3 58.3 %collective-permute-start.17 = (bf16[640,2048]{1,0:T(8,128)(2,1)}, bf16[640,2048]{1,0:T(8,128)(2,1)}, u32[]{:S(2)}, u32[]{:S(2)}) collective-permute-start(bf16[640,2048]{1,0:T(8,128)(2,1)} %get-tuple-element.101.left_own_ref.refs_5_), channel_id=1, source_target_pairs={{0,16},{16,0},{1,17},{17,1},{2,18},{18,2},{3,19},{19,3},{4,20},{20... | collective-permute-start | bytes 7864328 | tf_op jit(solution)/shard_map/ppermute | solution.py:666
  519.0 38.1 %collective-permute-start.23 = (bf16[640,1024]{1,0:T(8,128)(2,1)}, bf16[640,1024]{1,0:T(8,128)(2,1)}, u32[]{:S(2)}, u32[]{:S(2)}) collective-permute-start(bf16[640,1024]{1,0:T(8,128)(2,1)} %convolution_convert_fusion.2.refs_2_), channel_id=1, source_target_pairs={{0,1},{1,0},{2,3},{3,2},{4,5},{5,4},{6,7},{7,6},{8,9},{9,8},{10,11... | collective-permute-start | bytes 3932168 | tf_op jit(solution)/shard_map/ppermute | solution.py:669
  527.3 24.7 %collective-permute-start.26 = (bf16[4,128,1024]{2,1,0:T(8,128)(2,1)}, bf16[4,128,1024]{2,1,0:T(8,128)(2,1)}, u32[]{:S(2)}, u32[]{:S(2)}) collective-permute-start(bf16[4,128,1024]{2,1,0:T(8,128)(2,1)} %weight_grad.12), channel_id=1, source_target_pairs={{0,2},{2,0},{4,6},{6,4},{8,10},{10,8},{12,14},{14,12},{1,3},{3,1},... | collective-permute-start | bytes 3145736 | tf_op jit(solution)/shard_map/ppermute | solution.py:663
  527.9 32.3 %collective-permute-start.24 = (bf16[640,384]{1,0:T(8,128)(2,1)}, bf16[640,384]{1,0:T(8,128)(2,1)}, u32[]{:S(2)}, u32[]{:S(2)}) collective-permute-start(bf16[640,384]{1,0:T(8,128)(2,1)} %get-tuple-element.119), channel_id=1, source_target_pairs={{0,1},{1,0},{2,3},{3,2},{4,5},{5,4},{6,7},{7,6},{8,9},{9,8},{10,11... | collective-permute-start | bytes 1474568 | tf_op jit(solution)/shard_map/ppermute | solution.py:669
  529.4 44.6 %collective-permute-start.18 = (bf16[4,128,640]{2,1,0:T(8,128)(2,1)}, bf16[4,128,640]{2,1,0:T(8,128)(2,1)}, u32[]{:S(2)}, u32[]{:S(2)}) collective-permute-start(bf16[4,128,640]{2,1,0:T(8,128)(2,1)} %copy-done.36), channel_id=1, source_target_pairs={{0,2},{2,0},{4,6},{6,4},{8,10},{10,8},{12,14},{14,12},{1,3},{3,1},... | collective-permute-start | bytes 1966088 | tf_op jit(solution)/shard_map/ppermute | solution.py:663
  579.7 12.1 %collective-permute-start.29 = (f32[33,128]{1,0:T(8,128)S(1)}, f32[33,128]{1,0:T(8,128)S(1)}, u32[]{:S(2)}, u32[]{:S(2)}) collective-permute-start(f32[33,128]{1,0:T(8,128)S(1)} %fusion.40), channel_id=1, source_target_pairs={{0,4},{2,6},{4,8},{6,10},{8,12},{10,14},{12,0},{14,2},{1,5},{3,7},... | collective-permute-start | bytes 50696 | tf_op jit(solution)/shard_map/ppermute | solution.py:660
  580.2 11.6 %collective-permute-start.30 = (f32[33,128]{1,0:T(8,128)S(1)}, f32[33,128]{1,0:T(8,128)S(1)}, u32[]{:S(2)}, u32[]{:S(2)}) collective-permute-start(f32[33,128]{1,0:T(8,128)S(1)} %fusion.40), channel_id=1, source_target_pairs={{0,8},{2,10},{4,12},{6,14},{8,0},{10,2},{12,4},{14,6},{1,9},{3,11}... | collective-permute-start | bytes 50696 | tf_op jit(solution)/shard_map/ppermute | solution.py:660
  589.2 15.0 %collective-permute-start.32 = (bf16[128,1024]{1,0:T(8,128)(2,1)}, bf16[128,1024]{1,0:T(8,128)(2,1)S(1)}, u32[]{:S(2)}, u32[]{:S(2)}) collective-permute-start(bf16[128,1024]{1,0:T(8,128)(2,1)} %get-tuple-element.192), channel_id=1, source_target_pairs={{0,4},{2,6},{4,8},{6,10},{8,12},{10,14},{12,0},{14,2},{1,5},{3,7},... | collective-permute-start | bytes 786440 | tf_op jit(solution)/shard_map/ppermute | solution.py:660
  589.3 33.0 %collective-permute-start.33 = (bf16[128,1024]{1,0:T(8,128)(2,1)}, bf16[128,1024]{1,0:T(8,128)(2,1)}, u32[]{:S(2)}, u32[]{:S(2)}) collective-permute-start(bf16[128,1024]{1,0:T(8,128)(2,1)} %get-tuple-element.191), channel_id=1, source_target_pairs={{0,8},{2,10},{4,12},{6,14},{8,0},{10,2},{12,4},{14,6},{1,9},{3,11}... | collective-permute-start | bytes 786440 | tf_op jit(solution)/shard_map/ppermute | solution.py:660
  591.8 31.9 %collective-permute-start.34 = (bf16[128,1024]{1,0:T(8,128)(2,1)}, bf16[128,1024]{1,0:T(8,128)(2,1)}, u32[]{:S(2)}, u32[]{:S(2)}) collective-permute-start(bf16[128,1024]{1,0:T(8,128)(2,1)} %get-tuple-element.190), channel_id=1, source_target_pairs={{0,12},{2,14},{4,0},{6,2},{8,4},{10,6},{12,8},{14,10},{1,13},{3,15... | collective-permute-start | bytes 786440 | tf_op jit(solution)/shard_map/ppermute | solution.py:660
  628.1 13.4 %collective-permute-start.38 = (bf16[128,640]{1,0:T(8,128)(2,1)S(1)}, bf16[128,640]{1,0:T(8,128)(2,1)S(1)}, u32[]{:S(2)}, u32[]{:S(2)}) collective-permute-start(bf16[128,640]{1,0:T(8,128)(2,1)S(1)} %get-tuple-element.197), channel_id=1, source_target_pairs={{0,8},{2,10},{4,12},{6,14},{8,0},{10,2},{12,4},{14,6},{1,9},{3,11}... | collective-permute-start | bytes 491528 | tf_op jit(solution)/shard_map/ppermute | solution.py:660
  629.8 15.1 %collective-permute-start.39 = (bf16[128,640]{1,0:T(8,128)(2,1)S(1)}, bf16[128,640]{1,0:T(8,128)(2,1)S(1)}, u32[]{:S(2)}, u32[]{:S(2)}) collective-permute-start(bf16[128,640]{1,0:T(8,128)(2,1)S(1)} %get-tuple-element.196), channel_id=1, source_target_pairs={{0,12},{2,14},{4,0},{6,2},{8,4},{10,6},{12,8},{14,10},{1,13},{3,15... | collective-permute-start | bytes 491528 | tf_op jit(solution)/shard_map/ppermute | solution.py:660
  633.3 12.7 %collective-permute-start.35 = (f32[128,384]{1,0:T(8,128)S(1)}, f32[128,384]{1,0:T(8,128)S(1)}, u32[]{:S(2)}, u32[]{:S(2)}) collective-permute-start(f32[128,384]{1,0:T(8,128)S(1)} %slice.194), channel_id=1, source_target_pairs={{0,1},{1,0},{2,3},{3,2},{4,5},{5,4},{6,7},{7,6},{8,9},{9,8},{10,11... | collective-permute-start | bytes 589832 | tf_op jit(solution)/shard_map/ppermute | solution.py:669
  (76 other events, 841.4 us)
Sparse Core Ops, SparseCore 0:
  11.1 68.4 all-gather.2
  81.8 166.6 all-gather.4
  402.9 52.2 reduce-scatter.4
  506.1 111.8 reduce-scatter.2
